TPU v7x, 32 devices: a whole 2x2x4 slice. The times are simulated.
32 devices in a mesh: groups: 2 (over y), tm: 8 (over z, x), head: 2 (over core).
Axes of the slice: x: 2, y: 2, z: 4, core: 2. Of those that a mesh axis runs over, the one named last changes fastest.
Arguments:
- queries: bfloat16 [1536, 2560], P(('groups', 'tm'), 'head'), parts along dimension 0, may hold values from -1000 to 1000
- keys: bfloat16 [1536, 2560], P(('groups', 'tm'), 'head'), parts along dimension 0, may hold values from -1000 to 1000
- values: bfloat16 [1536, 2560], P(('groups', 'tm'), 'head'), parts along dimension 0, may hold values from -6 to 6
- q_gain: float32 [2560], P('head'), may hold values from 1 to 2
- k_gain: float32 [2560], P('head'), may hold values from 1 to 2
- frames: int32 [16], P(('groups', 'tm')), parts along dimension 0, may hold values from 1 to 3
- flags: int32 [16, 2], P(('groups', 'tm')), parts along dimension 0, may hold values 0 or 1
Outputs:
- attended: bfloat16 [1536, 2560], P(('groups', 'tm'), 'head'), parts along dimension 0
There are 2 independent parts, one for each index of `groups`. A program takes and returns all parts, laid end to end along the dimension named above; an argument that names none is the same for every part. Nothing has to cross between parts.
All inputs are finite; a program needn't handle non-finite values. No bound on the sum of `flags` on one device may be relied on, other than what follows from the above.
Results may differ from a plain program's by a relative error of at most 0.011.
Values may be sent and summed in bfloat16 or wider, within the bound.
No kernel may reach another device: no remote copies, remote signals or barrier semaphores. Data moves between devices by JAX's collectives and lax.ppermute only.
A program may use at most 128 MiB of HBM per device.

v0:
```python
from functools import reduce
import math

import jax
import jax.numpy as jnp
from jax import lax
from jax.sharding import PartitionSpec as P

HD = 128
FT = 32


EPSILON = 1e-06


def passed_along(value, axis, steps):
    count = lax.axis_size(axis)
    first, last = (max(0, -steps), min(count, count - steps))
    return lax.ppermute(value, axis, [(source, source + steps) for source in range(first, last)])


def spread(value, axis, source):
    kept = jnp.where(lax.axis_index(axis) == source, value, 0).astype(value.dtype)
    return lax.psum(kept, axis)


def slide_rows(buffer, offset_rows, window_len):
    filler = jnp.zeros((window_len,) + buffer.shape[1:], buffer.dtype)
    return lax.dynamic_slice_in_dim(
        jnp.concatenate([buffer, filler], 0), offset_rows, window_len, 0
    )


def append_window(earlier, later):
    window_len = later[2].shape[0]
    later_count = jnp.sum(later[2].astype(jnp.float32)).astype(jnp.int32)
    from_later = jnp.arange(window_len, dtype=jnp.int32) >= window_len - later_count
    merged = []
    for previous, incoming in zip(earlier, later):
        shifted = slide_rows(previous, later_count, window_len)
        choose_mask = from_later.reshape((window_len,) + (1,) * (incoming.ndim - 1))
        merged.append(jnp.where(choose_mask, incoming, shifted))
    return tuple(merged)


def local(queries, keys, values, q_gain, k_gain, frames, flags):
    row_count, col_count = queries.shape
    head_count = col_count // HD
    full_width = col_count * lax.axis_size("head")
    q_wide = queries.astype(jnp.float32)
    k_wide = keys.astype(jnp.float32)
    q_energy, k_energy = lax.psum(
        (jnp.sum(q_wide * q_wide, axis=1), jnp.sum(k_wide * k_wide, axis=1)), "head"
    )
    q_norm = (q_wide * lax.rsqrt(q_energy / full_width + EPSILON)[:, None] * q_gain).astype(
        jnp.bfloat16
    )
    k_norm = (k_wide * lax.rsqrt(k_energy / full_width + EPSILON)[:, None] * k_gain).astype(
        jnp.bfloat16
    )
    valid_rows = frames[0] * FT
    window_len = 2 * FT

    def tail_rows(source):
        leading = jnp.zeros((window_len, col_count), jnp.bfloat16)
        return slide_rows(jnp.concatenate([leading, source], 0), valid_rows, window_len)

    own_flags = (jnp.arange(window_len, dtype=jnp.int32) >= window_len - valid_rows).astype(
        jnp.bfloat16
    )
    own_window = (tail_rows(k_norm), tail_rows(values), own_flags)
    from_last = passed_along((own_window[0], own_window[1], own_window[2]), "tm", 1)
    from_earlier = passed_along((own_window[0], own_window[1], own_window[2]), "tm", 2)
    window_keys, window_values, window_flags = append_window(from_earlier, from_last)
    sink_keys, sink_values = (spread(k_norm[:FT], "tm", 0), spread(values[:FT], "tm", 0))
    scaling = 1.0 / math.sqrt(HD)
    q_heads = q_norm.reshape(row_count, head_count, HD)
    slot_index = jnp.arange(row_count, dtype=jnp.int32)
    live_keys = slot_index < valid_rows
    use_sink = flags[0, 0] > 0
    use_window = flags[0, 1] > 0
    key_groups = (
        (k_norm, values, live_keys),
        (window_keys, window_values, (window_flags > 0) & use_window),
        (sink_keys, sink_values, jnp.full((sink_keys.shape[0],), use_sink)),
    )

    def score_block(key_rows, allowed):
        k_heads = key_rows.reshape(key_rows.shape[0], head_count, HD)
        products = (
            jnp.einsum("qhd,khd->hqk", q_heads, k_heads, preferred_element_type=jnp.float32)
            * scaling
        )
        return jnp.where(allowed[None, None, :], products, -jnp.inf)

    logits = [score_block(key_rows, allowed) for key_rows, value_rows, allowed in key_groups]
    highest = reduce(
        jnp.maximum, [jnp.max(block_scores, axis=2, keepdims=True) for block_scores in logits]
    )
    denominator = jnp.zeros((head_count, row_count), jnp.float32)
    blended = jnp.zeros((row_count, head_count, HD), jnp.float32)
    for block_scores, group in zip(logits, key_groups):
        weight = jnp.exp(block_scores - highest).astype(jnp.bfloat16)
        denominator = denominator + jnp.sum(weight, axis=2, dtype=jnp.float32)
        value_heads = group[1].reshape(group[1].shape[0], head_count, HD)
        blended = blended + jnp.einsum(
            "hqk,khd->qhd", weight, value_heads, preferred_element_type=jnp.float32
        )
    blended = blended / jnp.transpose(denominator)[:, :, None]
    blended = jnp.where(live_keys[:, None, None], blended, 0.0)
    return blended.reshape(row_count, col_count).astype(jnp.bfloat16)


def solution(mesh):
    placed = (
        P(("groups", "tm"), "head"),
        P(("groups", "tm"), "head"),
        P(("groups", "tm"), "head"),
        P("head"),
        P("head"),
        P(("groups", "tm")),
        P(("groups", "tm"), None),
    )
    return jax.shard_map(
        local, mesh=mesh, in_specs=placed, out_specs=P(("groups", "tm"), "head"), check_vma=False
    )
```

profile of v0, /device:TPU:0, one launch (start us, length us, event | category | flops | bytes accessed | tf_op | source)
XLA Modules:
  0.0 111.2 jit_solution(5486374469623921674)
XLA Ops:
  6.5 0.0 all-reduce.7.cloned.1.call-start
  7.2 5.0 %collective-permute-start.1 = (bf16[64]{0:T(256)(128)(2,1)S(1)}, bf16[64]{0:T(256)(128)(2,1)S(1)}, u32[]{:S(2)}, u32[]{:S(2)}) collective-permute-start(bf16[64]{0:T(256)(128)(2,1)S(1)} %compare_convert_fusion), channel_id=1, source_target_pairs={{0,4},{2,6},{4,8},{6,10},{8,12},{10,14},{1,5},{3,7},{5,9},{7,11},{... | collective-permute-start | bytes 392 | tf_op jit(solution)/shard_map/ppermute | solution.py:19
  12.2 3.4 %collective-permute-start = (bf16[64]{0:T(256)(128)(2,1)S(1)}, bf16[64]{0:T(256)(128)(2,1)S(1)}, u32[]{:S(2)}, u32[]{:S(2)}) collective-permute-start(bf16[64]{0:T(256)(128)(2,1)S(1)} %compare_convert_fusion), channel_id=1, source_target_pairs={{0,2},{2,4},{4,6},{6,8},{8,10},{10,12},{12,14},{1,3},{3,5},{5,7},{... | collective-permute-start | bytes 392 | tf_op jit(solution)/shard_map/ppermute | solution.py:19
  15.6 1.1 fusion.7
  16.7 0.1 fusion.10
  16.9 2.5 %all-reduce.3 = (f32[96]{0:T(128)S(1)}, f32[96]{0:T(128)S(1)}) all-reduce(f32[96]{0:T(128)S(1)} %fusion.7, f32[96]{0:T(128)S(1)} %fusion.10), channel_id=1, replica_groups=mesh['groups'=2,'tm'=8,'head'=2] {'head'}, use_global_device_ids=true, to_apply=%region_1.0 | all-reduce | flops 192 | bytes 1536 | tf_op jit(solution)/shard_map/psum | solution.py:52
  19.4 0.0 copy-start
  19.4 0.1 fusion.12
  19.5 0.8 copy-done
  20.3 0.2 fusion.18
  20.5 3.5 %collective-permute-start.4 = (bf16[64,1280]{1,0:T(8,128)(2,1)S(1)}, bf16[64,1280]{1,0:T(8,128)(2,1)S(1)}, u32[]{:S(2)}, u32[]{:S(2)}) collective-permute-start(bf16[64,1280]{1,0:T(8,128)(2,1)S(1)} %get-tuple-element.9), channel_id=1, source_target_pairs={{0,2},{2,4},{4,6},{6,8},{8,10},{10,12},{12,14},{1,3},{3,5},{5,7},{... | collective-permute-start | bytes 491528 | tf_op jit(solution)/shard_map/ppermute | solution.py:19
  24.0 3.5 %collective-permute-start.5 = (bf16[64,1280]{1,0:T(8,128)(2,1)S(1)}, bf16[64,1280]{1,0:T(8,128)(2,1)S(1)}, u32[]{:S(2)}, u32[]{:S(2)}) collective-permute-start(bf16[64,1280]{1,0:T(8,128)(2,1)S(1)} %get-tuple-element.9), channel_id=1, source_target_pairs={{0,4},{2,6},{4,8},{6,10},{8,12},{10,14},{1,5},{3,7},{5,9},{7,11},{... | collective-permute-start | bytes 491528 | tf_op jit(solution)/shard_map/ppermute | solution.py:19
  27.5 3.4 %collective-permute-start.2 = (bf16[64,1280]{1,0:T(8,128)(2,1)S(1)}, bf16[64,1280]{1,0:T(8,128)(2,1)S(1)}, u32[]{:S(2)}, u32[]{:S(2)}) collective-permute-start(bf16[64,1280]{1,0:T(8,128)(2,1)S(1)} %get-tuple-element.10), channel_id=1, source_target_pairs={{0,2},{2,4},{4,6},{6,8},{8,10},{10,12},{12,14},{1,3},{3,5},{5,7},{... | collective-permute-start | bytes 491528 | tf_op jit(solution)/shard_map/ppermute | solution.py:19
  30.9 0.6 copy_bitcast_fusion
  31.5 0.7 copy_bitcast_fusion.1
  32.2 0.0 all-reduce.7.cloned.1.call-update
  32.2 0.2 copy.17
  32.4 0.0 copy-start.5
  32.4 0.0 copy-start.2
  32.5 0.0 copy-start.4
  32.5 0.2 copy.24
  32.7 0.4 copy-done.5
  33.1 0.6 fusion.26
  33.7 0.0 copy-done.2
  33.7 0.1 fusion.9
  33.9 0.2 copy.16
  34.7 0.3 fusion.28
  35.7 0.0 collective-permute-done
  35.7 1.9 %collective-permute-start.3 = (bf16[64,1280]{1,0:T(8,128)(2,1)S(1)}, bf16[64,1280]{1,0:T(8,128)(2,1)S(1)}, u32[]{:S(2)}, u32[]{:S(2)}) collective-permute-start(bf16[64,1280]{1,0:T(8,128)(2,1)S(1)} %get-tuple-element.10), channel_id=1, source_target_pairs={{0,4},{2,6},{4,8},{6,10},{8,12},{10,14},{1,5},{3,7},{5,9},{7,11},{... | collective-permute-start | bytes 491528 | tf_op jit(solution)/shard_map/ppermute | solution.py:19
  37.6 0.7 convert_reduce_fusion.3
  38.9 0.0 collective-permute-done.1
  38.9 0.1 compare_and_fusion
  39.0 60.8 %all-reduce.7.cloned.1.call-done = (bf16[32,10,128]{2,0,1:T(8,128)(2,1)}, bf16[32,10,128]{2,0,1:T(8,128)(2,1)}) async-done(((bf16[32,10,128]{2,0,1:T(8,128)(2,1)}, bf16[32,10,128]{2,0,1:T(8,128)(2,1)}), (bf16[32,10,128]{2,0,1:T(8,128)(2,1)}, bf16[32,10,128]{2,0,1:T(8,128)(2,1)})) %all-reduce.7.cloned.1.call-update) | async-done | bytes 163856 | tf_op jit(solution)/shard_map/psum | solution.py:24
  99.8 1.1 fusion.27
  100.9 0.0 collective-permute-done.4
  100.9 0.0 collective-permute-done.5
  100.9 0.0 collective-permute-done.2
  100.9 0.0 collective-permute-done.3
  100.9 0.2 fusion.16
  101.1 0.2 select_reduce_fusion
  101.4 0.1 convert_reduce_fusion.1
  101.6 0.1 convert_reduce_fusion
  101.7 0.4 convolution_bitcast_fusion.2
  102.0 0.4 fusion.1
  102.4 0.5 copy-done.6
  102.9 0.3 fusion.5
  103.3 0.2 copy.29
  103.5 0.9 copy.30
  (14 shorter events, 0.1 us)
Async XLA Ops:
  6.5 10.2 %copy-start.1 = (bf16[96,1280]{1,0:T(8,128)(2,1)S(1)}, bf16[96,1280]{1,0:T(8,128)(2,1)}, u32[]{:S(2)}) copy-start(bf16[96,1280]{1,0:T(8,128)(2,1)} %param.8) | copy-start | bytes 737284
  6.5 93.2 %all-reduce.7.cloned.1.call-start = ((), (), s32[]{:S(2)}) async-start(), calls=%async_computation | async-start | bytes 327680 | tf_op jit(solution)/shard_map/psum | solution.py:24
  7.2 31.7 %collective-permute-start.1 = (bf16[64]{0:T(256)(128)(2,1)S(1)}, bf16[64]{0:T(256)(128)(2,1)S(1)}, u32[]{:S(2)}, u32[]{:S(2)}) collective-permute-start(bf16[64]{0:T(256)(128)(2,1)S(1)} %compare_convert_fusion), channel_id=1, source_target_pairs={{0,4},{2,6},{4,8},{6,10},{8,12},{10,14},{1,5},{3,7},{5,9},{7,11},{... | collective-permute-start | bytes 392 | tf_op jit(solution)/shard_map/ppermute | solution.py:19
  12.2 23.5 %collective-permute-start = (bf16[64]{0:T(256)(128)(2,1)S(1)}, bf16[64]{0:T(256)(128)(2,1)S(1)}, u32[]{:S(2)}, u32[]{:S(2)}) collective-permute-start(bf16[64]{0:T(256)(128)(2,1)S(1)} %compare_convert_fusion), channel_id=1, source_target_pairs={{0,2},{2,4},{4,6},{6,8},{8,10},{10,12},{12,14},{1,3},{3,5},{5,7},{... | collective-permute-start | bytes 392 | tf_op jit(solution)/shard_map/ppermute | solution.py:19
  16.9 2.5 %copy-start.3 = (f32[1280]{0:T(1024)S(1)}, f32[1280]{0:T(1024)}, u32[]{:S(2)}) copy-start(f32[1280]{0:T(1024)} %param.11) | copy-start | bytes 15364
  19.4 0.9 copy-start
  20.5 80.4 %collective-permute-start.4 = (bf16[64,1280]{1,0:T(8,128)(2,1)S(1)}, bf16[64,1280]{1,0:T(8,128)(2,1)S(1)}, u32[]{:S(2)}, u32[]{:S(2)}) collective-permute-start(bf16[64,1280]{1,0:T(8,128)(2,1)S(1)} %get-tuple-element.9), channel_id=1, source_target_pairs={{0,2},{2,4},{4,6},{6,8},{8,10},{10,12},{12,14},{1,3},{3,5},{5,7},{... | collective-permute-start | bytes 491528 | tf_op jit(solution)/shard_map/ppermute | solution.py:19
  24.0 76.9 %collective-permute-start.5 = (bf16[64,1280]{1,0:T(8,128)(2,1)S(1)}, bf16[64,1280]{1,0:T(8,128)(2,1)S(1)}, u32[]{:S(2)}, u32[]{:S(2)}) collective-permute-start(bf16[64,1280]{1,0:T(8,128)(2,1)S(1)} %get-tuple-element.9), channel_id=1, source_target_pairs={{0,4},{2,6},{4,8},{6,10},{8,12},{10,14},{1,5},{3,7},{5,9},{7,11},{... | collective-permute-start | bytes 491528 | tf_op jit(solution)/shard_map/ppermute | solution.py:19
  27.5 73.4 %collective-permute-start.2 = (bf16[64,1280]{1,0:T(8,128)(2,1)S(1)}, bf16[64,1280]{1,0:T(8,128)(2,1)S(1)}, u32[]{:S(2)}, u32[]{:S(2)}) collective-permute-start(bf16[64,1280]{1,0:T(8,128)(2,1)S(1)} %get-tuple-element.10), channel_id=1, source_target_pairs={{0,2},{2,4},{4,6},{6,8},{8,10},{10,12},{12,14},{1,3},{3,5},{5,7},{... | collective-permute-start | bytes 491528 | tf_op jit(solution)/shard_map/ppermute | solution.py:19
  32.4 0.7 copy-start.5
  32.4 1.3 %copy-start.2 = (bf16[96,1280]{1,0:T(8,128)(2,1)S(1)}, bf16[96,1280]{1,0:T(8,128)(2,1)}, u32[]{:S(2)}) copy-start(bf16[96,1280]{1,0:T(8,128)(2,1)} %param.7) | copy-start | bytes 737284
  32.5 1.3 %copy-start.4 = (f32[1280]{0:T(1024)S(1)}, f32[1280]{0:T(1024)}, u32[]{:S(2)}) copy-start(f32[1280]{0:T(1024)} %param.10) | copy-start | bytes 15364
  35.7 65.2 %collective-permute-start.3 = (bf16[64,1280]{1,0:T(8,128)(2,1)S(1)}, bf16[64,1280]{1,0:T(8,128)(2,1)S(1)}, u32[]{:S(2)}, u32[]{:S(2)}) collective-permute-start(bf16[64,1280]{1,0:T(8,128)(2,1)S(1)} %get-tuple-element.10), channel_id=1, source_target_pairs={{0,4},{2,6},{4,8},{6,10},{8,12},{10,14},{1,5},{3,7},{5,9},{7,11},{... | collective-permute-start | bytes 491528 | tf_op jit(solution)/shard_map/ppermute | solution.py:19
  102.0 0.9 copy-start.6
Sparse Core Ops, SparseCore 0:
  32.3 67.4 all-reduce.6
where the time goes:
time: 112 us; the launch traced here: 111 us
  waiting for transfers between devices  60.8 us (54%)
  starting transfers between devices  20.6 us (18%)
  between operations  16.3 us (15%)
  other arithmetic  4.21 us (4%)
  local copies, waits for them, and re-layouts  4.14 us (4%)
  matrix products  2.67 us (2%)
  blocking collectives  2.47 us (2%)
    psum x1, waiting for transfers between devices, spread(): return lax.psum(kept, axis)  60.8 us
    ppermute x6, starting transfers between devices, passed_along(): lax.ppermute(value, axis, [(source, source + steps) for source in range(f...  20.6 us
    psum x1, blocking collectives, local(): lax.psum((jnp.sum(q_wide * q_wide, axis=1), jnp.sum(k_wide * k_wide, axis...  2.47 us
  transfers between devices with their start and end apart: 7, of which 1 were waited for; matrix products, arithmetic and copies ran while one was open for 6% of the time, Pallas kernels for 0%

commit v1 on v0

v1 whole, which is shorter than its diff:
```python
import math

import jax
import jax.numpy as jnp
from jax import lax
from jax.experimental import pallas as pl
from jax.experimental.pallas import tpu as pltpu
from jax.sharding import PartitionSpec as P

HD = 128
FT = 32
EPSILON = 1e-06
LANES = 128
VMEM = pl.BlockSpec(memory_space=pltpu.VMEM)
SMEM = pl.BlockSpec(memory_space=pltpu.SMEM)
PARAMS = pltpu.CompilerParams(vmem_limit_bytes=8 << 20)


def tree_rounds(count):
    top = 1
    while top * 2 < count:
        top *= 2
    strides = [1] if count > 1 else []
    while top >= 2:
        strides.append(top)
        top //= 2
    held, rounds = [0], []
    for stride in strides:
        pairs = [(h, h + stride) for h in held if h + stride < count and h + stride not in held]
        rounds.append((stride, pairs))
        held = held + [target for _, target in pairs]
    return rounds


def sums_kernel(q_ref, k_ref, sums_ref):
    rows = q_ref.shape[0]
    q = q_ref[...].astype(jnp.float32)
    k = k_ref[...].astype(jnp.float32)
    q_sum = jnp.sum(q * q, axis=1, keepdims=True)
    k_sum = jnp.sum(k * k, axis=1, keepdims=True)
    lane = lax.broadcasted_iota(jnp.int32, (rows, LANES), 1)
    sums_ref[...] = jnp.where(lane < LANES // 2, q_sum, k_sum)


def pack_kernel(full_width, frames_ref, q_ref, k_ref, v_ref, qg_ref, kg_ref, mine_ref, other_ref,
                qn_ref, kn_ref, sink_ref, near_ref, far_ref):
    cols = q_ref.shape[1]
    sums = mine_ref[...] + other_ref[...]
    factor = lax.rsqrt(sums / full_width + EPSILON)
    qn_ref[...] = (q_ref[...].astype(jnp.float32) * factor[:, :1] * qg_ref[...]).astype(jnp.bfloat16)
    kn = (k_ref[...].astype(jnp.float32) * factor[:, LANES // 2:LANES // 2 + 1] * kg_ref[...]).astype(jnp.bfloat16)
    kn_ref[...] = kn
    sink_ref[:, :cols] = kn[:FT]
    sink_ref[:, cols:] = v_ref[:FT, :]
    count = frames_ref[0]
    last = pl.multiple_of((count - 1) * FT, FT)
    before = pl.multiple_of(jnp.maximum(count - 2, 0) * FT, FT)
    mark = jnp.full((FT, LANES), count.astype(jnp.float32), jnp.float32).astype(jnp.bfloat16)
    last_k = kn_ref[pl.ds(last, FT), :]
    last_v = v_ref[pl.ds(last, FT), :]
    near_ref[:FT, :cols] = last_k
    near_ref[:FT, cols:2 * cols] = last_v
    near_ref[FT:, :cols] = kn_ref[pl.ds(before, FT), :]
    near_ref[FT:, cols:2 * cols] = v_ref[pl.ds(before, FT), :]
    near_ref[:FT, 2 * cols:] = mark
    near_ref[FT:, 2 * cols:] = mark
    far_ref[:, :cols] = last_k
    far_ref[:, cols:2 * cols] = last_v
    far_ref[:, 2 * cols:] = mark


def attend_kernel(frames_ref, flags_ref, q_ref, k_ref, v_ref, sink_ref, near_ref, far_ref, out_ref):
    rows, cols = q_ref.shape
    count = frames_ref[0]
    use_sink = flags_ref[0, 0] > 0
    use_window = flags_ref[0, 1] > 0
    span = rows + 3 * FT
    slot = lax.broadcasted_iota(jnp.int32, (1, span), 1)
    near_mark = jnp.max(near_ref[:1, 2 * cols:].astype(jnp.float32), axis=1, keepdims=True)
    far_mark = jnp.max(far_ref[:1, 2 * cols:].astype(jnp.float32), axis=1, keepdims=True)
    near_two = near_mark > 1.5
    window = jnp.where(use_window, 1.0, 0.0)
    sink = jnp.where(use_sink, 1.0, 0.0)
    has_last = near_mark * window
    has_before = jnp.where(near_two, near_mark, far_mark) * window
    allow = jnp.where(slot < count * FT, 1.0, 0.0)
    allow = jnp.where(slot >= rows, has_last, allow)
    allow = jnp.where(slot >= rows + FT, has_before, allow)
    allow = jnp.where(slot >= rows + 2 * FT, sink, allow)
    allowed = allow > 0.5
    live = lax.broadcasted_iota(jnp.int32, (rows, HD), 0) < count * FT
    pick = jnp.broadcast_to(near_mark, (FT, HD)) > 1.5
    scaling = 1.0 / math.sqrt(HD)
    for head in range(cols // HD):
        a, b = head * HD, (head + 1) * HD
        keys = jnp.concatenate(
            [k_ref[:, a:b], near_ref[:FT, a:b], jnp.where(pick, near_ref[FT:, a:b], far_ref[:, a:b]), sink_ref[:, a:b]], 0
        )
        a, b = cols + a, cols + b
        vals = jnp.concatenate(
            [v_ref[:, a - cols:b - cols], near_ref[:FT, a:b], jnp.where(pick, near_ref[FT:, a:b], far_ref[:, a:b]),
             sink_ref[:, a:b]], 0
        )
        score = lax.dot_general(
            q_ref[:, a - cols:b - cols], keys, (((1,), (1,)), ((), ())), preferred_element_type=jnp.float32
        ) * scaling
        score = jnp.where(allowed, score, -jnp.inf)
        weight = jnp.exp(score - jnp.max(score, axis=1, keepdims=True)).astype(jnp.bfloat16)
        denominator = jnp.sum(weight.astype(jnp.float32), axis=1, keepdims=True)
        blended = lax.dot_general(weight, vals, (((1,), (0,)), ((), ())), preferred_element_type=jnp.float32)
        out_ref[:, a - cols:b - cols] = jnp.where(live, blended / denominator, 0.0).astype(jnp.bfloat16)


def local(queries, keys, values, q_gain, k_gain, frames, flags):
    rows, cols = queries.shape
    full_width = cols * lax.axis_size("head")
    count = lax.axis_size("tm")
    heads = lax.axis_size("head")
    here = lax.axis_index("tm")
    f32, bf16 = jnp.float32, jnp.bfloat16
    shape = jax.ShapeDtypeStruct

    mine = pl.pallas_call(
        sums_kernel, out_shape=shape((rows, LANES), f32), in_specs=[VMEM] * 2, out_specs=VMEM, name="sums", compiler_params=PARAMS
    )(queries, keys)
    other = lax.ppermute(mine, "head", [(0, 1), (1, 0)])
    qn, kn, sink, near, far = pl.pallas_call(
        lambda *refs: pack_kernel(full_width, *refs),
        out_shape=(
            shape((rows, cols), bf16), shape((rows, cols), bf16), shape((FT, 2 * cols), bf16),
            shape((2 * FT, 2 * cols + LANES), bf16), shape((FT, 2 * cols + LANES), bf16),
        ),
        in_specs=[SMEM] + [VMEM] * 7, out_specs=(VMEM,) * 5, name="pack", compiler_params=PARAMS,
    )(frames, queries, keys, values, q_gain.reshape(1, cols), k_gain.reshape(1, cols), mine, other)

    near_in = lax.ppermute(near, "tm", [(i, i + 1) for i in range(count - 1)])
    far_in = lax.ppermute(far, "tm", [(i, i + 2) for i in range(count - 2)])
    held = here == 0
    for stride, pairs in tree_rounds(count):
        came = lax.ppermute(sink, "tm", pairs)
        sink = jnp.where(held, sink, came)
        held = here < 2 if stride == 1 else here % stride < 2
    return pl.pallas_call(
        attend_kernel, out_shape=shape((rows, cols), bf16), in_specs=[SMEM] * 2 + [VMEM] * 6, out_specs=VMEM, name="attend", compiler_params=PARAMS
    )(frames, flags, qn, kn, values, sink, near_in, far_in)


def solution(mesh):
    placed = (
        P(("groups", "tm"), "head"),
        P(("groups", "tm"), "head"),
        P(("groups", "tm"), "head"),
        P("head"),
        P("head"),
        P(("groups", "tm")),
        P(("groups", "tm"), None),
    )
    return jax.shard_map(
        local, mesh=mesh, in_specs=placed, out_specs=P(("groups", "tm"), "head"), check_vma=False
    )
```

time: 112 us -> 40 us (0.36)
  the two profiles are of different devices: /device:TPU:0 before, /device:TPU:24 now
where the time goes in v1:
time: 40 us; the launch traced here: 39.7 us
  waiting for transfers between devices  23.4 us (58%)
  starting transfers between devices  7.53 us (19%)
  Pallas kernels  4.36 us (11%)
  local copies, waits for them, and re-layouts  3.52 us (9%)
  between operations  0.82 us (2%)
    ppermute x3, waiting for transfers between devices, local(): came = lax.ppermute(sink, 'tm', pairs)  11.7 us
    ppermute x1, waiting for transfers between devices, local(): near_in = lax.ppermute(near, 'tm', [(i, i + 1) for i in range(count - 1)])  9.29 us
    pallas_call x1, Pallas kernels, local(): pl.pallas_call(attend_kernel, out_shape=shape((rows, cols), bf16), in_spe...  4 us
    ppermute x1, starting transfers between devices, local(): near_in = lax.ppermute(near, 'tm', [(i, i + 1) for i in range(count - 1)])  3.53 us
    unnamed x18, local copies, waits for them, and re-layouts  3.51 us
    ppermute x3, starting transfers between devices, local(): came = lax.ppermute(sink, 'tm', pairs)  2.63 us
    ppermute x1, waiting for transfers between devices, local(): far_in = lax.ppermute(far, 'tm', [(i, i + 2) for i in range(count - 2)])  1.89 us
    ppermute x1, starting transfers between devices, local(): far_in = lax.ppermute(far, 'tm', [(i, i + 2) for i in range(count - 2)])  1.29 us
  transfers between devices with their start and end apart: 6, of which 4 were waited for; matrix products, arithmetic and copies ran while one was open for 0% of the time, Pallas kernels for 0%

profile of v1, /device:TPU:24, one launch (start us, length us, event | category | flops | bytes accessed | tf_op | source)
XLA Modules:
  0.0 39.7 jit_solution(2014957855706842115)
XLA Ops:
  0.0 0.0 copy-start
  0.0 0.9 %copy-done = bf16[96,1280]{1,0:T(8,128)(2,1)S(1)} copy-done((bf16[96,1280]{1,0:T(8,128)(2,1)S(1)}, bf16[96,1280]{1,0:T(8,128)(2,1)}, u32[]{:S(2)}) %copy-start) | copy-done | bytes 245784
  0.9 0.0 copy-start.2
  0.9 0.9 %copy-done.2 = bf16[96,1280]{1,0:T(8,128)(2,1)S(1)} copy-done((bf16[96,1280]{1,0:T(8,128)(2,1)S(1)}, bf16[96,1280]{1,0:T(8,128)(2,1)}, u32[]{:S(2)}) %copy-start.2) | copy-done | bytes 245784
  1.9 0.0 copy-start.7
  1.9 0.0 copy-start.1
  1.9 0.0 copy-start.3
  1.9 0.2 sums.1.refs_6_
  2.1 0.0 copy-start.8
  2.1 0.1 collective-permute-start
  2.8 0.0 copy-done.7
  2.8 0.0 copy-done.8
  2.9 0.5 %collective-permute-done.refs_7_ = f32[96,128]{1,0:T(8,128)S(1)} collective-permute-done((f32[96,128]{1,0:T(8,128)S(1)}, f32[96,128]{1,0:T(8,128)S(1)}, u32[]{:S(2)}, u32[]{:S(2)}) %collective-permute-start) | collective-permute-done | bytes 49184 | tf_op jit(solution)/shard_map/ppermute | solution.py:126
  3.4 0.0 copy-done.1
  3.4 0.0 copy-done.3
  3.4 0.0 copy-start.4
  3.4 0.9 %copy-done.4 = bf16[96,1280]{1,0:T(8,128)(2,1)S(1)} copy-done((bf16[96,1280]{1,0:T(8,128)(2,1)S(1)}, bf16[96,1280]{1,0:T(8,128)(2,1)}, u32[]{:S(2)}) %copy-start.4) | copy-done | bytes 245784
  4.3 0.2 pack.1
  4.5 0.7 %collective-permute-start.1 = (bf16[32,2560]{1,0:T(8,128)(2,1)S(1)}, bf16[32,2560]{1,0:T(8,128)(2,1)S(1)}, u32[]{:S(2)}, u32[]{:S(2)}) collective-permute-start(bf16[32,2560]{1,0:T(8,128)(2,1)S(1)} %get-tuple-element.12), channel_id=1, source_target_pairs={{0,2},{1,3},{16,18},{17,19}} | collective-permute-start | bytes 491528 | tf_op jit(solution)/shard_map/ppermute | solution.py:140
  5.2 0.0 collective-permute-done.1
  5.2 0.7 %collective-permute-start.2 = (bf16[32,2560]{1,0:T(8,128)(2,1)S(1)}, bf16[32,2560]{1,0:T(8,128)(2,1)S(1)}, u32[]{:S(2)}, u32[]{:S(2)}) collective-permute-start(bf16[32,2560]{1,0:T(8,128)(2,1)S(1)} %broadcast_select_fusion), channel_id=1, source_target_pairs={{0,8},{2,10},{1,9},{3,11},{16,24},{18,26},{17,25},{19,27}} | collective-permute-start | bytes 491528 | tf_op jit(solution)/shard_map/ppermute | solution.py:140
  5.9 0.0 collective-permute-done.2
  6.0 1.3 %collective-permute-start.3 = (bf16[32,2560]{1,0:T(8,128)(2,1)S(1)}, bf16[32,2560]{1,0:T(8,128)(2,1)S(1)}, u32[]{:S(2)}, u32[]{:S(2)}) collective-permute-start(bf16[32,2560]{1,0:T(8,128)(2,1)S(1)} %broadcast_select_fusion.1), channel_id=1, source_target_pairs={{0,4},{2,6},{8,12},{10,14},{1,5},{3,7},{9,13},{11,15},{16,20},{18,... | collective-permute-start | bytes 491528 | tf_op jit(solution)/shard_map/ppermute | solution.py:140
  7.3 1.3 %collective-permute-start.5 = (bf16[32,2688]{1,0:T(8,128)(2,1)S(1)}, bf16[32,2688]{1,0:T(8,128)(2,1)S(1)}, u32[]{:S(2)}, u32[]{:S(2)}) collective-permute-start(bf16[32,2688]{1,0:T(8,128)(2,1)S(1)} %get-tuple-element.14), channel_id=1, source_target_pairs={{0,4},{2,6},{4,8},{6,10},{8,12},{10,14},{1,5},{3,7},{5,9},{7,11},{... | collective-permute-start | bytes 516104 | tf_op jit(solution)/shard_map/ppermute | solution.py:137
  8.6 0.0 copy-start.5
  8.6 3.5 %collective-permute-start.4 = (bf16[64,2688]{1,0:T(8,128)(2,1)S(1)}, bf16[64,2688]{1,0:T(8,128)(2,1)S(1)}, u32[]{:S(2)}, u32[]{:S(2)}) collective-permute-start(bf16[64,2688]{1,0:T(8,128)(2,1)S(1)} %get-tuple-element.13), channel_id=1, source_target_pairs={{0,2},{2,4},{4,6},{6,8},{8,10},{10,12},{12,14},{1,3},{3,5},{5,7},{... | collective-permute-start | bytes 1032200 | tf_op jit(solution)/shard_map/ppermute | solution.py:136
  12.1 11.7 %collective-permute-done.3 = bf16[32,2560]{1,0:T(8,128)(2,1)S(1)} collective-permute-done((bf16[32,2560]{1,0:T(8,128)(2,1)S(1)}, bf16[32,2560]{1,0:T(8,128)(2,1)S(1)}, u32[]{:S(2)}, u32[]{:S(2)}) %collective-permute-start.3) | collective-permute-done | bytes 163872 | tf_op jit(solution)/shard_map/ppermute | solution.py:140
  23.8 1.9 %collective-permute-done.5.far_ref = bf16[32,2688]{1,0:T(8,128)(2,1)S(1)} collective-permute-done((bf16[32,2688]{1,0:T(8,128)(2,1)S(1)}, bf16[32,2688]{1,0:T(8,128)(2,1)S(1)}, u32[]{:S(2)}, u32[]{:S(2)}) %collective-permute-start.5) | collective-permute-done | bytes 172064 | tf_op jit(solution)/shard_map/ppermute | solution.py:137
  25.7 9.3 %collective-permute-done.4.near_ref = bf16[64,2688]{1,0:T(8,128)(2,1)S(1)} collective-permute-done((bf16[64,2688]{1,0:T(8,128)(2,1)S(1)}, bf16[64,2688]{1,0:T(8,128)(2,1)S(1)}, u32[]{:S(2)}, u32[]{:S(2)}) %collective-permute-start.4) | collective-permute-done | bytes 344096 | tf_op jit(solution)/shard_map/ppermute | solution.py:136
  35.0 0.0 copy-start.6
  35.0 0.0 copy-done.5
  35.0 0.7 %copy-done.6 = s32[1,2]{1,0:T(1,128)S(1)} copy-done((s32[1,2]{1,0:T(1,128)S(1)}, s32[1,2]{1,0:T(1,128)}, u32[]{:S(2)}) %copy-start.6) | copy-done | bytes 32
  35.7 4.0 %attend.1 = bf16[96,1280]{1,0:T(8,128)(2,1)} custom-call(s32[1]{0:T(128)S(6)} %copy.8.refs_0_.frames_ref, s32[1,2]{1,0:T(1,128)S(1)} %copy-done.6, bf16[96,1280]{1,0:T(8,128)(2,1)S(1)} %get-tuple-element.10.q_ref, bf16[96,1280]{1,0:T(8,128)(2,1)S(1)} %get-tuple-element.11.k_ref, bf16[96,1280]{1,0:T(8,128)(2,1)S(1)} %copy-done.5, ...), custom_call_target="tpu_custom_call" | custom-call | tf_op jit(solution)/shard_map/attend/pallas_call | solution.py:143
  (5 shorter events, 0.1 us)
Async XLA Ops:
  0.0 0.9 %copy-start = (bf16[96,1280]{1,0:T(8,128)(2,1)S(1)}, bf16[96,1280]{1,0:T(8,128)(2,1)}, u32[]{:S(2)}) copy-start(bf16[96,1280]{1,0:T(8,128)(2,1)} %refs_1_.1) | copy-start | bytes 737284
  0.9 0.9 %copy-start.2 = (bf16[96,1280]{1,0:T(8,128)(2,1)S(1)}, bf16[96,1280]{1,0:T(8,128)(2,1)}, u32[]{:S(2)}) copy-start(bf16[96,1280]{1,0:T(8,128)(2,1)} %refs_2_.1) | copy-start | bytes 737284
  1.9 0.9 %copy-start.7 = (f32[1280]{0:T(1024)S(1)}, f32[1280]{0:T(1024)}, u32[]{:S(2)}) copy-start(f32[1280]{0:T(1024)} %param.10) | copy-start | bytes 15364
  1.9 1.5 %copy-start.1 = (bf16[96,1280]{1,0:T(8,128)(2,1)S(1)}, bf16[96,1280]{1,0:T(8,128)(2,1)}, u32[]{:S(2)}) copy-start(bf16[96,1280]{1,0:T(8,128)(2,1)} %refs_1_.1) | copy-start | bytes 737284
  1.9 1.5 %copy-start.3 = (bf16[96,1280]{1,0:T(8,128)(2,1)S(1)}, bf16[96,1280]{1,0:T(8,128)(2,1)}, u32[]{:S(2)}) copy-start(bf16[96,1280]{1,0:T(8,128)(2,1)} %refs_2_.1) | copy-start | bytes 737284
  2.1 0.8 %copy-start.8 = (f32[1280]{0:T(1024)S(1)}, f32[1280]{0:T(1024)}, u32[]{:S(2)}) copy-start(f32[1280]{0:T(1024)} %param.11) | copy-start | bytes 15364
  2.1 1.3 %collective-permute-start = (f32[96,128]{1,0:T(8,128)S(1)}, f32[96,128]{1,0:T(8,128)S(1)}, u32[]{:S(2)}, u32[]{:S(2)}) collective-permute-start(f32[96,128]{1,0:T(8,128)S(1)} %sums.1.refs_6_), channel_id=1, source_target_pairs={{0,1},{1,0},{2,3},{3,2},{4,5},{5,4},{6,7},{7,6},{8,9},{9,8},{10,11... | collective-permute-start | bytes 147464 | tf_op jit(solution)/shard_map/ppermute | solution.py:126
  3.4 0.9 %copy-start.4 = (bf16[96,1280]{1,0:T(8,128)(2,1)S(1)}, bf16[96,1280]{1,0:T(8,128)(2,1)}, u32[]{:S(2)}) copy-start(bf16[96,1280]{1,0:T(8,128)(2,1)} %v_ref.1) | copy-start | bytes 737284
  4.5 0.7 %collective-permute-start.1 = (bf16[32,2560]{1,0:T(8,128)(2,1)S(1)}, bf16[32,2560]{1,0:T(8,128)(2,1)S(1)}, u32[]{:S(2)}, u32[]{:S(2)}) collective-permute-start(bf16[32,2560]{1,0:T(8,128)(2,1)S(1)} %get-tuple-element.12), channel_id=1, source_target_pairs={{0,2},{1,3},{16,18},{17,19}} | collective-permute-start | bytes 491528 | tf_op jit(solution)/shard_map/ppermute | solution.py:140
  5.2 0.7 %collective-permute-start.2 = (bf16[32,2560]{1,0:T(8,128)(2,1)S(1)}, bf16[32,2560]{1,0:T(8,128)(2,1)S(1)}, u32[]{:S(2)}, u32[]{:S(2)}) collective-permute-start(bf16[32,2560]{1,0:T(8,128)(2,1)S(1)} %broadcast_select_fusion), channel_id=1, source_target_pairs={{0,8},{2,10},{1,9},{3,11},{16,24},{18,26},{17,25},{19,27}} | collective-permute-start | bytes 491528 | tf_op jit(solution)/shard_map/ppermute | solution.py:140
  6.0 17.8 %collective-permute-start.3 = (bf16[32,2560]{1,0:T(8,128)(2,1)S(1)}, bf16[32,2560]{1,0:T(8,128)(2,1)S(1)}, u32[]{:S(2)}, u32[]{:S(2)}) collective-permute-start(bf16[32,2560]{1,0:T(8,128)(2,1)S(1)} %broadcast_select_fusion.1), channel_id=1, source_target_pairs={{0,4},{2,6},{8,12},{10,14},{1,5},{3,7},{9,13},{11,15},{16,20},{18,... | collective-permute-start | bytes 491528 | tf_op jit(solution)/shard_map/ppermute | solution.py:140
  7.3 18.4 %collective-permute-start.5 = (bf16[32,2688]{1,0:T(8,128)(2,1)S(1)}, bf16[32,2688]{1,0:T(8,128)(2,1)S(1)}, u32[]{:S(2)}, u32[]{:S(2)}) collective-permute-start(bf16[32,2688]{1,0:T(8,128)(2,1)S(1)} %get-tuple-element.14), channel_id=1, source_target_pairs={{0,4},{2,6},{4,8},{6,10},{8,12},{10,14},{1,5},{3,7},{5,9},{7,11},{... | collective-permute-start | bytes 516104 | tf_op jit(solution)/shard_map/ppermute | solution.py:137
  8.6 26.4 %copy-start.5 = (bf16[96,1280]{1,0:T(8,128)(2,1)S(1)}, bf16[96,1280]{1,0:T(8,128)(2,1)}, u32[]{:S(2)}) copy-start(bf16[96,1280]{1,0:T(8,128)(2,1)} %v_ref.1) | copy-start | bytes 737284
  8.6 26.4 %collective-permute-start.4 = (bf16[64,2688]{1,0:T(8,128)(2,1)S(1)}, bf16[64,2688]{1,0:T(8,128)(2,1)S(1)}, u32[]{:S(2)}, u32[]{:S(2)}) collective-permute-start(bf16[64,2688]{1,0:T(8,128)(2,1)S(1)} %get-tuple-element.13), channel_id=1, source_target_pairs={{0,2},{2,4},{4,6},{6,8},{8,10},{10,12},{12,14},{1,3},{3,5},{5,7},{... | collective-permute-start | bytes 1032200 | tf_op jit(solution)/shard_map/ppermute | solution.py:136
  35.0 0.7 %copy-start.6 = (s32[1,2]{1,0:T(1,128)S(1)}, s32[1,2]{1,0:T(1,128)}, u32[]{:S(2)}) copy-start(s32[1,2]{1,0:T(1,128)} %flags_ref.1) | copy-start | bytes 28

commit v2 on v1

v2 whole, which is shorter than its diff:
```python
import math

import jax
import jax.numpy as jnp
from jax import lax
from jax.experimental import pallas as pl
from jax.experimental.pallas import tpu as pltpu
from jax.sharding import PartitionSpec as P


HD = 128
FT = 32
EPSILON = 1e-06
LANES = 128
VMEM = pl.BlockSpec(memory_space=pltpu.VMEM)
HBM = pl.BlockSpec(memory_space=pltpu.HBM)
PARAMS = pltpu.CompilerParams(vmem_limit_bytes=8 << 20)
F32 = jnp.float32
BF16 = jnp.bfloat16


def tree_rounds(count):
    top = 1
    while top * 2 < count:
        top *= 2
    strides = [1] if count > 1 else []
    while top >= 2:
        strides.append(top)
        top //= 2
    held, rounds = [0], []
    for stride in strides:
        pairs = [(h, h + stride) for h in held if h + stride < count and h + stride not in held]
        rounds.append((stride, pairs))
        held = held + [target for _, target in pairs]
    return rounds


def call(kernel, shapes, operands, specs=None, scratch=(), aliases=None):
    single = not isinstance(shapes, tuple)
    return pl.pallas_call(
        kernel,
        out_shape=shapes,
        in_specs=[VMEM] * len(operands) if specs is None else specs,
        out_specs=VMEM if single else (VMEM,) * len(shapes),
        scratch_shapes=list(scratch),
        input_output_aliases=aliases or {},
        compiler_params=PARAMS,
    )(*operands)


def lead_kernel(k_ref, v_ref, sink_ref, sums_ref, sem):
    cols = k_ref.shape[1]

    @pl.when(lax.axis_index("tm") == 0)
    def _():
        first = pltpu.make_async_copy(k_ref.at[:FT, :], sink_ref.at[:, :cols], sem.at[0])
        second = pltpu.make_async_copy(v_ref.at[:FT, :], sink_ref.at[:, cols:], sem.at[1])
        first.start()
        second.start()
        first.wait()
        k = sink_ref[:, :cols].astype(F32)
        sums_ref[...] = jnp.broadcast_to(jnp.sum(k * k, axis=1, keepdims=True), sums_ref.shape)
        second.wait()


def lead_norm_kernel(full_width, raw_ref, kg_ref, mine_ref, other_ref, sink_ref):
    cols = kg_ref.shape[1]

    @pl.when(lax.axis_index("tm") == 0)
    def _():
        factor = lax.rsqrt((mine_ref[:, :1] + other_ref[:, :1]) / full_width + EPSILON)
        sink_ref[:, :cols] = (raw_ref[:, :cols].astype(F32) * factor * kg_ref[...]).astype(BF16)
        sink_ref[:, cols:] = raw_ref[:, cols:]


def sums_kernel(q_ref, k_ref, sums_ref):
    q = q_ref[...].astype(F32)
    k = k_ref[...].astype(F32)
    q_sum = jnp.sum(q * q, axis=1, keepdims=True)
    k_sum = jnp.sum(k * k, axis=1, keepdims=True)
    lane = lax.broadcasted_iota(jnp.int32, sums_ref.shape, 1)
    sums_ref[...] = jnp.where(lane < LANES // 2, q_sum, k_sum)


def pack_kernel(full_width, frames_ref, q_ref, k_ref, v_ref, qg_ref, kg_ref, mine_ref, other_ref,
                qn_ref, kn_ref, near_ref, far_ref):
    rows, cols = q_ref.shape
    factor = lax.rsqrt((mine_ref[...] + other_ref[...]) / full_width + EPSILON)
    qn_ref[...] = (q_ref[...].astype(F32) * factor[:, :1] * qg_ref[...]).astype(BF16)
    kn_ref[...] = (k_ref[...].astype(F32) * factor[:, LANES // 2:LANES // 2 + 1] * kg_ref[...]).astype(BF16)
    count = frames_ref[...].reshape(1, 1).astype(F32)
    counts = jnp.broadcast_to(count, (FT, cols))
    mark = jnp.broadcast_to(count, (FT, LANES)).astype(BF16)
    for ref, at in ((kn_ref, 0), (v_ref, cols)):
        last, before = ref[:FT, :], ref[:FT, :]
        for frame in range(1, rows // FT):
            here = ref[frame * FT:(frame + 1) * FT, :]
            last = jnp.where(counts > frame + 0.5, here, last)
            before = jnp.where(counts > frame + 1.5, here, before)
        near_ref[:FT, at:at + cols] = last
        near_ref[FT:, at:at + cols] = before
        far_ref[:, at:at + cols] = last
    near_ref[:FT, 2 * cols:] = mark
    near_ref[FT:, 2 * cols:] = mark
    far_ref[:, 2 * cols:] = mark


def fold_kernel(frames_ref, flags_ref, q_ref, k_ref, v_ref, near_ref, far_ref, acc_ref, top_ref, den_ref):
    rows, cols = q_ref.shape
    span = rows + 2 * FT
    slot = lax.broadcasted_iota(jnp.int32, (1, span), 1)
    count = frames_ref[...].reshape(1, 1)
    window = jnp.where(flags_ref[:, 1:2] > 0, 1.0, 0.0)
    near_mark = near_ref[:1, 2 * cols:2 * cols + 1].astype(F32)
    far_mark = far_ref[:1, 2 * cols:2 * cols + 1].astype(F32)
    has_last = near_mark * window
    has_before = jnp.where(near_mark > 1.5, near_mark, far_mark) * window
    allow = jnp.where(slot < count * FT, 1.0, 0.0)
    allow = jnp.where(slot >= rows, has_last, allow)
    allow = jnp.where(slot >= rows + FT, has_before, allow)
    allowed = allow > 0.5
    pick = jnp.broadcast_to(near_mark, (FT, HD)) > 1.5
    ones = jnp.ones((span, HD), BF16)
    for head in range(cols // HD):
        a = head * HD
        b = a + HD
        near_k, far_k = near_ref[FT:, a:b], far_ref[:, a:b]
        keys = jnp.concatenate([k_ref[:, a:b], near_ref[:FT, a:b], jnp.where(pick, near_k, far_k)], 0)
        near_v, far_v = near_ref[FT:, cols + a:cols + b], far_ref[:, cols + a:cols + b]
        vals = jnp.concatenate([v_ref[:, a:b], near_ref[:FT, cols + a:cols + b], jnp.where(pick, near_v, far_v)], 0)
        score = lax.dot_general(
            q_ref[:, a:b], keys, (((1,), (1,)), ((), ())), preferred_element_type=F32
        ) * (1.0 / math.sqrt(HD))
        score = jnp.where(allowed, score, -jnp.inf)
        top = jnp.max(score, axis=1, keepdims=True)
        weight = jnp.exp(score - top).astype(BF16)
        both = jnp.dot(weight, jnp.concatenate([vals, ones], 1), preferred_element_type=F32)
        acc_ref[:, a:b] = both[:, :HD]
        den_ref[:, a:b] = both[:, HD:]
        top_ref[:, a:b] = jnp.broadcast_to(top, (rows, HD))


def finish_kernel(frames_ref, flags_ref, q_ref, sink_ref, acc_ref, top_ref, den_ref, out_ref):
    rows, cols = q_ref.shape
    use_sink = jnp.broadcast_to(flags_ref[:, 0:1], (rows, FT)) > 0
    live = lax.broadcasted_iota(jnp.int32, (rows, HD), 0) < frames_ref[...].reshape(1, 1) * FT
    ones = jnp.ones((FT, HD), BF16)
    for head in range(cols // HD):
        a = head * HD
        b = a + HD
        score = lax.dot_general(
            q_ref[:, a:b], sink_ref[:, a:b], (((1,), (1,)), ((), ())), preferred_element_type=F32
        ) * (1.0 / math.sqrt(HD))
        score = jnp.where(use_sink, score, -jnp.inf)
        old = top_ref[:, a:b]
        top = jnp.maximum(old, jnp.max(score, axis=1, keepdims=True))
        weight = jnp.exp(score - top[:, :FT]).astype(BF16)
        both = jnp.dot(
            weight, jnp.concatenate([sink_ref[:, cols + a:cols + b], ones], 1), preferred_element_type=F32
        )
        keep = jnp.exp(old - top)
        blended = (acc_ref[:, a:b] * keep + both[:, :HD]) / (den_ref[:, a:b] * keep + both[:, HD:])
        out_ref[:, a:b] = jnp.where(live, blended, 0.0).astype(BF16)


def local(queries, keys, values, q_gain, k_gain, frames, flags):
    rows, cols = queries.shape
    heads = lax.axis_size("head")
    full_width = cols * heads
    count = lax.axis_size("tm")
    here = lax.axis_index("tm")
    shape = jax.ShapeDtypeStruct
    q_gain, k_gain = q_gain.reshape(1, cols), k_gain.reshape(1, cols)
    swap = [(h, (h + 1) % heads) for h in range(heads)]

    raw, mine = call(
        lead_kernel, (shape((FT, 2 * cols), BF16), shape((FT, LANES), F32)),
        (pltpu.with_memory_space_constraint(keys, pltpu.HBM), pltpu.with_memory_space_constraint(values, pltpu.HBM)),
        specs=[HBM, HBM], scratch=[pltpu.SemaphoreType.DMA((2,))],
    )
    other = lax.ppermute(mine, ("tm", "head"), swap)
    sink = call(
        lambda *refs: lead_norm_kernel(full_width, *refs), shape((FT, 2 * cols), BF16),
        (raw, k_gain, mine, other),
    )
    mine = call(sums_kernel, shape((rows, LANES), F32), (queries, keys))
    other = lax.ppermute(mine, "head", swap)
    qn, kn, near, far = call(
        lambda *refs: pack_kernel(full_width, *refs),
        (
            shape((rows, cols), BF16), shape((rows, cols), BF16),
            shape((2 * FT, 2 * cols + LANES), BF16), shape((FT, 2 * cols + LANES), BF16),
        ),
        (frames, queries, keys, values, q_gain, k_gain, mine, other),
    )
    near = lax.ppermute(near, "tm", [(i, i + 1) for i in range(count - 1)])
    far = lax.ppermute(far, "tm", [(i, i + 2) for i in range(count - 2)])
    rounds = tree_rounds(count)
    held = here == 0
    for stride, pairs in rounds:
        came = lax.ppermute(sink, "tm", pairs)
        sink = jnp.where(held, sink, came)
        held = here < 2 if stride == 1 else here % stride < 2
    acc, top, den = call(fold_kernel, (shape((rows, cols), F32),) * 3, (frames, flags, qn, kn, values, near, far))
    return call(finish_kernel, shape((rows, cols), BF16), (frames, flags, qn, sink, acc, top, den))


def solution(mesh):
    placed = (
        P(("groups", "tm"), "head"),
        P(("groups", "tm"), "head"),
        P(("groups", "tm"), "head"),
        P("head"),
        P("head"),
        P(("groups", "tm")),
        P(("groups", "tm"), None),
    )
    return jax.shard_map(
        local, mesh=mesh, in_specs=placed, out_specs=P(("groups", "tm"), "head"), check_vma=False
    )
```

time: 40 us -> 34.7 us (0.87)
  the two profiles are of different devices: /device:TPU:24 before, /device:TPU:12 now
where the time goes in v2:
time: 34.7 us; the launch traced here: 34.4 us
  waiting for transfers between devices  16.6 us (48%)
  starting transfers between devices  10.9 us (31%)
  Pallas kernels  5.11 us (15%)
  local copies, waits for them, and re-layouts  0.87 us (3%)
  between operations  0.87 us (3%)
    ppermute x1, waiting for transfers between devices, local(): near = lax.ppermute(near, 'tm', [(i, i + 1) for i in range(count - 1)])  9.82 us
    ppermute x1, waiting for transfers between devices, local(): far = lax.ppermute(far, 'tm', [(i, i + 2) for i in range(count - 2)])  6.25 us
    pallas_call x6, Pallas kernels, call(): pl.pallas_call(kernel, out_shape=shapes, in_specs=[VMEM] * len(operands)...  5.11 us
    ppermute x1, starting transfers between devices, local(): far = lax.ppermute(far, 'tm', [(i, i + 2) for i in range(count - 2)])  3.96 us
    ppermute x1, starting transfers between devices, local(): near = lax.ppermute(near, 'tm', [(i, i + 1) for i in range(count - 1)])  3.4 us
    ppermute x3, starting transfers between devices, local(): came = lax.ppermute(sink, 'tm', pairs)  2.77 us
    unnamed x12, local copies, waits for them, and re-layouts  0.86 us
  transfers between devices with their start and end apart: 7, of which 3 were waited for; matrix products, arithmetic and copies ran while one was open for 0% of the time, Pallas kernels for 8%

profile of v2, /device:TPU:12, one launch (start us, length us, event | category | flops | bytes accessed | tf_op | source)
XLA Modules:
  0.0 34.4 jit_solution(6700324176117439548)
XLA Ops:
  0.0 0.0 copy-start.4
  0.0 0.7 %collective-permute-start.1 = (f32[32,128]{1,0:T(8,128)S(1)}, f32[32,128]{1,0:T(8,128)S(1)}, u32[]{:S(2)}, u32[]{:S(2)}) collective-permute-start(f32[32,128]{1,0:T(8,128)S(1)} %get-tuple-element.16.refs_2_), channel_id=1, source_target_pairs={{0,1},{1,0},{16,17},{17,16}} | collective-permute-start | bytes 49160 | tf_op jit(solution)/shard_map/ppermute | solution.py:181
  0.7 0.0 copy-done.4
  0.7 0.0 collective-permute-done.1.refs_3_
  0.8 0.7 %collective-permute-start.2 = (bf16[32,2560]{1,0:T(8,128)(2,1)S(1)}, bf16[32,2560]{1,0:T(8,128)(2,1)S(1)}, u32[]{:S(2)}, u32[]{:S(2)}) collective-permute-start(bf16[32,2560]{1,0:T(8,128)(2,1)S(1)} %shard_map.76), channel_id=1, source_target_pairs={{0,2},{1,3},{16,18},{17,19}} | collective-permute-start | bytes 491528 | tf_op jit(solution)/shard_map/ppermute | solution.py:201
  1.4 0.0 copy-start
  1.5 0.0 copy-start.2
  1.5 0.0 collective-permute-done.2
  1.5 0.0 copy-start.1
  1.5 0.8 %collective-permute-start.3 = (bf16[32,2560]{1,0:T(8,128)(2,1)S(1)}, bf16[32,2560]{1,0:T(8,128)(2,1)S(1)}, u32[]{:S(2)}, u32[]{:S(2)}) collective-permute-start(bf16[32,2560]{1,0:T(8,128)(2,1)S(1)} %broadcast_select_fusion), channel_id=1, source_target_pairs={{0,8},{2,10},{1,9},{3,11},{16,24},{18,26},{17,25},{19,27}} | collective-permute-start | bytes 491528 | tf_op jit(solution)/shard_map/ppermute | solution.py:201
  2.3 0.1 copy-done
  2.4 0.1 copy-done.2
  2.5 0.0 copy-start.5
  2.5 0.2 shard_map.73.refs_6_
  2.7 0.1 collective-permute-start
  3.4 0.0 copy-done.5
  3.4 0.5 %collective-permute-done.refs_7_ = f32[96,128]{1,0:T(8,128)S(1)} collective-permute-done((f32[96,128]{1,0:T(8,128)S(1)}, f32[96,128]{1,0:T(8,128)S(1)}, u32[]{:S(2)}, u32[]{:S(2)}) %collective-permute-start) | collective-permute-done | bytes 49184 | tf_op jit(solution)/shard_map/ppermute | solution.py:187
  4.0 0.0 copy-done.1
  4.0 0.2 shard_map.74
  4.2 4.0 %collective-permute-start.6 = (bf16[32,2688]{1,0:T(8,128)(2,1)S(1)}, bf16[32,2688]{1,0:T(8,128)(2,1)S(1)}, u32[]{:S(2)}, u32[]{:S(2)}) collective-permute-start(bf16[32,2688]{1,0:T(8,128)(2,1)S(1)} %get-tuple-element.19), channel_id=1, source_target_pairs={{0,4},{2,6},{4,8},{6,10},{8,12},{10,14},{1,5},{3,7},{5,9},{7,11},{... | collective-permute-start | bytes 516104 | tf_op jit(solution)/shard_map/ppermute | solution.py:197
  8.2 3.4 %collective-permute-start.5 = (bf16[64,2688]{1,0:T(8,128)(2,1)S(1)}, bf16[64,2688]{1,0:T(8,128)(2,1)S(1)}, u32[]{:S(2)}, u32[]{:S(2)}) collective-permute-start(bf16[64,2688]{1,0:T(8,128)(2,1)S(1)} %get-tuple-element.18), channel_id=1, source_target_pairs={{0,2},{2,4},{4,6},{6,8},{8,10},{10,12},{12,14},{1,3},{3,5},{5,7},{... | collective-permute-start | bytes 1032200 | tf_op jit(solution)/shard_map/ppermute | solution.py:196
  11.6 0.0 collective-permute-done.3
  11.6 1.3 %collective-permute-start.4 = (bf16[32,2560]{1,0:T(8,128)(2,1)S(1)}, bf16[32,2560]{1,0:T(8,128)(2,1)S(1)}, u32[]{:S(2)}, u32[]{:S(2)}) collective-permute-start(bf16[32,2560]{1,0:T(8,128)(2,1)S(1)} %broadcast_select_fusion.1), channel_id=1, source_target_pairs={{0,4},{2,6},{8,12},{10,14},{1,5},{3,7},{9,13},{11,15},{16,20},{18,... | collective-permute-start | bytes 491528 | tf_op jit(solution)/shard_map/ppermute | solution.py:201
  12.9 6.2 %collective-permute-done.6.far_ref = bf16[32,2688]{1,0:T(8,128)(2,1)S(1)} collective-permute-done((bf16[32,2688]{1,0:T(8,128)(2,1)S(1)}, bf16[32,2688]{1,0:T(8,128)(2,1)S(1)}, u32[]{:S(2)}, u32[]{:S(2)}) %collective-permute-start.6) | collective-permute-done | bytes 172064 | tf_op jit(solution)/shard_map/ppermute | solution.py:197
  19.2 9.8 %collective-permute-done.5.near_ref = bf16[64,2688]{1,0:T(8,128)(2,1)S(1)} collective-permute-done((bf16[64,2688]{1,0:T(8,128)(2,1)S(1)}, bf16[64,2688]{1,0:T(8,128)(2,1)S(1)}, u32[]{:S(2)}, u32[]{:S(2)}) %collective-permute-start.5) | collective-permute-done | bytes 344096 | tf_op jit(solution)/shard_map/ppermute | solution.py:196
  29.0 0.0 copy-start.3
  29.0 0.7 %copy-done.3 = s32[1,2]{1,0:T(1,128)S(1)} copy-done((s32[1,2]{1,0:T(1,128)S(1)}, s32[1,2]{1,0:T(1,128)}, u32[]{:S(2)}) %copy-start.3) | copy-done | bytes 32
  29.7 2.4 %shard_map.77 = (f32[96,1280]{1,0:T(8,128)S(1)}, f32[96,1280]{1,0:T(8,128)S(1)}, f32[96,1280]{1,0:T(8,128)S(1)}) custom-call(s32[1]{0:T(128)S(6)} %copy.8.refs_0_.frames_ref, s32[1,2]{1,0:T(1,128)S(1)} %copy-done.3, bf16[96,1280]{1,0:T(8,128)(2,1)S(1)} %get-tuple-element.14.q_ref, bf16[96,1280]{1,0:T(8,128)(2,1)S(1)} %get-tuple-element.17.k_ref, ...), custom_call_target="tpu_custom_call" | custom-call | tf_op jit(solution)/shard_map/pallas_call | solution.py:40
  32.1 0.0 collective-permute-done.4
  32.1 2.3 %shard_map.78 = bf16[96,1280]{1,0:T(8,128)(2,1)} custom-call(s32[1]{0:T(128)S(6)} %copy.8.refs_0_.frames_ref, s32[1,2]{1,0:T(1,128)S(1)} %copy-done.3, bf16[96,1280]{1,0:T(8,128)(2,1)S(1)} %get-tuple-element.14.q_ref, bf16[32,2560]{1,0:T(8,128)(2,1)S(1)} %broadcast_select_fusion.2.sink_ref, f32[96,1280]{1,0:T(8,128)S(1)} %get-tuple-element.20.acc_ref, ...), custom_call_target="tpu_custom_call" | custom-call | tf_op jit(solution)/shard_map/pallas_call | solution.py:40
  (7 shorter events, 0.1 us)
Async XLA Ops:
  0.0 0.7 %copy-start.4 = (f32[1280]{0:T(1024)S(1)}, f32[1280]{0:T(1024)}, u32[]{:S(2)}) copy-start(f32[1280]{0:T(1024)} %param.11) | copy-start | bytes 15364
  0.0 0.7 %collective-permute-start.1 = (f32[32,128]{1,0:T(8,128)S(1)}, f32[32,128]{1,0:T(8,128)S(1)}, u32[]{:S(2)}, u32[]{:S(2)}) collective-permute-start(f32[32,128]{1,0:T(8,128)S(1)} %get-tuple-element.16.refs_2_), channel_id=1, source_target_pairs={{0,1},{1,0},{16,17},{17,16}} | collective-permute-start | bytes 49160 | tf_op jit(solution)/shard_map/ppermute | solution.py:181
  0.8 0.7 %collective-permute-start.2 = (bf16[32,2560]{1,0:T(8,128)(2,1)S(1)}, bf16[32,2560]{1,0:T(8,128)(2,1)S(1)}, u32[]{:S(2)}, u32[]{:S(2)}) collective-permute-start(bf16[32,2560]{1,0:T(8,128)(2,1)S(1)} %shard_map.76), channel_id=1, source_target_pairs={{0,2},{1,3},{16,18},{17,19}} | collective-permute-start | bytes 491528 | tf_op jit(solution)/shard_map/ppermute | solution.py:201
  1.4 0.9 %copy-start = (bf16[96,1280]{1,0:T(8,128)(2,1)S(1)}, bf16[96,1280]{1,0:T(8,128)(2,1)}, u32[]{:S(2)}) copy-start(bf16[96,1280]{1,0:T(8,128)(2,1)} %k_ref.3) | copy-start | bytes 737284
  1.5 1.1 %copy-start.2 = (bf16[96,1280]{1,0:T(8,128)(2,1)S(1)}, bf16[96,1280]{1,0:T(8,128)(2,1)}, u32[]{:S(2)}) copy-start(bf16[96,1280]{1,0:T(8,128)(2,1)} %refs_1_.1) | copy-start | bytes 737284
  1.5 2.5 %copy-start.1 = (bf16[96,1280]{1,0:T(8,128)(2,1)S(1)}, bf16[96,1280]{1,0:T(8,128)(2,1)}, u32[]{:S(2)}) copy-start(bf16[96,1280]{1,0:T(8,128)(2,1)} %v_ref.3) | copy-start | bytes 737284
  1.5 10.1 %collective-permute-start.3 = (bf16[32,2560]{1,0:T(8,128)(2,1)S(1)}, bf16[32,2560]{1,0:T(8,128)(2,1)S(1)}, u32[]{:S(2)}, u32[]{:S(2)}) collective-permute-start(bf16[32,2560]{1,0:T(8,128)(2,1)S(1)} %broadcast_select_fusion), channel_id=1, source_target_pairs={{0,8},{2,10},{1,9},{3,11},{16,24},{18,26},{17,25},{19,27}} | collective-permute-start | bytes 491528 | tf_op jit(solution)/shard_map/ppermute | solution.py:201
  2.5 0.9 %copy-start.5 = (f32[1280]{0:T(1024)S(1)}, f32[1280]{0:T(1024)}, u32[]{:S(2)}) copy-start(f32[1280]{0:T(1024)} %param.10) | copy-start | bytes 15364
  2.7 1.3 %collective-permute-start = (f32[96,128]{1,0:T(8,128)S(1)}, f32[96,128]{1,0:T(8,128)S(1)}, u32[]{:S(2)}, u32[]{:S(2)}) collective-permute-start(f32[96,128]{1,0:T(8,128)S(1)} %shard_map.73.refs_6_), channel_id=1, source_target_pairs={{0,1},{1,0},{2,3},{3,2},{4,5},{5,4},{6,7},{7,6},{8,9},{9,8},{10,11... | collective-permute-start | bytes 147464 | tf_op jit(solution)/shard_map/ppermute | solution.py:187
  4.2 15.0 %collective-permute-start.6 = (bf16[32,2688]{1,0:T(8,128)(2,1)S(1)}, bf16[32,2688]{1,0:T(8,128)(2,1)S(1)}, u32[]{:S(2)}, u32[]{:S(2)}) collective-permute-start(bf16[32,2688]{1,0:T(8,128)(2,1)S(1)} %get-tuple-element.19), channel_id=1, source_target_pairs={{0,4},{2,6},{4,8},{6,10},{8,12},{10,14},{1,5},{3,7},{5,9},{7,11},{... | collective-permute-start | bytes 516104 | tf_op jit(solution)/shard_map/ppermute | solution.py:197
  8.2 20.8 %collective-permute-start.5 = (bf16[64,2688]{1,0:T(8,128)(2,1)S(1)}, bf16[64,2688]{1,0:T(8,128)(2,1)S(1)}, u32[]{:S(2)}, u32[]{:S(2)}) collective-permute-start(bf16[64,2688]{1,0:T(8,128)(2,1)S(1)} %get-tuple-element.18), channel_id=1, source_target_pairs={{0,2},{2,4},{4,6},{6,8},{8,10},{10,12},{12,14},{1,3},{3,5},{5,7},{... | collective-permute-start | bytes 1032200 | tf_op jit(solution)/shard_map/ppermute | solution.py:196
  11.6 20.5 %collective-permute-start.4 = (bf16[32,2560]{1,0:T(8,128)(2,1)S(1)}, bf16[32,2560]{1,0:T(8,128)(2,1)S(1)}, u32[]{:S(2)}, u32[]{:S(2)}) collective-permute-start(bf16[32,2560]{1,0:T(8,128)(2,1)S(1)} %broadcast_select_fusion.1), channel_id=1, source_target_pairs={{0,4},{2,6},{8,12},{10,14},{1,5},{3,7},{9,13},{11,15},{16,20},{18,... | collective-permute-start | bytes 491528 | tf_op jit(solution)/shard_map/ppermute | solution.py:201
  29.0 0.7 %copy-start.3 = (s32[1,2]{1,0:T(1,128)S(1)}, s32[1,2]{1,0:T(1,128)}, u32[]{:S(2)}) copy-start(s32[1,2]{1,0:T(1,128)} %flags_ref.3) | copy-start | bytes 28

commit v3 on v2

v3 whole, which is shorter than its diff:
```python
import math

import jax
import jax.numpy as jnp
from jax import lax
from jax.experimental import pallas as pl
from jax.experimental.pallas import tpu as pltpu
from jax.sharding import PartitionSpec as P


HD = 128
FT = 32
EPSILON = 1e-06
LANES = 128
VMEM = pl.BlockSpec(memory_space=pltpu.VMEM)
HBM = pl.BlockSpec(memory_space=pltpu.HBM)
SMEM = pl.BlockSpec(memory_space=pltpu.SMEM)
PARAMS = pltpu.CompilerParams(vmem_limit_bytes=8 << 20)
F32 = jnp.float32
BF16 = jnp.bfloat16


def tree_rounds(count):
    top = 1
    while top * 2 < count:
        top *= 2
    strides = [2] if count > 2 else []
    while top >= 4:
        strides.append(top)
        top //= 2
    strides.append(1)
    held, rounds = [0], []
    for number, stride in enumerate(strides):
        pairs = [(h, h + stride) for h in held if h + stride < count and h + stride not in held]
        period, width = (count, 1) if number == 0 else (2, 1) if stride == 1 else (2 * stride, 4)
        rounds.append((pairs, period, width))
        held = sorted(held + [target for _, target in pairs])
    return rounds


def call(kernel, shapes, operands, specs=None, scratch=(), out_specs=None):
    single = not isinstance(shapes, tuple)
    return pl.pallas_call(
        kernel,
        out_shape=shapes,
        in_specs=[VMEM] * len(operands) if specs is None else specs,
        out_specs=out_specs or (VMEM if single else (VMEM,) * len(shapes)),
        scratch_shapes=list(scratch),
        compiler_params=PARAMS,
    )(*operands)


def load_kernel(q_hbm, k_hbm, v_hbm, flags_hbm, q_ref, k_ref, v_ref, sums_ref, ctl_ref, flags_ref, sem):
    copies = [
        pltpu.make_async_copy(source, target, sem.at[i])
        for i, (source, target) in enumerate(
            ((q_hbm, q_ref), (k_hbm, k_ref), (v_hbm, v_ref), (flags_hbm, flags_ref))
        )
    ]
    for copy in copies:
        copy.start()
    lane = lax.broadcasted_iota(jnp.int32, sums_ref.shape, 1)
    copies[0].wait()
    q = q_ref[...].astype(F32)
    q_sum = jnp.sum(q * q, axis=1, keepdims=True)
    copies[1].wait()
    k = k_ref[...].astype(F32)
    k_sum = jnp.sum(k * k, axis=1, keepdims=True)
    sums_ref[...] = jnp.where(lane < LANES // 2, q_sum, k_sum)
    copies[3].wait()
    row = lax.broadcasted_iota(jnp.int32, ctl_ref.shape, 0)
    ctl_ref[...] = jnp.where(row == 1, flags_ref[0, 0], flags_ref[0, 1]).astype(F32)
    copies[2].wait()


def pack_kernel(full_width, frames_ref, flags_ref, q_ref, k_ref, v_ref, qg_ref, kg_ref, mine_ref, other_ref,
                ctl_ref, qn_ref, kn_ref, sink_k_ref, sink_v_ref, near_ref, far_ref):
    rows, cols = q_ref.shape
    factor = lax.rsqrt((mine_ref[...] + other_ref[...]) / full_width + EPSILON)
    qn_ref[...] = (q_ref[...].astype(F32) * factor[:, :1] * qg_ref[...]).astype(BF16)
    kn_ref[...] = (k_ref[...].astype(F32) * factor[:, LANES // 2:LANES // 2 + 1] * kg_ref[...]).astype(BF16)
    sink_k_ref[...] = kn_ref[:FT, :]
    sink_v_ref[...] = v_ref[:FT, :]
    row = lax.broadcasted_iota(jnp.int32, ctl_ref.shape, 0)
    ctl = jnp.where(row == 0, frames_ref[0].astype(F32), flags_ref[...])
    ctl_ref[...] = ctl
    count = ctl[:1, :1]
    counts = jnp.broadcast_to(count, (FT, cols))
    mark = jnp.broadcast_to(count, (FT, LANES)).astype(BF16)
    for ref, at in ((kn_ref, 0), (v_ref, cols)):
        last, before = ref[:FT, :], ref[:FT, :]
        for frame in range(1, rows // FT):
            here = ref[frame * FT:(frame + 1) * FT, :]
            last = jnp.where(counts > frame + 0.5, here, last)
            before = jnp.where(counts > frame + 1.5, here, before)
        near_ref[:FT, at:at + cols] = last
        near_ref[FT:, at:at + cols] = before
        far_ref[:, at:at + cols] = last
    near_ref[:FT, 2 * cols:] = mark
    near_ref[FT:, 2 * cols:] = mark
    far_ref[:, 2 * cols:] = mark


def own_kernel(ctl_ref, q_ref, k_ref, v_ref, acc_ref, top_ref, den_ref):
    rows, cols = q_ref.shape
    slot = lax.broadcasted_iota(jnp.int32, (rows, rows), 1).astype(F32)
    allowed = slot < ctl_ref[:1, :1] * FT
    ones = jnp.ones((rows, HD), BF16)
    for a in range(0, cols, HD):
        b = a + HD
        score = lax.dot_general(
            q_ref[:, a:b], k_ref[:, a:b], (((1,), (1,)), ((), ())), preferred_element_type=F32
        ) * (1.0 / math.sqrt(HD))
        score = jnp.where(allowed, score, -jnp.inf)
        top = jnp.max(score, axis=1, keepdims=True)
        weight = jnp.exp(score - top).astype(BF16)
        both = jnp.dot(weight, jnp.concatenate([v_ref[:, a:b], ones], 1), preferred_element_type=F32)
        acc_ref[:, a:b] = both[:, :HD]
        den_ref[:, a:b] = both[:, HD:]
        top_ref[:, a:b] = jnp.broadcast_to(top, (rows, HD))


def finish_kernel(ctl_ref, q_ref, sink_k_ref, sink_v_ref, near_ref, far_ref, acc_ref, top_ref, den_ref, out_ref):
    rows, cols = q_ref.shape
    span = 3 * FT
    count = ctl_ref[:1, :1]
    sink = ctl_ref[1:2, :1]
    window = ctl_ref[2:3, :1]
    near_mark = near_ref[:1, 2 * cols:2 * cols + 1].astype(F32)
    far_mark = far_ref[:1, 2 * cols:2 * cols + 1].astype(F32)
    has_before = jnp.where(near_mark > 1.5, near_mark, far_mark) * window
    slot = lax.broadcasted_iota(jnp.int32, (rows, span), 1)
    allow = jnp.where(slot < FT, near_mark * window, jnp.where(slot < 2 * FT, has_before, sink))
    allowed = allow > 0.5
    live = lax.broadcasted_iota(jnp.int32, (rows, HD), 0).astype(F32) < count * FT
    pick = jnp.broadcast_to(near_mark, (FT, HD)) > 1.5
    ones = jnp.ones((span, HD), BF16)
    for a in range(0, cols, HD):
        b = a + HD
        before = jnp.where(pick, near_ref[FT:, a:b], far_ref[:, a:b])
        keys = jnp.concatenate([near_ref[:FT, a:b], before, sink_k_ref[:, a:b]], 0)
        before = jnp.where(pick, near_ref[FT:, cols + a:cols + b], far_ref[:, cols + a:cols + b])
        vals = jnp.concatenate([near_ref[:FT, cols + a:cols + b], before, sink_v_ref[:, a:b]], 0)
        score = lax.dot_general(
            q_ref[:, a:b], keys, (((1,), (1,)), ((), ())), preferred_element_type=F32
        ) * (1.0 / math.sqrt(HD))
        score = jnp.where(allowed, score, -jnp.inf)
        old = top_ref[:, a:b]
        top = jnp.maximum(old, jnp.max(score, axis=1, keepdims=True))
        weight = jnp.exp(score - top[:, :span]).astype(BF16)
        both = jnp.dot(weight, jnp.concatenate([vals, ones], 1), preferred_element_type=F32)
        keep = jnp.exp(old - top)
        blended = (acc_ref[:, a:b] * keep + both[:, :HD]) / (den_ref[:, a:b] * keep + both[:, HD:])
        out_ref[:, a:b] = jnp.where(live, blended, 0.0).astype(BF16)


def local(queries, keys, values, q_gain, k_gain, frames, flags):
    rows, cols = queries.shape
    heads = lax.axis_size("head")
    full_width = cols * heads
    count = lax.axis_size("tm")
    here = lax.axis_index("tm")
    shape = jax.ShapeDtypeStruct
    block = shape((rows, cols), BF16)
    wide = shape((rows, cols), F32)
    q_gain, k_gain = q_gain.reshape(1, cols), k_gain.reshape(1, cols)
    in_hbm = lambda x: pltpu.with_memory_space_constraint(x, pltpu.HBM)

    q, k, v, mine, ctl_flags = call(
        load_kernel, (block, block, block, shape((rows, LANES), F32), shape((8, LANES), F32)),
        tuple(in_hbm(x) for x in (queries, keys, values, flags)), specs=[HBM] * 4,
        scratch=[pltpu.SMEM((1, 2), jnp.int32), pltpu.SemaphoreType.DMA((4,))],
    )
    other = lax.ppermute(mine, "head", [(h, (h + 1) % heads) for h in range(heads)])
    ctl, qn, kn, sink_k, sink_v, near, far = call(
        lambda *refs: pack_kernel(full_width, *refs),
        (
            shape((8, LANES), F32), block, block, shape((FT, cols), BF16), shape((FT, cols), BF16),
            shape((2 * FT, 2 * cols + LANES), BF16), shape((FT, 2 * cols + LANES), BF16),
        ),
        (frames, ctl_flags, q, k, v, q_gain, k_gain, mine, other), specs=[SMEM] + [VMEM] * 8,
    )
    near = lax.ppermute(near, "tm", [(i, i + 1) for i in range(count - 1)])
    far = lax.ppermute(far, "tm", [(i, i + 2) for i in range(count - 2)])
    rounds = tree_rounds(count)
    for pairs, period, width in rounds:
        came_k = lax.ppermute(sink_k, "tm", pairs)
        came_v = lax.ppermute(sink_v, "tm", pairs)
        kept = here % period < width
        sink_k = jnp.where(kept, sink_k, came_k)
        sink_v = jnp.where(kept, sink_v, came_v)
    acc, top, den = call(own_kernel, (wide, wide, wide), (ctl, qn, kn, v))
    return call(finish_kernel, block, (ctl, qn, sink_k, sink_v, near, far, acc, top, den))


def solution(mesh):
    placed = (
        P(("groups", "tm"), "head"),
        P(("groups", "tm"), "head"),
        P(("groups", "tm"), "head"),
        P("head"),
        P("head"),
        P(("groups", "tm")),
        P(("groups", "tm"), None),
    )
    return jax.shard_map(
        local, mesh=mesh, in_specs=placed, out_specs=P(("groups", "tm"), "head"), check_vma=False
    )
```

time: 34.7 us -> 32.1 us (0.925)
  the two profiles are of different devices: /device:TPU:12 before, /device:TPU:30 now
where the time goes in v3:
time: 32.1 us; the launch traced here: 31.8 us
  waiting for transfers between devices  15.9 us (50%)
  starting transfers between devices  7.9 us (25%)
  Pallas kernels  7.04 us (22%)
  between operations  0.89 us (3%)
    ppermute x3, waiting for transfers between devices, local(): came_k = lax.ppermute(sink_k, 'tm', pairs)  14.5 us
    pallas_call x4, Pallas kernels, call(): pl.pallas_call(kernel, out_shape=shapes, in_specs=[VMEM] * len(operands)...  7.04 us
    ppermute x3, starting transfers between devices, local(): came_k = lax.ppermute(sink_k, 'tm', pairs)  2.62 us
    ppermute x3, starting transfers between devices, local(): came_v = lax.ppermute(sink_v, 'tm', pairs)  2.62 us
    ppermute x1, starting transfers between devices, local(): far = lax.ppermute(far, 'tm', [(i, i + 2) for i in range(count - 2)])  1.29 us
    ppermute x1, starting transfers between devices, local(): near = lax.ppermute(near, 'tm', [(i, i + 1) for i in range(count - 1)])  1.29 us
    ppermute x3, waiting for transfers between devices, local(): came_v = lax.ppermute(sink_v, 'tm', pairs)  0.87 us
  transfers between devices with their start and end apart: 9, of which 3 were waited for; matrix products, arithmetic and copies ran while one was open for 0% of the time, Pallas kernels for 8%

profile of v3, /device:TPU:30, one launch (start us, length us, event | category | flops | bytes accessed | tf_op | source)
XLA Modules:
  0.0 31.8 jit_solution(10051547206276767589)
XLA Ops:
  0.0 0.0 copy-start
  0.0 1.3 %shard_map.73 = (bf16[96,1280]{1,0:T(8,128)(2,1)S(1)}, bf16[96,1280]{1,0:T(8,128)(2,1)S(1)}, bf16[96,1280]{1,0:T(8,128)(2,1)S(1)}, f32[96,128]{1,0:T(8,128)S(1)}, f32[8,128]{1,0:T(8,128)S(1)}) custom-call(bf16[96,1280]{1,0:T(8,128)(2,1)} %q_hbm.1, bf16[96,1280]{1,0:T(8,128)(2,1)} %k_hbm.1, bf16[96,1280]{1,0:T(8,128)(2,1)} %v_hbm.1, s32[1,2]{1,0:T(1,128)} %flags_hbm.1), custom_call_target="tpu_custom_call" | custom-call | tf_op jit(solution)/shard_map/pallas_call | solution.py:43
  1.3 0.0 copy-start.1
  1.3 0.1 collective-permute-start
  2.0 0.0 copy-done
  2.0 0.0 copy-done.1
  2.1 0.5 %collective-permute-done.refs_8_ = f32[96,128]{1,0:T(8,128)S(1)} collective-permute-done((f32[96,128]{1,0:T(8,128)S(1)}, f32[96,128]{1,0:T(8,128)S(1)}, u32[]{:S(2)}, u32[]{:S(2)}) %collective-permute-start) | collective-permute-done | bytes 49184 | tf_op jit(solution)/shard_map/ppermute | solution.py:174
  2.6 0.2 shard_map.74
  2.8 0.7 %collective-permute-start.1 = (bf16[32,1280]{1,0:T(8,128)(2,1)S(1)}, bf16[32,1280]{1,0:T(8,128)(2,1)S(1)}, u32[]{:S(2)}, u32[]{:S(2)}) collective-permute-start(bf16[32,1280]{1,0:T(8,128)(2,1)S(1)} %get-tuple-element.27), channel_id=1, source_target_pairs={{0,4},{1,5},{16,20},{17,21}} | collective-permute-start | bytes 245768 | tf_op jit(solution)/shard_map/ppermute | solution.py:187
  3.5 0.7 %collective-permute-start.4 = (bf16[32,1280]{1,0:T(8,128)(2,1)S(1)}, bf16[32,1280]{1,0:T(8,128)(2,1)S(1)}, u32[]{:S(2)}, u32[]{:S(2)}) collective-permute-start(bf16[32,1280]{1,0:T(8,128)(2,1)S(1)} %get-tuple-element.28), channel_id=1, source_target_pairs={{0,4},{1,5},{16,20},{17,21}} | collective-permute-start | bytes 245768 | tf_op jit(solution)/shard_map/ppermute | solution.py:188
  4.2 1.3 %collective-permute-start.8 = (bf16[32,2688]{1,0:T(8,128)(2,1)S(1)}, bf16[32,2688]{1,0:T(8,128)(2,1)S(1)}, u32[]{:S(2)}, u32[]{:S(2)}) collective-permute-start(bf16[32,2688]{1,0:T(8,128)(2,1)S(1)} %get-tuple-element.30), channel_id=1, source_target_pairs={{0,4},{2,6},{4,8},{6,10},{8,12},{10,14},{1,5},{3,7},{5,9},{7,11},{... | collective-permute-start | bytes 516104 | tf_op jit(solution)/shard_map/ppermute | solution.py:184
  5.5 1.3 %collective-permute-start.7 = (bf16[64,2688]{1,0:T(8,128)(2,1)S(1)}, bf16[64,2688]{1,0:T(8,128)(2,1)S(1)}, u32[]{:S(2)}, u32[]{:S(2)}) collective-permute-start(bf16[64,2688]{1,0:T(8,128)(2,1)S(1)} %get-tuple-element.29), channel_id=1, source_target_pairs={{0,2},{2,4},{4,6},{6,8},{8,10},{10,12},{12,14},{1,3},{3,5},{5,7},{... | collective-permute-start | bytes 1032200 | tf_op jit(solution)/shard_map/ppermute | solution.py:183
  6.8 2.4 %shard_map.75 = (f32[96,1280]{1,0:T(8,128)S(1)}, f32[96,1280]{1,0:T(8,128)S(1)}, f32[96,1280]{1,0:T(8,128)S(1)}) custom-call(f32[8,128]{1,0:T(8,128)S(1)} %get-tuple-element.25.ctl_ref, bf16[96,1280]{1,0:T(8,128)(2,1)S(1)} %get-tuple-element.26.q_ref, bf16[96,1280]{1,0:T(8,128)(2,1)S(1)} %get-tuple-element.31.k_ref, ...), custom_call_target="tpu_custom_call" | custom-call | tf_op jit(solution)/shard_map/pallas_call | solution.py:43
  9.2 0.0 collective-permute-done.1
  9.2 0.7 %collective-permute-start.2 = (bf16[32,1280]{1,0:T(8,128)(2,1)S(1)}, bf16[32,1280]{1,0:T(8,128)(2,1)S(1)}, u32[]{:S(2)}, u32[]{:S(2)}) collective-permute-start(bf16[32,1280]{1,0:T(8,128)(2,1)S(1)} %broadcast_select_fusion.1), channel_id=1, source_target_pairs={{0,8},{4,12},{1,9},{5,13},{16,24},{20,28},{17,25},{21,29}} | collective-permute-start | bytes 245768 | tf_op jit(solution)/shard_map/ppermute | solution.py:187
  9.9 0.0 collective-permute-done.4
  9.9 0.7 %collective-permute-start.5 = (bf16[32,1280]{1,0:T(8,128)(2,1)S(1)}, bf16[32,1280]{1,0:T(8,128)(2,1)S(1)}, u32[]{:S(2)}, u32[]{:S(2)}) collective-permute-start(bf16[32,1280]{1,0:T(8,128)(2,1)S(1)} %broadcast_select_fusion), channel_id=1, source_target_pairs={{0,8},{4,12},{1,9},{5,13},{16,24},{20,28},{17,25},{21,29}} | collective-permute-start | bytes 245768 | tf_op jit(solution)/shard_map/ppermute | solution.py:188
  10.6 0.0 collective-permute-done.2
  10.6 1.3 %collective-permute-start.3 = (bf16[32,1280]{1,0:T(8,128)(2,1)S(1)}, bf16[32,1280]{1,0:T(8,128)(2,1)S(1)}, u32[]{:S(2)}, u32[]{:S(2)}) collective-permute-start(bf16[32,1280]{1,0:T(8,128)(2,1)S(1)} %broadcast_select_fusion.3), channel_id=1, source_target_pairs={{0,2},{4,6},{8,10},{12,14},{1,3},{5,7},{9,11},{13,15},{16,18},{20,... | collective-permute-start | bytes 245768 | tf_op jit(solution)/shard_map/ppermute | solution.py:187
  11.9 0.0 collective-permute-done.5
  12.0 1.3 %collective-permute-start.6 = (bf16[32,1280]{1,0:T(8,128)(2,1)S(1)}, bf16[32,1280]{1,0:T(8,128)(2,1)S(1)}, u32[]{:S(2)}, u32[]{:S(2)}) collective-permute-start(bf16[32,1280]{1,0:T(8,128)(2,1)S(1)} %broadcast_select_fusion.2), channel_id=1, source_target_pairs={{0,2},{4,6},{8,10},{12,14},{1,3},{5,7},{9,11},{13,15},{16,18},{20,... | collective-permute-start | bytes 245768 | tf_op jit(solution)/shard_map/ppermute | solution.py:188
  13.3 14.5 %collective-permute-done.3 = bf16[32,1280]{1,0:T(8,128)(2,1)S(1)} collective-permute-done((bf16[32,1280]{1,0:T(8,128)(2,1)S(1)}, bf16[32,1280]{1,0:T(8,128)(2,1)S(1)}, u32[]{:S(2)}, u32[]{:S(2)}) %collective-permute-start.3) | collective-permute-done | bytes 81952 | tf_op jit(solution)/shard_map/ppermute | solution.py:187
  27.7 0.9 %collective-permute-done.6 = bf16[32,1280]{1,0:T(8,128)(2,1)S(1)} collective-permute-done((bf16[32,1280]{1,0:T(8,128)(2,1)S(1)}, bf16[32,1280]{1,0:T(8,128)(2,1)S(1)}, u32[]{:S(2)}, u32[]{:S(2)}) %collective-permute-start.6) | collective-permute-done | bytes 81952 | tf_op jit(solution)/shard_map/ppermute | solution.py:188
  28.6 0.0 collective-permute-done.8.far_ref
  28.6 0.0 collective-permute-done.7.near_ref
  28.6 3.2 %shard_map.76 = bf16[96,1280]{1,0:T(8,128)(2,1)} custom-call(f32[8,128]{1,0:T(8,128)S(1)} %get-tuple-element.25.ctl_ref, bf16[96,1280]{1,0:T(8,128)(2,1)S(1)} %get-tuple-element.26.q_ref, bf16[32,1280]{1,0:T(8,128)(2,1)S(1)} %broadcast_select_fusion.5.sink_k_ref, bf16[32,1280]{1,0:T(8,128)(2,1)S(1)} %broadcast_select_fusion.4.sink_v_ref, ...), custom_call_target="tpu_custom_call" | custom-call | tf_op jit(solution)/shard_map/pallas_call | solution.py:43
  (8 shorter events, 0.1 us)
Async XLA Ops:
  0.0 2.0 %copy-start = (f32[1280]{0:T(1024)S(1)}, f32[1280]{0:T(1024)}, u32[]{:S(2)}) copy-start(f32[1280]{0:T(1024)} %param.10) | copy-start | bytes 15364
  1.3 0.8 %copy-start.1 = (f32[1280]{0:T(1024)S(1)}, f32[1280]{0:T(1024)}, u32[]{:S(2)}) copy-start(f32[1280]{0:T(1024)} %param.11) | copy-start | bytes 15364
  1.3 1.3 %collective-permute-start = (f32[96,128]{1,0:T(8,128)S(1)}, f32[96,128]{1,0:T(8,128)S(1)}, u32[]{:S(2)}, u32[]{:S(2)}) collective-permute-start(f32[96,128]{1,0:T(8,128)S(1)} %get-tuple-element.24.refs_7_), channel_id=1, source_target_pairs={{0,1},{1,0},{2,3},{3,2},{4,5},{5,4},{6,7},{7,6},{8,9},{9,8},{10,11... | collective-permute-start | bytes 147464 | tf_op jit(solution)/shard_map/ppermute | solution.py:174
  2.8 6.4 %collective-permute-start.1 = (bf16[32,1280]{1,0:T(8,128)(2,1)S(1)}, bf16[32,1280]{1,0:T(8,128)(2,1)S(1)}, u32[]{:S(2)}, u32[]{:S(2)}) collective-permute-start(bf16[32,1280]{1,0:T(8,128)(2,1)S(1)} %get-tuple-element.27), channel_id=1, source_target_pairs={{0,4},{1,5},{16,20},{17,21}} | collective-permute-start | bytes 245768 | tf_op jit(solution)/shard_map/ppermute | solution.py:187
  3.5 6.4 %collective-permute-start.4 = (bf16[32,1280]{1,0:T(8,128)(2,1)S(1)}, bf16[32,1280]{1,0:T(8,128)(2,1)S(1)}, u32[]{:S(2)}, u32[]{:S(2)}) collective-permute-start(bf16[32,1280]{1,0:T(8,128)(2,1)S(1)} %get-tuple-element.28), channel_id=1, source_target_pairs={{0,4},{1,5},{16,20},{17,21}} | collective-permute-start | bytes 245768 | tf_op jit(solution)/shard_map/ppermute | solution.py:188
  4.2 24.5 %collective-permute-start.8 = (bf16[32,2688]{1,0:T(8,128)(2,1)S(1)}, bf16[32,2688]{1,0:T(8,128)(2,1)S(1)}, u32[]{:S(2)}, u32[]{:S(2)}) collective-permute-start(bf16[32,2688]{1,0:T(8,128)(2,1)S(1)} %get-tuple-element.30), channel_id=1, source_target_pairs={{0,4},{2,6},{4,8},{6,10},{8,12},{10,14},{1,5},{3,7},{5,9},{7,11},{... | collective-permute-start | bytes 516104 | tf_op jit(solution)/shard_map/ppermute | solution.py:184
  5.5 23.2 %collective-permute-start.7 = (bf16[64,2688]{1,0:T(8,128)(2,1)S(1)}, bf16[64,2688]{1,0:T(8,128)(2,1)S(1)}, u32[]{:S(2)}, u32[]{:S(2)}) collective-permute-start(bf16[64,2688]{1,0:T(8,128)(2,1)S(1)} %get-tuple-element.29), channel_id=1, source_target_pairs={{0,2},{2,4},{4,6},{6,8},{8,10},{10,12},{12,14},{1,3},{3,5},{5,7},{... | collective-permute-start | bytes 1032200 | tf_op jit(solution)/shard_map/ppermute | solution.py:183
  9.2 1.4 %collective-permute-start.2 = (bf16[32,1280]{1,0:T(8,128)(2,1)S(1)}, bf16[32,1280]{1,0:T(8,128)(2,1)S(1)}, u32[]{:S(2)}, u32[]{:S(2)}) collective-permute-start(bf16[32,1280]{1,0:T(8,128)(2,1)S(1)} %broadcast_select_fusion.1), channel_id=1, source_target_pairs={{0,8},{4,12},{1,9},{5,13},{16,24},{20,28},{17,25},{21,29}} | collective-permute-start | bytes 245768 | tf_op jit(solution)/shard_map/ppermute | solution.py:187
  9.9 2.0 %collective-permute-start.5 = (bf16[32,1280]{1,0:T(8,128)(2,1)S(1)}, bf16[32,1280]{1,0:T(8,128)(2,1)S(1)}, u32[]{:S(2)}, u32[]{:S(2)}) collective-permute-start(bf16[32,1280]{1,0:T(8,128)(2,1)S(1)} %broadcast_select_fusion), channel_id=1, source_target_pairs={{0,8},{4,12},{1,9},{5,13},{16,24},{20,28},{17,25},{21,29}} | collective-permute-start | bytes 245768 | tf_op jit(solution)/shard_map/ppermute | solution.py:188
  10.6 17.1 %collective-permute-start.3 = (bf16[32,1280]{1,0:T(8,128)(2,1)S(1)}, bf16[32,1280]{1,0:T(8,128)(2,1)S(1)}, u32[]{:S(2)}, u32[]{:S(2)}) collective-permute-start(bf16[32,1280]{1,0:T(8,128)(2,1)S(1)} %broadcast_select_fusion.3), channel_id=1, source_target_pairs={{0,2},{4,6},{8,10},{12,14},{1,3},{5,7},{9,11},{13,15},{16,18},{20,... | collective-permute-start | bytes 245768 | tf_op jit(solution)/shard_map/ppermute | solution.py:187
  12.0 16.7 %collective-permute-start.6 = (bf16[32,1280]{1,0:T(8,128)(2,1)S(1)}, bf16[32,1280]{1,0:T(8,128)(2,1)S(1)}, u32[]{:S(2)}, u32[]{:S(2)}) collective-permute-start(bf16[32,1280]{1,0:T(8,128)(2,1)S(1)} %broadcast_select_fusion.2), channel_id=1, source_target_pairs={{0,2},{4,6},{8,10},{12,14},{1,3},{5,7},{9,11},{13,15},{16,18},{20,... | collective-permute-start | bytes 245768 | tf_op jit(solution)/shard_map/ppermute | solution.py:188

commit v4 on v3

--- a/solution.py
+++ b/solution.py
@@ -21,20 +21,15 @@
 
 
 def tree_rounds(count):
-    top = 1
-    while top * 2 < count:
-        top *= 2
-    strides = [2] if count > 2 else []
-    while top >= 4:
-        strides.append(top)
-        top //= 2
-    strides.append(1)
+    stride = 1
+    while stride * 2 < count:
+        stride *= 2
     held, rounds = [0], []
-    for number, stride in enumerate(strides):
-        pairs = [(h, h + stride) for h in held if h + stride < count and h + stride not in held]
-        period, width = (count, 1) if number == 0 else (2, 1) if stride == 1 else (2 * stride, 4)
-        rounds.append((pairs, period, width))
+    while stride:
+        pairs = [(h, h + stride) for h in held if h + stride < count]
+        rounds.append((pairs, 2 * stride))
         held = sorted(held + [target for _, target in pairs])
+        stride //= 2
     return rounds
 
 
@@ -101,28 +96,33 @@
     far_ref[:, 2 * cols:] = mark
 
 
-def own_kernel(ctl_ref, q_ref, k_ref, v_ref, acc_ref, top_ref, den_ref):
+def own_kernel(ctl_ref, q_ref, k_ref, v_ref, acc_ref, top_ref, den_ref, score_ref, weight_ref):
     rows, cols = q_ref.shape
+    heads = [(i, i * HD, (i + 1) * HD) for i in range(cols // HD)]
     slot = lax.broadcasted_iota(jnp.int32, (rows, rows), 1).astype(F32)
     allowed = slot < ctl_ref[:1, :1] * FT
     ones = jnp.ones((rows, HD), BF16)
-    for a in range(0, cols, HD):
-        b = a + HD
+    for i, a, b in heads:
         score = lax.dot_general(
             q_ref[:, a:b], k_ref[:, a:b], (((1,), (1,)), ((), ())), preferred_element_type=F32
         ) * (1.0 / math.sqrt(HD))
-        score = jnp.where(allowed, score, -jnp.inf)
+        score_ref[i] = jnp.where(allowed, score, -jnp.inf)
+    for i, a, b in heads:
+        score = score_ref[i]
         top = jnp.max(score, axis=1, keepdims=True)
-        weight = jnp.exp(score - top).astype(BF16)
-        both = jnp.dot(weight, jnp.concatenate([v_ref[:, a:b], ones], 1), preferred_element_type=F32)
+        top_ref[:, a:b] = jnp.broadcast_to(top, (rows, HD))
+        weight_ref[i] = jnp.exp(score - top).astype(BF16)
+    for i, a, b in heads:
+        both = jnp.dot(weight_ref[i], jnp.concatenate([v_ref[:, a:b], ones], 1), preferred_element_type=F32)
         acc_ref[:, a:b] = both[:, :HD]
         den_ref[:, a:b] = both[:, HD:]
-        top_ref[:, a:b] = jnp.broadcast_to(top, (rows, HD))
-
-
-def finish_kernel(ctl_ref, q_ref, sink_k_ref, sink_v_ref, near_ref, far_ref, acc_ref, top_ref, den_ref, out_ref):
+
+
+def finish_kernel(ctl_ref, q_ref, sink_k_ref, sink_v_ref, near_ref, far_ref, acc_ref, top_ref, den_ref, out_ref,
+                  score_ref, weight_ref, keep_ref):
     rows, cols = q_ref.shape
     span = 3 * FT
+    heads = [(i, i * HD, (i + 1) * HD) for i in range(cols // HD)]
     count = ctl_ref[:1, :1]
     sink = ctl_ref[1:2, :1]
     window = ctl_ref[2:3, :1]
@@ -135,21 +135,24 @@
     live = lax.broadcasted_iota(jnp.int32, (rows, HD), 0).astype(F32) < count * FT
     pick = jnp.broadcast_to(near_mark, (FT, HD)) > 1.5
     ones = jnp.ones((span, HD), BF16)
-    for a in range(0, cols, HD):
-        b = a + HD
+    for i, a, b in heads:
         before = jnp.where(pick, near_ref[FT:, a:b], far_ref[:, a:b])
         keys = jnp.concatenate([near_ref[:FT, a:b], before, sink_k_ref[:, a:b]], 0)
-        before = jnp.where(pick, near_ref[FT:, cols + a:cols + b], far_ref[:, cols + a:cols + b])
-        vals = jnp.concatenate([near_ref[:FT, cols + a:cols + b], before, sink_v_ref[:, a:b]], 0)
         score = lax.dot_general(
             q_ref[:, a:b], keys, (((1,), (1,)), ((), ())), preferred_element_type=F32
         ) * (1.0 / math.sqrt(HD))
-        score = jnp.where(allowed, score, -jnp.inf)
+        score_ref[i] = jnp.where(allowed, score, -jnp.inf)
+    for i, a, b in heads:
+        score = score_ref[i]
         old = top_ref[:, a:b]
         top = jnp.maximum(old, jnp.max(score, axis=1, keepdims=True))
-        weight = jnp.exp(score - top[:, :span]).astype(BF16)
-        both = jnp.dot(weight, jnp.concatenate([vals, ones], 1), preferred_element_type=F32)
-        keep = jnp.exp(old - top)
+        keep_ref[i] = jnp.exp(old - top)
+        weight_ref[i] = jnp.exp(score - top[:, :span]).astype(BF16)
+    for i, a, b in heads:
+        before = jnp.where(pick, near_ref[FT:, cols + a:cols + b], far_ref[:, cols + a:cols + b])
+        vals = jnp.concatenate([near_ref[:FT, cols + a:cols + b], before, sink_v_ref[:, a:b]], 0)
+        both = jnp.dot(weight_ref[i], jnp.concatenate([vals, ones], 1), preferred_element_type=F32)
+        keep = keep_ref[i]
         blended = (acc_ref[:, a:b] * keep + both[:, :HD]) / (den_ref[:, a:b] * keep + both[:, HD:])
         out_ref[:, a:b] = jnp.where(live, blended, 0.0).astype(BF16)
 
@@ -183,14 +186,23 @@
     near = lax.ppermute(near, "tm", [(i, i + 1) for i in range(count - 1)])
     far = lax.ppermute(far, "tm", [(i, i + 2) for i in range(count - 2)])
     rounds = tree_rounds(count)
-    for pairs, period, width in rounds:
+    for pairs, period in rounds:
         came_k = lax.ppermute(sink_k, "tm", pairs)
         came_v = lax.ppermute(sink_v, "tm", pairs)
-        kept = here % period < width
+        kept = here % period == 0
         sink_k = jnp.where(kept, sink_k, came_k)
         sink_v = jnp.where(kept, sink_v, came_v)
-    acc, top, den = call(own_kernel, (wide, wide, wide), (ctl, qn, kn, v))
-    return call(finish_kernel, block, (ctl, qn, sink_k, sink_v, near, far, acc, top, den))
+    acc, top, den = call(
+        own_kernel, (wide, wide, wide), (ctl, qn, kn, v),
+        scratch=[pltpu.VMEM((cols // HD, rows, rows), F32), pltpu.VMEM((cols // HD, rows, rows), BF16)],
+    )
+    return call(
+        finish_kernel, block, (ctl, qn, sink_k, sink_v, near, far, acc, top, den),
+        scratch=[
+            pltpu.VMEM((cols // HD, rows, 3 * FT), F32), pltpu.VMEM((cols // HD, rows, 3 * FT), BF16),
+            pltpu.VMEM((cols // HD, rows, HD), F32),
+        ],
+    )
 
 
 def solution(mesh):

time: 32.1 us -> 26.1 us (0.81)
  the two profiles are of different devices: /device:TPU:30 before, /device:TPU:10 now
where the time goes in v4:
time: 26.1 us; the launch traced here: 25.8 us
  starting transfers between devices  12.3 us (47%)
  waiting for transfers between devices  9.2 us (35%)
  Pallas kernels  3.39 us (13%)
  between operations  0.89 us (3%)
    ppermute x3, waiting for transfers between devices, local(): came_k = lax.ppermute(sink_k, 'tm', pairs)  7.68 us
    ppermute x1, starting transfers between devices, local(): far = lax.ppermute(far, 'tm', [(i, i + 2) for i in range(count - 2)])  3.48 us
    ppermute x1, starting transfers between devices, local(): near = lax.ppermute(near, 'tm', [(i, i + 1) for i in range(count - 1)])  3.46 us
    pallas_call x4, Pallas kernels, call(): pl.pallas_call(kernel, out_shape=shapes, in_specs=[VMEM] * len(operands)...  3.39 us
    ppermute x3, starting transfers between devices, local(): came_k = lax.ppermute(sink_k, 'tm', pairs)  2.62 us
    ppermute x3, starting transfers between devices, local(): came_v = lax.ppermute(sink_v, 'tm', pairs)  2.62 us
    ppermute x3, waiting for transfers between devices, local(): came_v = lax.ppermute(sink_v, 'tm', pairs)  0.99 us
    ppermute x1, waiting for transfers between devices, local(): lax.ppermute(mine, 'head', [(h, (h + 1) % heads) for h in range(heads)])  0.52 us
  transfers between devices with their start and end apart: 9, of which 3 were waited for; matrix products, arithmetic and copies ran while one was open for 0% of the time, Pallas kernels for 2%

profile of v4, /device:TPU:10, one launch (start us, length us, event | category | flops | bytes accessed | tf_op | source)
XLA Modules:
  0.0 25.8 jit_solution(13601135576351687456)
XLA Ops:
  0.0 0.0 copy-start
  0.0 1.3 %shard_map.73 = (bf16[96,1280]{1,0:T(8,128)(2,1)S(1)}, bf16[96,1280]{1,0:T(8,128)(2,1)S(1)}, bf16[96,1280]{1,0:T(8,128)(2,1)S(1)}, f32[96,128]{1,0:T(8,128)S(1)}, f32[8,128]{1,0:T(8,128)S(1)}) custom-call(bf16[96,1280]{1,0:T(8,128)(2,1)} %q_hbm.1, bf16[96,1280]{1,0:T(8,128)(2,1)} %k_hbm.1, bf16[96,1280]{1,0:T(8,128)(2,1)} %v_hbm.1, s32[1,2]{1,0:T(1,128)} %flags_hbm.1), custom_call_target="tpu_custom_call" | custom-call | tf_op jit(solution)/shard_map/pallas_call | solution.py:38
  1.3 0.0 copy-start.1
  1.3 0.1 collective-permute-start
  2.0 0.0 copy-done
  2.0 0.0 copy-done.1
  2.1 0.5 %collective-permute-done.refs_8_ = f32[96,128]{1,0:T(8,128)S(1)} collective-permute-done((f32[96,128]{1,0:T(8,128)S(1)}, f32[96,128]{1,0:T(8,128)S(1)}, u32[]{:S(2)}, u32[]{:S(2)}) %collective-permute-start) | collective-permute-done | bytes 49184 | tf_op jit(solution)/shard_map/ppermute | solution.py:177
  2.6 0.2 shard_map.74
  2.8 0.7 %collective-permute-start.1 = (bf16[32,1280]{1,0:T(8,128)(2,1)S(1)}, bf16[32,1280]{1,0:T(8,128)(2,1)S(1)}, u32[]{:S(2)}, u32[]{:S(2)}) collective-permute-start(bf16[32,1280]{1,0:T(8,128)(2,1)S(1)} %get-tuple-element.27), channel_id=1, source_target_pairs={{0,8},{1,9},{16,24},{17,25}} | collective-permute-start | bytes 245768 | tf_op jit(solution)/shard_map/ppermute | solution.py:190
  3.5 0.7 %collective-permute-start.4 = (bf16[32,1280]{1,0:T(8,128)(2,1)S(1)}, bf16[32,1280]{1,0:T(8,128)(2,1)S(1)}, u32[]{:S(2)}, u32[]{:S(2)}) collective-permute-start(bf16[32,1280]{1,0:T(8,128)(2,1)S(1)} %get-tuple-element.28), channel_id=1, source_target_pairs={{0,8},{1,9},{16,24},{17,25}} | collective-permute-start | bytes 245768 | tf_op jit(solution)/shard_map/ppermute | solution.py:191
  4.2 3.5 %collective-permute-start.8 = (bf16[32,2688]{1,0:T(8,128)(2,1)S(1)}, bf16[32,2688]{1,0:T(8,128)(2,1)S(1)}, u32[]{:S(2)}, u32[]{:S(2)}) collective-permute-start(bf16[32,2688]{1,0:T(8,128)(2,1)S(1)} %get-tuple-element.30), channel_id=1, source_target_pairs={{0,4},{2,6},{4,8},{6,10},{8,12},{10,14},{1,5},{3,7},{5,9},{7,11},{... | collective-permute-start | bytes 516104 | tf_op jit(solution)/shard_map/ppermute | solution.py:187
  7.7 3.5 %collective-permute-start.7 = (bf16[64,2688]{1,0:T(8,128)(2,1)S(1)}, bf16[64,2688]{1,0:T(8,128)(2,1)S(1)}, u32[]{:S(2)}, u32[]{:S(2)}) collective-permute-start(bf16[64,2688]{1,0:T(8,128)(2,1)S(1)} %get-tuple-element.29), channel_id=1, source_target_pairs={{0,2},{2,4},{4,6},{6,8},{8,10},{10,12},{12,14},{1,3},{3,5},{5,7},{... | collective-permute-start | bytes 1032200 | tf_op jit(solution)/shard_map/ppermute | solution.py:186
  11.1 0.6 %shard_map.75 = (f32[96,1280]{1,0:T(8,128)S(1)}, f32[96,1280]{1,0:T(8,128)S(1)}, f32[96,1280]{1,0:T(8,128)S(1)}) custom-call(f32[8,128]{1,0:T(8,128)S(1)} %get-tuple-element.25.ctl_ref, bf16[96,1280]{1,0:T(8,128)(2,1)S(1)} %get-tuple-element.26.q_ref, bf16[96,1280]{1,0:T(8,128)(2,1)S(1)} %get-tuple-element.31.k_ref, ...), custom_call_target="tpu_custom_call" | custom-call | tf_op jit(solution)/shard_map/pallas_call | solution.py:38
  11.7 0.0 collective-permute-done.1
  11.7 0.7 %collective-permute-start.2 = (bf16[32,1280]{1,0:T(8,128)(2,1)S(1)}, bf16[32,1280]{1,0:T(8,128)(2,1)S(1)}, u32[]{:S(2)}, u32[]{:S(2)}) collective-permute-start(bf16[32,1280]{1,0:T(8,128)(2,1)S(1)} %broadcast_select_fusion.1), channel_id=1, source_target_pairs={{0,4},{8,12},{1,5},{9,13},{16,20},{24,28},{17,21},{25,29}} | collective-permute-start | bytes 245768 | tf_op jit(solution)/shard_map/ppermute | solution.py:190
  12.4 0.0 collective-permute-done.4
  12.4 0.7 %collective-permute-start.5 = (bf16[32,1280]{1,0:T(8,128)(2,1)S(1)}, bf16[32,1280]{1,0:T(8,128)(2,1)S(1)}, u32[]{:S(2)}, u32[]{:S(2)}) collective-permute-start(bf16[32,1280]{1,0:T(8,128)(2,1)S(1)} %broadcast_select_fusion), channel_id=1, source_target_pairs={{0,4},{8,12},{1,5},{9,13},{16,20},{24,28},{17,21},{25,29}} | collective-permute-start | bytes 245768 | tf_op jit(solution)/shard_map/ppermute | solution.py:191
  13.1 0.0 collective-permute-done.2
  13.1 1.3 %collective-permute-start.3 = (bf16[32,1280]{1,0:T(8,128)(2,1)S(1)}, bf16[32,1280]{1,0:T(8,128)(2,1)S(1)}, u32[]{:S(2)}, u32[]{:S(2)}) collective-permute-start(bf16[32,1280]{1,0:T(8,128)(2,1)S(1)} %broadcast_select_fusion.3), channel_id=1, source_target_pairs={{0,2},{4,6},{8,10},{12,14},{1,3},{5,7},{9,11},{13,15},{16,18},{20,... | collective-permute-start | bytes 245768 | tf_op jit(solution)/shard_map/ppermute | solution.py:190
  14.4 0.0 collective-permute-done.5
  14.5 1.3 %collective-permute-start.6 = (bf16[32,1280]{1,0:T(8,128)(2,1)S(1)}, bf16[32,1280]{1,0:T(8,128)(2,1)S(1)}, u32[]{:S(2)}, u32[]{:S(2)}) collective-permute-start(bf16[32,1280]{1,0:T(8,128)(2,1)S(1)} %broadcast_select_fusion.2), channel_id=1, source_target_pairs={{0,2},{4,6},{8,10},{12,14},{1,3},{5,7},{9,11},{13,15},{16,18},{20,... | collective-permute-start | bytes 245768 | tf_op jit(solution)/shard_map/ppermute | solution.py:191
  15.8 7.7 %collective-permute-done.3 = bf16[32,1280]{1,0:T(8,128)(2,1)S(1)} collective-permute-done((bf16[32,1280]{1,0:T(8,128)(2,1)S(1)}, bf16[32,1280]{1,0:T(8,128)(2,1)S(1)}, u32[]{:S(2)}, u32[]{:S(2)}) %collective-permute-start.3) | collective-permute-done | bytes 81952 | tf_op jit(solution)/shard_map/ppermute | solution.py:190
  23.5 1.0 %collective-permute-done.6 = bf16[32,1280]{1,0:T(8,128)(2,1)S(1)} collective-permute-done((bf16[32,1280]{1,0:T(8,128)(2,1)S(1)}, bf16[32,1280]{1,0:T(8,128)(2,1)S(1)}, u32[]{:S(2)}, u32[]{:S(2)}) %collective-permute-start.6) | collective-permute-done | bytes 81952 | tf_op jit(solution)/shard_map/ppermute | solution.py:191
  24.5 0.0 collective-permute-done.8.far_ref
  24.5 0.0 collective-permute-done.7.near_ref
  24.5 1.3 %shard_map.76 = bf16[96,1280]{1,0:T(8,128)(2,1)} custom-call(f32[8,128]{1,0:T(8,128)S(1)} %get-tuple-element.25.ctl_ref, bf16[96,1280]{1,0:T(8,128)(2,1)S(1)} %get-tuple-element.26.q_ref, bf16[32,1280]{1,0:T(8,128)(2,1)S(1)} %broadcast_select_fusion.5.sink_k_ref, bf16[32,1280]{1,0:T(8,128)(2,1)S(1)} %broadcast_select_fusion.4.sink_v_ref, ...), custom_call_target="tpu_custom_call" | custom-call | tf_op jit(solution)/shard_map/pallas_call | solution.py:38
  (8 shorter events, 0.1 us)
Async XLA Ops:
  0.0 2.0 %copy-start = (f32[1280]{0:T(1024)S(1)}, f32[1280]{0:T(1024)}, u32[]{:S(2)}) copy-start(f32[1280]{0:T(1024)} %param.10) | copy-start | bytes 15364
  1.3 0.8 %copy-start.1 = (f32[1280]{0:T(1024)S(1)}, f32[1280]{0:T(1024)}, u32[]{:S(2)}) copy-start(f32[1280]{0:T(1024)} %param.11) | copy-start | bytes 15364
  1.3 1.3 %collective-permute-start = (f32[96,128]{1,0:T(8,128)S(1)}, f32[96,128]{1,0:T(8,128)S(1)}, u32[]{:S(2)}, u32[]{:S(2)}) collective-permute-start(f32[96,128]{1,0:T(8,128)S(1)} %get-tuple-element.24.refs_7_), channel_id=1, source_target_pairs={{0,1},{1,0},{2,3},{3,2},{4,5},{5,4},{6,7},{7,6},{8,9},{9,8},{10,11... | collective-permute-start | bytes 147464 | tf_op jit(solution)/shard_map/ppermute | solution.py:177
  2.8 8.9 %collective-permute-start.1 = (bf16[32,1280]{1,0:T(8,128)(2,1)S(1)}, bf16[32,1280]{1,0:T(8,128)(2,1)S(1)}, u32[]{:S(2)}, u32[]{:S(2)}) collective-permute-start(bf16[32,1280]{1,0:T(8,128)(2,1)S(1)} %get-tuple-element.27), channel_id=1, source_target_pairs={{0,8},{1,9},{16,24},{17,25}} | collective-permute-start | bytes 245768 | tf_op jit(solution)/shard_map/ppermute | solution.py:190
  3.5 8.9 %collective-permute-start.4 = (bf16[32,1280]{1,0:T(8,128)(2,1)S(1)}, bf16[32,1280]{1,0:T(8,128)(2,1)S(1)}, u32[]{:S(2)}, u32[]{:S(2)}) collective-permute-start(bf16[32,1280]{1,0:T(8,128)(2,1)S(1)} %get-tuple-element.28), channel_id=1, source_target_pairs={{0,8},{1,9},{16,24},{17,25}} | collective-permute-start | bytes 245768 | tf_op jit(solution)/shard_map/ppermute | solution.py:191
  4.2 20.3 %collective-permute-start.8 = (bf16[32,2688]{1,0:T(8,128)(2,1)S(1)}, bf16[32,2688]{1,0:T(8,128)(2,1)S(1)}, u32[]{:S(2)}, u32[]{:S(2)}) collective-permute-start(bf16[32,2688]{1,0:T(8,128)(2,1)S(1)} %get-tuple-element.30), channel_id=1, source_target_pairs={{0,4},{2,6},{4,8},{6,10},{8,12},{10,14},{1,5},{3,7},{5,9},{7,11},{... | collective-permute-start | bytes 516104 | tf_op jit(solution)/shard_map/ppermute | solution.py:187
  7.7 16.8 %collective-permute-start.7 = (bf16[64,2688]{1,0:T(8,128)(2,1)S(1)}, bf16[64,2688]{1,0:T(8,128)(2,1)S(1)}, u32[]{:S(2)}, u32[]{:S(2)}) collective-permute-start(bf16[64,2688]{1,0:T(8,128)(2,1)S(1)} %get-tuple-element.29), channel_id=1, source_target_pairs={{0,2},{2,4},{4,6},{6,8},{8,10},{10,12},{12,14},{1,3},{3,5},{5,7},{... | collective-permute-start | bytes 1032200 | tf_op jit(solution)/shard_map/ppermute | solution.py:186
  11.7 1.4 %collective-permute-start.2 = (bf16[32,1280]{1,0:T(8,128)(2,1)S(1)}, bf16[32,1280]{1,0:T(8,128)(2,1)S(1)}, u32[]{:S(2)}, u32[]{:S(2)}) collective-permute-start(bf16[32,1280]{1,0:T(8,128)(2,1)S(1)} %broadcast_select_fusion.1), channel_id=1, source_target_pairs={{0,4},{8,12},{1,5},{9,13},{16,20},{24,28},{17,21},{25,29}} | collective-permute-start | bytes 245768 | tf_op jit(solution)/shard_map/ppermute | solution.py:190
  12.4 2.0 %collective-permute-start.5 = (bf16[32,1280]{1,0:T(8,128)(2,1)S(1)}, bf16[32,1280]{1,0:T(8,128)(2,1)S(1)}, u32[]{:S(2)}, u32[]{:S(2)}) collective-permute-start(bf16[32,1280]{1,0:T(8,128)(2,1)S(1)} %broadcast_select_fusion), channel_id=1, source_target_pairs={{0,4},{8,12},{1,5},{9,13},{16,20},{24,28},{17,21},{25,29}} | collective-permute-start | bytes 245768 | tf_op jit(solution)/shard_map/ppermute | solution.py:191
  13.1 10.3 %collective-permute-start.3 = (bf16[32,1280]{1,0:T(8,128)(2,1)S(1)}, bf16[32,1280]{1,0:T(8,128)(2,1)S(1)}, u32[]{:S(2)}, u32[]{:S(2)}) collective-permute-start(bf16[32,1280]{1,0:T(8,128)(2,1)S(1)} %broadcast_select_fusion.3), channel_id=1, source_target_pairs={{0,2},{4,6},{8,10},{12,14},{1,3},{5,7},{9,11},{13,15},{16,18},{20,... | collective-permute-start | bytes 245768 | tf_op jit(solution)/shard_map/ppermute | solution.py:190
  14.5 10.0 %collective-permute-start.6 = (bf16[32,1280]{1,0:T(8,128)(2,1)S(1)}, bf16[32,1280]{1,0:T(8,128)(2,1)S(1)}, u32[]{:S(2)}, u32[]{:S(2)}) collective-permute-start(bf16[32,1280]{1,0:T(8,128)(2,1)S(1)} %broadcast_select_fusion.2), channel_id=1, source_target_pairs={{0,2},{4,6},{8,10},{12,14},{1,3},{5,7},{9,11},{13,15},{16,18},{20,... | collective-permute-start | bytes 245768 | tf_op jit(solution)/shard_map/ppermute | solution.py:191

commit v5 on v4

v5 whole, which is shorter than its diff:
```python
import math

import jax
import jax.numpy as jnp
from jax import lax
from jax.experimental import pallas as pl
from jax.experimental.pallas import tpu as pltpu
from jax.sharding import PartitionSpec as P


HD = 128
FT = 32
EPSILON = 1e-06
LANES = 128
VMEM = pl.BlockSpec(memory_space=pltpu.VMEM)
HBM = pl.BlockSpec(memory_space=pltpu.HBM)
SMEM = pl.BlockSpec(memory_space=pltpu.SMEM)
PARAMS = pltpu.CompilerParams(vmem_limit_bytes=8 << 20)
F32 = jnp.float32
BF16 = jnp.bfloat16


def tree_rounds(count):
    stride = 1
    while stride * 2 < count:
        stride *= 2
    held, rounds = [0], []
    while stride:
        pairs = [(h, h + stride) for h in held if h + stride < count]
        rounds.append((pairs, 2 * stride))
        held = sorted(held + [target for _, target in pairs])
        stride //= 2
    return rounds


def call(kernel, shapes, operands, specs=None, scratch=(), out_specs=None):
    single = not isinstance(shapes, tuple)
    return pl.pallas_call(
        kernel,
        out_shape=shapes,
        in_specs=[VMEM] * len(operands) if specs is None else specs,
        out_specs=out_specs or (VMEM if single else (VMEM,) * len(shapes)),
        scratch_shapes=list(scratch),
        compiler_params=PARAMS,
    )(*operands)


def lead_kernel(k_hbm, v_hbm, sink_k_ref, sink_v_ref, sink_ref, sem):
    cols = k_hbm.shape[1]

    @pl.when(lax.axis_index("tm") == 0)
    def _():
        first = pltpu.make_async_copy(k_hbm.at[:FT, :], sink_k_ref, sem.at[0])
        second = pltpu.make_async_copy(v_hbm.at[:FT, :], sink_v_ref, sem.at[1])
        first.start()
        second.start()
        first.wait()
        second.wait()
        sink_ref[:, :cols] = sink_k_ref[...]
        sink_ref[:, cols:] = sink_v_ref[...]


def pack_kernel(frames_ref, k_ref, v_ref, near_ref, far_ref):
    rows, cols = k_ref.shape
    count = jnp.full((1, 1), frames_ref[0].astype(F32))
    counts = jnp.broadcast_to(count, (FT, cols))
    mark = jnp.broadcast_to(count, (FT, LANES)).astype(BF16)
    for ref, at in ((k_ref, 0), (v_ref, cols)):
        last, before = ref[:FT, :], ref[:FT, :]
        for frame in range(1, rows // FT):
            here = ref[frame * FT:(frame + 1) * FT, :]
            last = jnp.where(counts > frame + 0.5, here, last)
            before = jnp.where(counts > frame + 1.5, here, before)
        near_ref[:FT, at:at + cols] = last
        near_ref[FT:, at:at + cols] = before
        far_ref[:, at:at + cols] = last
    near_ref[:FT, 2 * cols:] = mark
    near_ref[FT:, 2 * cols:] = mark
    far_ref[:, 2 * cols:] = mark


def square_sums(ref):
    x = ref[...].astype(F32)
    return jnp.sum(x * x, axis=1, keepdims=True)


def sums_kernel(q_ref, k_ref, sums_ref):
    lane = lax.broadcasted_iota(jnp.int32, sums_ref.shape, 1)
    sums_ref[...] = jnp.where(lane < LANES // 2, square_sums(q_ref), square_sums(k_ref))


def own_kernel(full_width, frames_ref, flags_ref, q_ref, k_ref, v_ref, qg_ref, kg_ref, mine_ref, other_ref,
               ctl_ref, qn_ref, acc_ref, top_ref, den_ref, kn_ref, score_ref, weight_ref):
    rows, cols = q_ref.shape
    flags = flags_ref[...].astype(F32)
    row = lax.broadcasted_iota(jnp.int32, ctl_ref.shape, 0)
    ctl_ref[...] = jnp.where(row == 0, flags[:, :1], flags[:, 1:2])
    factor = lax.rsqrt((mine_ref[...] + other_ref[...]) / full_width + EPSILON)
    qn_ref[...] = (q_ref[...].astype(F32) * factor[:, :1] * qg_ref[...]).astype(BF16)
    kn_ref[...] = (k_ref[...].astype(F32) * factor[:, LANES // 2:LANES // 2 + 1] * kg_ref[...]).astype(BF16)
    heads = [(i, i * HD, (i + 1) * HD) for i in range(cols // HD)]
    allowed = lax.broadcasted_iota(jnp.int32, (rows, rows), 1) < frames_ref[0] * FT
    ones = jnp.ones((rows, HD), BF16)
    for i, a, b in heads:
        score = lax.dot_general(
            qn_ref[:, a:b], kn_ref[:, a:b], (((1,), (1,)), ((), ())), preferred_element_type=F32
        ) * (1.0 / math.sqrt(HD))
        score_ref[i] = jnp.where(allowed, score, -jnp.inf)
    for i, a, b in heads:
        score = score_ref[i]
        top = jnp.max(score, axis=1, keepdims=True)
        top_ref[:, a:b] = jnp.broadcast_to(top, (rows, HD))
        weight_ref[i] = jnp.exp(score - top).astype(BF16)
    for i, a, b in heads:
        both = jnp.dot(weight_ref[i], jnp.concatenate([v_ref[:, a:b], ones], 1), preferred_element_type=F32)
        acc_ref[:, a:b] = both[:, :HD]
        den_ref[:, a:b] = both[:, HD:]


def gather_kernel(near_ref, far_ref, sink_k_ref, next_ref, keys_ref, sums_ref):
    cols = sink_k_ref.shape[1]
    pick = jnp.broadcast_to(near_ref[:1, 2 * cols:2 * cols + 1].astype(F32), (FT, cols)) > 1.5
    second = jnp.full((FT, cols), lax.axis_index("tm"), jnp.int32) == 1
    keys_ref[:FT, :] = near_ref[:FT, :cols]
    keys_ref[FT:2 * FT, :] = jnp.where(pick, near_ref[FT:, :cols], far_ref[:, :cols])
    keys_ref[2 * FT:, :] = jnp.where(second, next_ref[:, :cols], sink_k_ref[...])
    sums_ref[...] = jnp.broadcast_to(square_sums(keys_ref), sums_ref.shape)


def finish_kernel(full_width, frames_ref, ctl_ref, q_ref, raw_ref, kg_ref, mine_ref, other_ref, sink_v_ref, next_ref,
                  near_ref, far_ref, acc_ref, top_ref, den_ref, out_ref, keys_ref, score_ref, weight_ref, keep_ref):
    rows, cols = q_ref.shape
    span = 3 * FT
    factor = lax.rsqrt((mine_ref[:, :1] + other_ref[:, :1]) / full_width + EPSILON)
    keys_ref[...] = (raw_ref[...].astype(F32) * factor * kg_ref[...]).astype(BF16)
    heads = [(i, i * HD, (i + 1) * HD) for i in range(cols // HD)]
    sink = ctl_ref[:1, :1]
    window = ctl_ref[1:2, :1]
    near_mark = near_ref[:1, 2 * cols:2 * cols + 1].astype(F32)
    far_mark = far_ref[:1, 2 * cols:2 * cols + 1].astype(F32)
    has_before = jnp.where(near_mark > 1.5, near_mark, far_mark) * window
    slot = lax.broadcasted_iota(jnp.int32, (rows, span), 1)
    allow = jnp.where(slot < FT, near_mark * window, jnp.where(slot < 2 * FT, has_before, sink))
    allowed = allow > 0.5
    live = lax.broadcasted_iota(jnp.int32, (rows, HD), 0) < frames_ref[0] * FT
    pick = jnp.broadcast_to(near_mark, (FT, HD)) > 1.5
    second = jnp.full((FT, HD), lax.axis_index("tm"), jnp.int32) == 1
    ones = jnp.ones((span, HD), BF16)
    for i, a, b in heads:
        score = lax.dot_general(
            q_ref[:, a:b], keys_ref[:, a:b], (((1,), (1,)), ((), ())), preferred_element_type=F32
        ) * (1.0 / math.sqrt(HD))
        score_ref[i] = jnp.where(allowed, score, -jnp.inf)
    for i, a, b in heads:
        score = score_ref[i]
        old = top_ref[:, a:b]
        top = jnp.maximum(old, jnp.max(score, axis=1, keepdims=True))
        keep_ref[i] = jnp.exp(old - top)
        weight_ref[i] = jnp.exp(score - top[:, :span]).astype(BF16)
    for i, a, b in heads:
        c, d = cols + a, cols + b
        before = jnp.where(pick, near_ref[FT:, c:d], far_ref[:, c:d])
        first = jnp.where(second, next_ref[:, c:d], sink_v_ref[:, a:b])
        vals = jnp.concatenate([near_ref[:FT, c:d], before, first], 0)
        both = jnp.dot(weight_ref[i], jnp.concatenate([vals, ones], 1), preferred_element_type=F32)
        keep = keep_ref[i]
        blended = (acc_ref[:, a:b] * keep + both[:, :HD]) / (den_ref[:, a:b] * keep + both[:, HD:])
        out_ref[:, a:b] = jnp.where(live, blended, 0.0).astype(BF16)


def local(queries, keys, values, q_gain, k_gain, frames, flags):
    rows, cols = queries.shape
    heads = lax.axis_size("head")
    full_width = cols * heads
    count = lax.axis_size("tm")
    here = lax.axis_index("tm")
    shape = jax.ShapeDtypeStruct
    block = shape((rows, cols), BF16)
    wide = shape((rows, cols), F32)
    frame = shape((FT, cols), BF16)
    q_gain, k_gain = q_gain.reshape(1, cols), k_gain.reshape(1, cols)
    swap = [(h, (h + 1) % heads) for h in range(heads)]
    in_hbm = lambda x: pltpu.with_memory_space_constraint(x, pltpu.HBM)
    scores = lambda n: [pltpu.VMEM((cols // HD, rows, n), F32), pltpu.VMEM((cols // HD, rows, n), BF16)]

    sink_k, sink_v, both = call(
        lead_kernel, (frame, frame, shape((FT, 2 * cols), BF16)), (in_hbm(keys), in_hbm(values)),
        specs=[HBM, HBM], scratch=[pltpu.SemaphoreType.DMA((2,))],
    )
    near, far = call(
        pack_kernel,
        (shape((2 * FT, 2 * cols + LANES), BF16), shape((FT, 2 * cols + LANES), BF16)),
        (frames, keys, values), specs=[SMEM, VMEM, VMEM],
    )
    near = lax.ppermute(near, "tm", [(i, i + 1) for i in range(count - 1)])
    far = lax.ppermute(far, "tm", [(i, i + 2) for i in range(count - 2)])
    both = lax.ppermute(both, "tm", [(0, 1)])
    rounds = tree_rounds(count)
    for pairs, period in rounds:
        pairs = [pair for pair in pairs if pair != (0, 1)]
        came_k = lax.ppermute(sink_k, "tm", pairs)
        came_v = lax.ppermute(sink_v, "tm", pairs)
        kept = here % period == 0
        sink_k = jnp.where(kept, sink_k, came_k)
        sink_v = jnp.where(kept, sink_v, came_v)
    mine = call(sums_kernel, shape((rows, LANES), F32), (queries, keys))
    other = lax.ppermute(mine, "head", swap)
    ctl, qn, acc, top, den = call(
        lambda *refs: own_kernel(full_width, *refs), (shape((8, LANES), F32), block, wide, wide, wide),
        (frames, flags, queries, keys, values, q_gain, k_gain, mine, other), specs=[SMEM] + [VMEM] * 8,
        scratch=[pltpu.VMEM((rows, cols), BF16)] + scores(rows),
    )
    raw, mine = call(
        gather_kernel, (shape((3 * FT, cols), BF16), shape((3 * FT, LANES), F32)),
        (near, far, sink_k, both),
    )
    other = lax.ppermute(mine, "head", swap)
    return call(
        lambda *refs: finish_kernel(full_width, *refs), block,
        (frames, ctl, qn, raw, k_gain, mine, other, sink_v, both, near, far, acc, top, den),
        specs=[SMEM] + [VMEM] * 13,
        scratch=[pltpu.VMEM((3 * FT, cols), BF16)] + scores(3 * FT)
        + [pltpu.VMEM((cols // HD, rows, HD), F32)],
    )


def solution(mesh):
    placed = (
        P(("groups", "tm"), "head"),
        P(("groups", "tm"), "head"),
        P(("groups", "tm"), "head"),
        P("head"),
        P("head"),
        P(("groups", "tm")),
        P(("groups", "tm"), None),
    )
    return jax.shard_map(
        local, mesh=mesh, in_specs=placed, out_specs=P(("groups", "tm"), "head"), check_vma=False
    )
```

time: 26.1 us -> 27.5 us (1.054)
  the two profiles are of different devices: /device:TPU:10 before, /device:TPU:11 now
where the time goes in v5:
time: 27.5 us; the launch traced here: 27.2 us
  starting transfers between devices  17 us (62%)
  waiting for transfers between devices  5.65 us (21%)
  Pallas kernels  2.62 us (10%)
  between operations  0.93 us (3%)
  local copies, waits for them, and re-layouts  0.92 us (3%)
    ppermute x3, waiting for transfers between devices, local(): came_k = lax.ppermute(sink_k, 'tm', pairs)  4.76 us
    ppermute x2, starting transfers between devices, local(): other = lax.ppermute(mine, 'head', swap)  4.54 us
    ppermute x1, starting transfers between devices, local(): far = lax.ppermute(far, 'tm', [(i, i + 2) for i in range(count - 2)])  3.2 us
    ppermute x1, starting transfers between devices, local(): near = lax.ppermute(near, 'tm', [(i, i + 1) for i in range(count - 1)])  3.18 us
    ppermute x3, starting transfers between devices, local(): came_k = lax.ppermute(sink_k, 'tm', pairs)  2.76 us
    pallas_call x6, Pallas kernels, call(): pl.pallas_call(kernel, out_shape=shapes, in_specs=[VMEM] * len(operands)...  2.62 us
    ppermute x3, starting transfers between devices, local(): came_v = lax.ppermute(sink_v, 'tm', pairs)  2.61 us
    unnamed x12, local copies, waits for them, and re-layouts  0.91 us
  transfers between devices with their start and end apart: 11, of which 2 were waited for; matrix products, arithmetic and copies ran while one was open for 0% of the time, Pallas kernels for 4%

profile of v5, /device:TPU:11, one launch (start us, length us, event | category | flops | bytes accessed | tf_op | source)
XLA Modules:
  0.0 27.2 jit_solution(5229255896877106963)
XLA Ops:
  0.0 0.0 copy-start
  0.0 0.0 copy-start.2
  0.0 0.0 copy-start.1
  0.0 0.8 %collective-permute-start.3 = (bf16[32,1280]{1,0:T(8,128)(2,1)S(1)}, bf16[32,1280]{1,0:T(8,128)(2,1)S(1)}, u32[]{:S(2)}, u32[]{:S(2)}) collective-permute-start(bf16[32,1280]{1,0:T(8,128)(2,1)S(1)} %get-tuple-element.21), channel_id=1, source_target_pairs={{0,8},{1,9},{16,24},{17,25}} | collective-permute-start | bytes 245768 | tf_op jit(solution)/shard_map/ppermute | solution.py:201
  0.8 0.1 copy-done
  0.9 0.1 copy-done.2
  1.1 0.2 shard_map.73.refs_7_
  1.2 0.7 %collective-permute-start = (f32[96,128]{1,0:T(8,128)S(1)}, f32[96,128]{1,0:T(8,128)S(1)}, u32[]{:S(2)}, u32[]{:S(2)}) collective-permute-start(f32[96,128]{1,0:T(8,128)S(1)} %shard_map.73.refs_7_), channel_id=1, source_target_pairs={{0,1},{1,0},{2,3},{3,2},{4,5},{5,4},{6,7},{7,6},{8,9},{9,8},{10,11... | collective-permute-start | bytes 147464 | tf_op jit(solution)/shard_map/ppermute | solution.py:207
  2.0 0.7 %collective-permute-start.8 = (bf16[32,1280]{1,0:T(8,128)(2,1)S(1)}, bf16[32,1280]{1,0:T(8,128)(2,1)S(1)}, u32[]{:S(2)}, u32[]{:S(2)}) collective-permute-start(bf16[32,1280]{1,0:T(8,128)(2,1)S(1)} %get-tuple-element.25), channel_id=1, source_target_pairs={{0,8},{1,9},{16,24},{17,25}} | collective-permute-start | bytes 245768 | tf_op jit(solution)/shard_map/ppermute | solution.py:202
  2.6 0.7 %collective-permute-start.6 = (bf16[32,2560]{1,0:T(8,128)(2,1)S(1)}, bf16[32,2560]{1,0:T(8,128)(2,1)S(1)}, u32[]{:S(2)}, u32[]{:S(2)}) collective-permute-start(bf16[32,2560]{1,0:T(8,128)(2,1)S(1)} %get-tuple-element.22), channel_id=1, source_target_pairs={{0,2},{1,3},{16,18},{17,19}} | collective-permute-start | bytes 491528 | tf_op jit(solution)/shard_map/ppermute | solution.py:197
  4.0 0.0 copy-done.1
  4.0 3.2 %collective-permute-start.2 = (bf16[32,2688]{1,0:T(8,128)(2,1)S(1)}, bf16[32,2688]{1,0:T(8,128)(2,1)S(1)}, u32[]{:S(2)}, u32[]{:S(2)}) collective-permute-start(bf16[32,2688]{1,0:T(8,128)(2,1)S(1)} %get-tuple-element.20), channel_id=1, source_target_pairs={{0,4},{2,6},{4,8},{6,10},{8,12},{10,14},{1,5},{3,7},{5,9},{7,11},{... | collective-permute-start | bytes 516104 | tf_op jit(solution)/shard_map/ppermute | solution.py:196
  7.2 0.0 copy-start.4
  7.3 0.0 copy-start.5
  7.3 0.7 %copy-done.4 = f32[1280]{0:T(1024)S(1)} copy-done((f32[1280]{0:T(1024)S(1)}, f32[1280]{0:T(1024)}, u32[]{:S(2)}) %copy-start.4) | copy-done | bytes 5144
  8.0 0.0 copy-done.5
  8.0 0.0 copy-start.3
  8.0 0.0 collective-permute-done.refs_8_
  8.0 3.2 %collective-permute-start.1 = (bf16[64,2688]{1,0:T(8,128)(2,1)S(1)}, bf16[64,2688]{1,0:T(8,128)(2,1)S(1)}, u32[]{:S(2)}, u32[]{:S(2)}) collective-permute-start(bf16[64,2688]{1,0:T(8,128)(2,1)S(1)} %get-tuple-element.19), channel_id=1, source_target_pairs={{0,2},{2,4},{4,6},{6,8},{8,10},{10,12},{12,14},{1,3},{3,5},{5,7},{... | collective-permute-start | bytes 1032200 | tf_op jit(solution)/shard_map/ppermute | solution.py:195
  11.2 0.0 copy-done.3
  11.2 0.8 %shard_map.74 = (f32[8,128]{1,0:T(8,128)S(1)}, bf16[96,1280]{1,0:T(8,128)(2,1)S(1)}, f32[96,1280]{1,0:T(8,128)S(1)}, f32[96,1280]{1,0:T(8,128)S(1)}, f32[96,1280]{1,0:T(8,128)S(1)}) custom-call(s32[1]{0:T(128)S(6)} %copy.8.refs_0_.frames_ref, s32[1,2]{1,0:T(1,128)S(1)} %copy-done.3, bf16[96,1280]{1,0:T(8,128)(2,1)S(1)} %copy-done.2, ...), custom_call_target="tpu_custom_call" | custom-call | tf_op jit(solution)/shard_map/pallas_call | solution.py:38
  12.0 0.0 collective-permute-done.3
  12.0 0.7 %collective-permute-start.4 = (bf16[32,1280]{1,0:T(8,128)(2,1)S(1)}, bf16[32,1280]{1,0:T(8,128)(2,1)S(1)}, u32[]{:S(2)}, u32[]{:S(2)}) collective-permute-start(bf16[32,1280]{1,0:T(8,128)(2,1)S(1)} %broadcast_select_fusion.1), channel_id=1, source_target_pairs={{0,4},{8,12},{1,5},{9,13},{16,20},{24,28},{17,21},{25,29}} | collective-permute-start | bytes 245768 | tf_op jit(solution)/shard_map/ppermute | solution.py:201
  12.7 0.0 collective-permute-done.8
  12.7 0.7 %collective-permute-start.9 = (bf16[32,1280]{1,0:T(8,128)(2,1)S(1)}, bf16[32,1280]{1,0:T(8,128)(2,1)S(1)}, u32[]{:S(2)}, u32[]{:S(2)}) collective-permute-start(bf16[32,1280]{1,0:T(8,128)(2,1)S(1)} %broadcast_select_fusion), channel_id=1, source_target_pairs={{0,4},{8,12},{1,5},{9,13},{16,20},{24,28},{17,21},{25,29}} | collective-permute-start | bytes 245768 | tf_op jit(solution)/shard_map/ppermute | solution.py:202
  13.4 0.0 collective-permute-done.4
  13.4 1.3 %collective-permute-start.5 = (bf16[32,1280]{1,0:T(8,128)(2,1)S(1)}, bf16[32,1280]{1,0:T(8,128)(2,1)S(1)}, u32[]{:S(2)}, u32[]{:S(2)}) collective-permute-start(bf16[32,1280]{1,0:T(8,128)(2,1)S(1)} %broadcast_select_fusion.3), channel_id=1, source_target_pairs={{4,6},{8,10},{12,14},{5,7},{9,11},{13,15},{20,22},{24,26},{28,30},... | collective-permute-start | bytes 245768 | tf_op jit(solution)/shard_map/ppermute | solution.py:201
  14.7 0.0 collective-permute-done.9
  14.7 1.3 %collective-permute-start.10 = (bf16[32,1280]{1,0:T(8,128)(2,1)S(1)}, bf16[32,1280]{1,0:T(8,128)(2,1)S(1)}, u32[]{:S(2)}, u32[]{:S(2)}) collective-permute-start(bf16[32,1280]{1,0:T(8,128)(2,1)S(1)} %broadcast_select_fusion.2), channel_id=1, source_target_pairs={{4,6},{8,10},{12,14},{5,7},{9,11},{13,15},{20,22},{24,26},{28,30},... | collective-permute-start | bytes 245768 | tf_op jit(solution)/shard_map/ppermute | solution.py:202
  16.0 4.8 %collective-permute-done.5 = bf16[32,1280]{1,0:T(8,128)(2,1)S(1)} collective-permute-done((bf16[32,1280]{1,0:T(8,128)(2,1)S(1)}, bf16[32,1280]{1,0:T(8,128)(2,1)S(1)}, u32[]{:S(2)}, u32[]{:S(2)}) %collective-permute-start.5) | collective-permute-done | bytes 81952 | tf_op jit(solution)/shard_map/ppermute | solution.py:201
  20.8 0.0 collective-permute-done.6.next_ref.refs_8_
  20.8 0.0 collective-permute-done.2.far_ref.refs_10_
  20.8 0.0 collective-permute-done.1.near_ref.refs_9_
  20.9 0.1 shard_map.77
  21.0 3.8 %collective-permute-start.7 = (f32[96,128]{1,0:T(8,128)S(1)}, f32[96,128]{1,0:T(8,128)S(1)}, u32[]{:S(2)}, u32[]{:S(2)}) collective-permute-start(f32[96,128]{1,0:T(8,128)S(1)} %get-tuple-element.24.refs_5_), channel_id=1, source_target_pairs={{0,1},{1,0},{2,3},{3,2},{4,5},{5,4},{6,7},{7,6},{8,9},{9,8},{10,11... | collective-permute-start | bytes 147464 | tf_op jit(solution)/shard_map/ppermute | solution.py:217
  24.8 0.0 collective-permute-done.10
  24.8 0.9 %collective-permute-done.7.refs_6_ = f32[96,128]{1,0:T(8,128)S(1)} collective-permute-done((f32[96,128]{1,0:T(8,128)S(1)}, f32[96,128]{1,0:T(8,128)S(1)}, u32[]{:S(2)}, u32[]{:S(2)}) %collective-permute-start.7) | collective-permute-done | bytes 49184 | tf_op jit(solution)/shard_map/ppermute | solution.py:217
  25.7 1.5 %shard_map.78 = bf16[96,1280]{1,0:T(8,128)(2,1)} custom-call(s32[1]{0:T(128)S(6)} %copy.8.refs_0_.frames_ref, f32[8,128]{1,0:T(8,128)S(1)} %get-tuple-element.17.refs_1_, bf16[96,1280]{1,0:T(8,128)(2,1)S(1)} %get-tuple-element.18.refs_2_, bf16[96,1280]{1,0:T(8,128)(2,1)S(1)} %get-tuple-element.23.refs_3_, f32[1,1280]{1,0:T(1,128)S(1)} %reshape.7.refs_6_.refs_4_, ...), custom_call_target="tpu_custom_call" | custom-call | tf_op jit(solution)/shard_map/pallas_call | solution.py:38
  (10 shorter events, 0.1 us)
Async XLA Ops:
  0.0 0.9 %copy-start = (bf16[96,1280]{1,0:T(8,128)(2,1)S(1)}, bf16[96,1280]{1,0:T(8,128)(2,1)}, u32[]{:S(2)}) copy-start(bf16[96,1280]{1,0:T(8,128)(2,1)} %k_hbm.1) | copy-start | bytes 737284
  0.0 1.1 %copy-start.2 = (bf16[96,1280]{1,0:T(8,128)(2,1)S(1)}, bf16[96,1280]{1,0:T(8,128)(2,1)}, u32[]{:S(2)}) copy-start(bf16[96,1280]{1,0:T(8,128)(2,1)} %refs_2_.1) | copy-start | bytes 737284
  0.0 3.9 %copy-start.1 = (bf16[96,1280]{1,0:T(8,128)(2,1)S(1)}, bf16[96,1280]{1,0:T(8,128)(2,1)}, u32[]{:S(2)}) copy-start(bf16[96,1280]{1,0:T(8,128)(2,1)} %v_hbm.1) | copy-start | bytes 737284
  0.0 11.9 %collective-permute-start.3 = (bf16[32,1280]{1,0:T(8,128)(2,1)S(1)}, bf16[32,1280]{1,0:T(8,128)(2,1)S(1)}, u32[]{:S(2)}, u32[]{:S(2)}) collective-permute-start(bf16[32,1280]{1,0:T(8,128)(2,1)S(1)} %get-tuple-element.21), channel_id=1, source_target_pairs={{0,8},{1,9},{16,24},{17,25}} | collective-permute-start | bytes 245768 | tf_op jit(solution)/shard_map/ppermute | solution.py:201
  1.2 6.8 %collective-permute-start = (f32[96,128]{1,0:T(8,128)S(1)}, f32[96,128]{1,0:T(8,128)S(1)}, u32[]{:S(2)}, u32[]{:S(2)}) collective-permute-start(f32[96,128]{1,0:T(8,128)S(1)} %shard_map.73.refs_7_), channel_id=1, source_target_pairs={{0,1},{1,0},{2,3},{3,2},{4,5},{5,4},{6,7},{7,6},{8,9},{9,8},{10,11... | collective-permute-start | bytes 147464 | tf_op jit(solution)/shard_map/ppermute | solution.py:207
  2.0 10.7 %collective-permute-start.8 = (bf16[32,1280]{1,0:T(8,128)(2,1)S(1)}, bf16[32,1280]{1,0:T(8,128)(2,1)S(1)}, u32[]{:S(2)}, u32[]{:S(2)}) collective-permute-start(bf16[32,1280]{1,0:T(8,128)(2,1)S(1)} %get-tuple-element.25), channel_id=1, source_target_pairs={{0,8},{1,9},{16,24},{17,25}} | collective-permute-start | bytes 245768 | tf_op jit(solution)/shard_map/ppermute | solution.py:202
  2.6 18.2 %collective-permute-start.6 = (bf16[32,2560]{1,0:T(8,128)(2,1)S(1)}, bf16[32,2560]{1,0:T(8,128)(2,1)S(1)}, u32[]{:S(2)}, u32[]{:S(2)}) collective-permute-start(bf16[32,2560]{1,0:T(8,128)(2,1)S(1)} %get-tuple-element.22), channel_id=1, source_target_pairs={{0,2},{1,3},{16,18},{17,19}} | collective-permute-start | bytes 491528 | tf_op jit(solution)/shard_map/ppermute | solution.py:197
  4.0 16.8 %collective-permute-start.2 = (bf16[32,2688]{1,0:T(8,128)(2,1)S(1)}, bf16[32,2688]{1,0:T(8,128)(2,1)S(1)}, u32[]{:S(2)}, u32[]{:S(2)}) collective-permute-start(bf16[32,2688]{1,0:T(8,128)(2,1)S(1)} %get-tuple-element.20), channel_id=1, source_target_pairs={{0,4},{2,6},{4,8},{6,10},{8,12},{10,14},{1,5},{3,7},{5,9},{7,11},{... | collective-permute-start | bytes 516104 | tf_op jit(solution)/shard_map/ppermute | solution.py:196
  7.2 0.7 %copy-start.4 = (f32[1280]{0:T(1024)S(1)}, f32[1280]{0:T(1024)}, u32[]{:S(2)}) copy-start(f32[1280]{0:T(1024)} %param.11) | copy-start | bytes 15364
  7.3 0.7 %copy-start.5 = (f32[1280]{0:T(1024)S(1)}, f32[1280]{0:T(1024)}, u32[]{:S(2)}) copy-start(f32[1280]{0:T(1024)} %param.10) | copy-start | bytes 15364
  8.0 3.2 %copy-start.3 = (s32[1,2]{1,0:T(1,128)S(1)}, s32[1,2]{1,0:T(1,128)}, u32[]{:S(2)}) copy-start(s32[1,2]{1,0:T(1,128)} %refs_1_.1) | copy-start | bytes 28
  8.0 12.9 %collective-permute-start.1 = (bf16[64,2688]{1,0:T(8,128)(2,1)S(1)}, bf16[64,2688]{1,0:T(8,128)(2,1)S(1)}, u32[]{:S(2)}, u32[]{:S(2)}) collective-permute-start(bf16[64,2688]{1,0:T(8,128)(2,1)S(1)} %get-tuple-element.19), channel_id=1, source_target_pairs={{0,2},{2,4},{4,6},{6,8},{8,10},{10,12},{12,14},{1,3},{3,5},{5,7},{... | collective-permute-start | bytes 1032200 | tf_op jit(solution)/shard_map/ppermute | solution.py:195
  12.0 1.4 %collective-permute-start.4 = (bf16[32,1280]{1,0:T(8,128)(2,1)S(1)}, bf16[32,1280]{1,0:T(8,128)(2,1)S(1)}, u32[]{:S(2)}, u32[]{:S(2)}) collective-permute-start(bf16[32,1280]{1,0:T(8,128)(2,1)S(1)} %broadcast_select_fusion.1), channel_id=1, source_target_pairs={{0,4},{8,12},{1,5},{9,13},{16,20},{24,28},{17,21},{25,29}} | collective-permute-start | bytes 245768 | tf_op jit(solution)/shard_map/ppermute | solution.py:201
  12.7 2.0 %collective-permute-start.9 = (bf16[32,1280]{1,0:T(8,128)(2,1)S(1)}, bf16[32,1280]{1,0:T(8,128)(2,1)S(1)}, u32[]{:S(2)}, u32[]{:S(2)}) collective-permute-start(bf16[32,1280]{1,0:T(8,128)(2,1)S(1)} %broadcast_select_fusion), channel_id=1, source_target_pairs={{0,4},{8,12},{1,5},{9,13},{16,20},{24,28},{17,21},{25,29}} | collective-permute-start | bytes 245768 | tf_op jit(solution)/shard_map/ppermute | solution.py:202
  13.4 7.4 %collective-permute-start.5 = (bf16[32,1280]{1,0:T(8,128)(2,1)S(1)}, bf16[32,1280]{1,0:T(8,128)(2,1)S(1)}, u32[]{:S(2)}, u32[]{:S(2)}) collective-permute-start(bf16[32,1280]{1,0:T(8,128)(2,1)S(1)} %broadcast_select_fusion.3), channel_id=1, source_target_pairs={{4,6},{8,10},{12,14},{5,7},{9,11},{13,15},{20,22},{24,26},{28,30},... | collective-permute-start | bytes 245768 | tf_op jit(solution)/shard_map/ppermute | solution.py:201
  14.7 10.1 %collective-permute-start.10 = (bf16[32,1280]{1,0:T(8,128)(2,1)S(1)}, bf16[32,1280]{1,0:T(8,128)(2,1)S(1)}, u32[]{:S(2)}, u32[]{:S(2)}) collective-permute-start(bf16[32,1280]{1,0:T(8,128)(2,1)S(1)} %broadcast_select_fusion.2), channel_id=1, source_target_pairs={{4,6},{8,10},{12,14},{5,7},{9,11},{13,15},{20,22},{24,26},{28,30},... | collective-permute-start | bytes 245768 | tf_op jit(solution)/shard_map/ppermute | solution.py:202
  21.0 4.7 %collective-permute-start.7 = (f32[96,128]{1,0:T(8,128)S(1)}, f32[96,128]{1,0:T(8,128)S(1)}, u32[]{:S(2)}, u32[]{:S(2)}) collective-permute-start(f32[96,128]{1,0:T(8,128)S(1)} %get-tuple-element.24.refs_5_), channel_id=1, source_target_pairs={{0,1},{1,0},{2,3},{3,2},{4,5},{5,4},{6,7},{7,6},{8,9},{9,8},{10,11... | collective-permute-start | bytes 147464 | tf_op jit(solution)/shard_map/ppermute | solution.py:217

commit v6 on v5

--- a/solution.py
+++ b/solution.py
@@ -89,15 +89,25 @@
     sums_ref[...] = jnp.where(lane < LANES // 2, square_sums(q_ref), square_sums(k_ref))
 
 
-def own_kernel(full_width, frames_ref, flags_ref, q_ref, k_ref, v_ref, qg_ref, kg_ref, mine_ref, other_ref,
-               ctl_ref, qn_ref, acc_ref, top_ref, den_ref, kn_ref, score_ref, weight_ref):
+def own_kernel(full_width, frames_ref, flags_hbm, q_ref, k_ref, v_ref, qg_hbm, kg_hbm, mine_ref, other_ref,
+               ctl_ref, gains_ref, qn_ref, acc_ref, top_ref, den_ref,
+               kn_ref, score_ref, weight_ref, qg_ref, kg_ref, flags_ref, sem):
     rows, cols = q_ref.shape
-    flags = flags_ref[...].astype(F32)
+    copies = [
+        pltpu.make_async_copy(source, target, sem.at[i])
+        for i, (source, target) in enumerate(((qg_hbm, qg_ref), (kg_hbm, kg_ref), (flags_hbm, flags_ref)))
+    ]
+    for copy in copies:
+        copy.start()
+    for copy in copies:
+        copy.wait()
     row = lax.broadcasted_iota(jnp.int32, ctl_ref.shape, 0)
-    ctl_ref[...] = jnp.where(row == 0, flags[:, :1], flags[:, 1:2])
+    ctl_ref[...] = jnp.where(row == 0, flags_ref[0, 0], flags_ref[0, 1]).astype(F32)
+    gains_ref[:1, :] = qg_ref[...].reshape(1, cols)
+    gains_ref[1:2, :] = kg_ref[...].reshape(1, cols)
     factor = lax.rsqrt((mine_ref[...] + other_ref[...]) / full_width + EPSILON)
-    qn_ref[...] = (q_ref[...].astype(F32) * factor[:, :1] * qg_ref[...]).astype(BF16)
-    kn_ref[...] = (k_ref[...].astype(F32) * factor[:, LANES // 2:LANES // 2 + 1] * kg_ref[...]).astype(BF16)
+    qn_ref[...] = (q_ref[...].astype(F32) * factor[:, :1] * gains_ref[:1, :]).astype(BF16)
+    kn_ref[...] = (k_ref[...].astype(F32) * factor[:, LANES // 2:LANES // 2 + 1] * gains_ref[1:2, :]).astype(BF16)
     heads = [(i, i * HD, (i + 1) * HD) for i in range(cols // HD)]
     allowed = lax.broadcasted_iota(jnp.int32, (rows, rows), 1) < frames_ref[0] * FT
     ones = jnp.ones((rows, HD), BF16)
@@ -117,22 +127,32 @@
         den_ref[:, a:b] = both[:, HD:]
 
 
-def gather_kernel(near_ref, far_ref, sink_k_ref, next_ref, keys_ref, sums_ref):
+def gather_kernel(near_ref, far_ref, sink_k_ref, next_ref, gains_ref, keys_ref, sums_ref, raw_ref):
     cols = sink_k_ref.shape[1]
     pick = jnp.broadcast_to(near_ref[:1, 2 * cols:2 * cols + 1].astype(F32), (FT, cols)) > 1.5
     second = jnp.full((FT, cols), lax.axis_index("tm"), jnp.int32) == 1
-    keys_ref[:FT, :] = near_ref[:FT, :cols]
-    keys_ref[FT:2 * FT, :] = jnp.where(pick, near_ref[FT:, :cols], far_ref[:, :cols])
-    keys_ref[2 * FT:, :] = jnp.where(second, next_ref[:, :cols], sink_k_ref[...])
-    sums_ref[...] = jnp.broadcast_to(square_sums(keys_ref), sums_ref.shape)
-
-
-def finish_kernel(full_width, frames_ref, ctl_ref, q_ref, raw_ref, kg_ref, mine_ref, other_ref, sink_v_ref, next_ref,
-                  near_ref, far_ref, acc_ref, top_ref, den_ref, out_ref, keys_ref, score_ref, weight_ref, keep_ref):
-    rows, cols = q_ref.shape
+    raw_ref[:FT, :] = near_ref[:FT, :cols]
+    raw_ref[FT:2 * FT, :] = jnp.where(pick, near_ref[FT:, :cols], far_ref[:, :cols])
+    raw_ref[2 * FT:, :] = jnp.where(second, next_ref[:, :cols], sink_k_ref[...])
+    sums_ref[...] = jnp.zeros_like(sums_ref)
+    sums_ref[:3 * FT, :] = jnp.broadcast_to(square_sums(raw_ref), (3 * FT, LANES))
+    keys_ref[...] = (raw_ref[...].astype(F32) * gains_ref[1:2, :]).astype(BF16)
+
+
+def score_kernel(q_ref, keys_ref, score_ref):
+    for i in range(q_ref.shape[1] // HD):
+        a, b = i * HD, (i + 1) * HD
+        score_ref[i] = lax.dot_general(
+            q_ref[:, a:b], keys_ref[:, a:b], (((1,), (1,)), ((), ())), preferred_element_type=F32
+        )
+
+
+def finish_kernel(full_width, frames_ref, ctl_ref, score_ref, mine_ref, other_ref, sink_v_ref, next_ref,
+                  near_ref, far_ref, acc_ref, top_ref, den_ref, out_ref, weight_ref, keep_ref):
+    rows, cols = out_ref.shape
     span = 3 * FT
-    factor = lax.rsqrt((mine_ref[:, :1] + other_ref[:, :1]) / full_width + EPSILON)
-    keys_ref[...] = (raw_ref[...].astype(F32) * factor * kg_ref[...]).astype(BF16)
+    factor = lax.rsqrt((mine_ref[...] + other_ref[...]) / full_width + EPSILON) * (1.0 / math.sqrt(HD))
+    factor = jnp.broadcast_to(jnp.transpose(factor)[:1, :span], (rows, span))
     heads = [(i, i * HD, (i + 1) * HD) for i in range(cols // HD)]
     sink = ctl_ref[:1, :1]
     window = ctl_ref[1:2, :1]
@@ -147,12 +167,7 @@
     second = jnp.full((FT, HD), lax.axis_index("tm"), jnp.int32) == 1
     ones = jnp.ones((span, HD), BF16)
     for i, a, b in heads:
-        score = lax.dot_general(
-            q_ref[:, a:b], keys_ref[:, a:b], (((1,), (1,)), ((), ())), preferred_element_type=F32
-        ) * (1.0 / math.sqrt(HD))
-        score_ref[i] = jnp.where(allowed, score, -jnp.inf)
-    for i, a, b in heads:
-        score = score_ref[i]
+        score = jnp.where(allowed, score_ref[i] * factor, -jnp.inf)
         old = top_ref[:, a:b]
         top = jnp.maximum(old, jnp.max(score, axis=1, keepdims=True))
         keep_ref[i] = jnp.exp(old - top)
@@ -178,7 +193,6 @@
     block = shape((rows, cols), BF16)
     wide = shape((rows, cols), F32)
     frame = shape((FT, cols), BF16)
-    q_gain, k_gain = q_gain.reshape(1, cols), k_gain.reshape(1, cols)
     swap = [(h, (h + 1) % heads) for h in range(heads)]
     in_hbm = lambda x: pltpu.with_memory_space_constraint(x, pltpu.HBM)
     scores = lambda n: [pltpu.VMEM((cols // HD, rows, n), F32), pltpu.VMEM((cols // HD, rows, n), BF16)]
@@ -205,22 +219,31 @@
         sink_v = jnp.where(kept, sink_v, came_v)
     mine = call(sums_kernel, shape((rows, LANES), F32), (queries, keys))
     other = lax.ppermute(mine, "head", swap)
-    ctl, qn, acc, top, den = call(
-        lambda *refs: own_kernel(full_width, *refs), (shape((8, LANES), F32), block, wide, wide, wide),
-        (frames, flags, queries, keys, values, q_gain, k_gain, mine, other), specs=[SMEM] + [VMEM] * 8,
-        scratch=[pltpu.VMEM((rows, cols), BF16)] + scores(rows),
-    )
-    raw, mine = call(
-        gather_kernel, (shape((3 * FT, cols), BF16), shape((3 * FT, LANES), F32)),
-        (near, far, sink_k, both),
+    ctl, gains, qn, acc, top, den = call(
+        lambda *refs: own_kernel(full_width, *refs),
+        (shape((8, LANES), F32), shape((8, cols), F32), block, wide, wide, wide),
+        (
+            frames, in_hbm(flags), queries, keys, values, in_hbm(q_gain), in_hbm(k_gain), mine, other,
+        ),
+        specs=[SMEM, HBM, VMEM, VMEM, VMEM, HBM, HBM, VMEM, VMEM],
+        scratch=[pltpu.VMEM((rows, cols), BF16)] + scores(rows) + [
+            pltpu.VMEM((cols,), F32), pltpu.VMEM((cols,), F32), pltpu.SMEM((1, 2), jnp.int32),
+            pltpu.SemaphoreType.DMA((3,)),
+        ],
+    )
+    keys, mine = call(
+        gather_kernel, (shape((3 * FT, cols), BF16), shape((LANES, LANES), F32)),
+        (near, far, sink_k, both, gains), scratch=[pltpu.VMEM((3 * FT, cols), BF16)],
     )
     other = lax.ppermute(mine, "head", swap)
+    score = call(score_kernel, shape((cols // HD, rows, 3 * FT), F32), (qn, keys))
     return call(
         lambda *refs: finish_kernel(full_width, *refs), block,
-        (frames, ctl, qn, raw, k_gain, mine, other, sink_v, both, near, far, acc, top, den),
-        specs=[SMEM] + [VMEM] * 13,
-        scratch=[pltpu.VMEM((3 * FT, cols), BF16)] + scores(3 * FT)
-        + [pltpu.VMEM((cols // HD, rows, HD), F32)],
+        (frames, ctl, score, mine, other, sink_v, both, near, far, acc, top, den),
+        specs=[SMEM] + [VMEM] * 11,
+        scratch=[
+            pltpu.VMEM((cols // HD, rows, 3 * FT), BF16), pltpu.VMEM((cols // HD, rows, HD), F32),
+        ],
     )
 
 

time: 27.5 us -> 27.4 us (level)
  the two profiles are of different devices: /device:TPU:11 before, /device:TPU:15 now
where the time goes in v6:
time: 27.4 us; the launch traced here: 27 us
  starting transfers between devices  16.9 us (62%)
  waiting for transfers between devices  5.41 us (20%)
  Pallas kernels  3.47 us (13%)
  between operations  0.9 us (3%)
    ppermute x3, waiting for transfers between devices, local(): came_k = lax.ppermute(sink_k, 'tm', pairs)  4.76 us
    ppermute x2, starting transfers between devices, local(): other = lax.ppermute(mine, 'head', swap)  4.53 us
    pallas_call x7, Pallas kernels, call(): pl.pallas_call(kernel, out_shape=shapes, in_specs=[VMEM] * len(operands)...  3.47 us
    ppermute x1, starting transfers between devices, local(): far = lax.ppermute(far, 'tm', [(i, i + 2) for i in range(count - 2)])  3.2 us
    ppermute x1, starting transfers between devices, local(): near = lax.ppermute(near, 'tm', [(i, i + 1) for i in range(count - 1)])  3.18 us
    ppermute x3, starting transfers between devices, local(): came_k = lax.ppermute(sink_k, 'tm', pairs)  2.76 us
    ppermute x3, starting transfers between devices, local(): came_v = lax.ppermute(sink_v, 'tm', pairs)  2.61 us
    ppermute x1, starting transfers between devices, local(): both = lax.ppermute(both, 'tm', [(0, 1)])  0.67 us
  transfers between devices with their start and end apart: 11, of which 2 were waited for; matrix products, arithmetic and copies ran while one was open for 0% of the time, Pallas kernels for 8%

profile of v6, /device:TPU:15, one launch (start us, length us, event | category | flops | bytes accessed | tf_op | source)
XLA Modules:
  0.0 27.0 jit_solution(4905032175821263119)
XLA Ops:
  0.0 0.0 copy-start
  0.0 0.0 copy-start.2
  0.0 0.0 copy-start.1
  0.0 0.8 %collective-permute-start.3 = (bf16[32,1280]{1,0:T(8,128)(2,1)S(1)}, bf16[32,1280]{1,0:T(8,128)(2,1)S(1)}, u32[]{:S(2)}, u32[]{:S(2)}) collective-permute-start(bf16[32,1280]{1,0:T(8,128)(2,1)S(1)} %get-tuple-element.22), channel_id=1, source_target_pairs={{0,8},{1,9},{16,24},{17,25}} | collective-permute-start | bytes 245768 | tf_op jit(solution)/shard_map/ppermute | solution.py:215
  0.8 0.1 copy-done
  0.9 0.1 copy-done.2
  1.1 0.2 shard_map.73.refs_7_
  1.2 0.7 %collective-permute-start = (f32[96,128]{1,0:T(8,128)S(1)}, f32[96,128]{1,0:T(8,128)S(1)}, u32[]{:S(2)}, u32[]{:S(2)}) collective-permute-start(f32[96,128]{1,0:T(8,128)S(1)} %shard_map.73.refs_7_), channel_id=1, source_target_pairs={{0,1},{1,0},{2,3},{3,2},{4,5},{5,4},{6,7},{7,6},{8,9},{9,8},{10,11... | collective-permute-start | bytes 147464 | tf_op jit(solution)/shard_map/ppermute | solution.py:221
  2.0 0.7 %collective-permute-start.8 = (bf16[32,1280]{1,0:T(8,128)(2,1)S(1)}, bf16[32,1280]{1,0:T(8,128)(2,1)S(1)}, u32[]{:S(2)}, u32[]{:S(2)}) collective-permute-start(bf16[32,1280]{1,0:T(8,128)(2,1)S(1)} %get-tuple-element.27), channel_id=1, source_target_pairs={{0,8},{1,9},{16,24},{17,25}} | collective-permute-start | bytes 245768 | tf_op jit(solution)/shard_map/ppermute | solution.py:216
  2.6 0.7 %collective-permute-start.6 = (bf16[32,2560]{1,0:T(8,128)(2,1)S(1)}, bf16[32,2560]{1,0:T(8,128)(2,1)S(1)}, u32[]{:S(2)}, u32[]{:S(2)}) collective-permute-start(bf16[32,2560]{1,0:T(8,128)(2,1)S(1)} %get-tuple-element.23), channel_id=1, source_target_pairs={{0,2},{1,3},{16,18},{17,19}} | collective-permute-start | bytes 491528 | tf_op jit(solution)/shard_map/ppermute | solution.py:211
  4.0 0.0 copy-done.1
  4.0 3.2 %collective-permute-start.2 = (bf16[32,2688]{1,0:T(8,128)(2,1)S(1)}, bf16[32,2688]{1,0:T(8,128)(2,1)S(1)}, u32[]{:S(2)}, u32[]{:S(2)}) collective-permute-start(bf16[32,2688]{1,0:T(8,128)(2,1)S(1)} %get-tuple-element.21), channel_id=1, source_target_pairs={{0,4},{2,6},{4,8},{6,10},{8,12},{10,14},{1,5},{3,7},{5,9},{7,11},{... | collective-permute-start | bytes 516104 | tf_op jit(solution)/shard_map/ppermute | solution.py:210
  7.3 0.0 collective-permute-done.refs_8_
  7.3 3.2 %collective-permute-start.1 = (bf16[64,2688]{1,0:T(8,128)(2,1)S(1)}, bf16[64,2688]{1,0:T(8,128)(2,1)S(1)}, u32[]{:S(2)}, u32[]{:S(2)}) collective-permute-start(bf16[64,2688]{1,0:T(8,128)(2,1)S(1)} %get-tuple-element.20), channel_id=1, source_target_pairs={{0,2},{2,4},{4,6},{6,8},{8,10},{10,12},{12,14},{1,3},{3,5},{5,7},{... | collective-permute-start | bytes 1032200 | tf_op jit(solution)/shard_map/ppermute | solution.py:209
  10.5 1.6 %shard_map.74 = (f32[8,128]{1,0:T(8,128)S(1)}, f32[8,1280]{1,0:T(8,128)S(1)}, bf16[96,1280]{1,0:T(8,128)(2,1)S(1)}, f32[96,1280]{1,0:T(8,128)S(1)}, f32[96,1280]{1,0:T(8,128)S(1)}, /*index=5*/f32[96,1280]{1,0:T(8,128)S(1)}) custom-call(s32[1]{0:T(128)S(6)} %copy.8.refs_0_.frames_ref, s32[1,2]{1,0:T(1,128)} %refs_1_.1, bf16[96,1280]{1,0:T(8,128)(2,1)S(1)} %copy-done.2, ...), custom_call_target="tpu_custom_call" | custom-call | tf_op jit(solution)/shard_map/pallas_call | solution.py:38
  12.1 0.0 collective-permute-done.3
  12.1 0.7 %collective-permute-start.4 = (bf16[32,1280]{1,0:T(8,128)(2,1)S(1)}, bf16[32,1280]{1,0:T(8,128)(2,1)S(1)}, u32[]{:S(2)}, u32[]{:S(2)}) collective-permute-start(bf16[32,1280]{1,0:T(8,128)(2,1)S(1)} %broadcast_select_fusion.1), channel_id=1, source_target_pairs={{0,4},{8,12},{1,5},{9,13},{16,20},{24,28},{17,21},{25,29}} | collective-permute-start | bytes 245768 | tf_op jit(solution)/shard_map/ppermute | solution.py:215
  12.8 0.0 collective-permute-done.8
  12.8 0.7 %collective-permute-start.9 = (bf16[32,1280]{1,0:T(8,128)(2,1)S(1)}, bf16[32,1280]{1,0:T(8,128)(2,1)S(1)}, u32[]{:S(2)}, u32[]{:S(2)}) collective-permute-start(bf16[32,1280]{1,0:T(8,128)(2,1)S(1)} %broadcast_select_fusion), channel_id=1, source_target_pairs={{0,4},{8,12},{1,5},{9,13},{16,20},{24,28},{17,21},{25,29}} | collective-permute-start | bytes 245768 | tf_op jit(solution)/shard_map/ppermute | solution.py:216
  13.5 0.0 collective-permute-done.4
  13.5 1.3 %collective-permute-start.5 = (bf16[32,1280]{1,0:T(8,128)(2,1)S(1)}, bf16[32,1280]{1,0:T(8,128)(2,1)S(1)}, u32[]{:S(2)}, u32[]{:S(2)}) collective-permute-start(bf16[32,1280]{1,0:T(8,128)(2,1)S(1)} %broadcast_select_fusion.3), channel_id=1, source_target_pairs={{4,6},{8,10},{12,14},{5,7},{9,11},{13,15},{20,22},{24,26},{28,30},... | collective-permute-start | bytes 245768 | tf_op jit(solution)/shard_map/ppermute | solution.py:215
  14.8 0.0 collective-permute-done.9
  14.8 1.3 %collective-permute-start.10 = (bf16[32,1280]{1,0:T(8,128)(2,1)S(1)}, bf16[32,1280]{1,0:T(8,128)(2,1)S(1)}, u32[]{:S(2)}, u32[]{:S(2)}) collective-permute-start(bf16[32,1280]{1,0:T(8,128)(2,1)S(1)} %broadcast_select_fusion.2), channel_id=1, source_target_pairs={{4,6},{8,10},{12,14},{5,7},{9,11},{13,15},{20,22},{24,26},{28,30},... | collective-permute-start | bytes 245768 | tf_op jit(solution)/shard_map/ppermute | solution.py:216
  16.1 4.8 %collective-permute-done.5 = bf16[32,1280]{1,0:T(8,128)(2,1)S(1)} collective-permute-done((bf16[32,1280]{1,0:T(8,128)(2,1)S(1)}, bf16[32,1280]{1,0:T(8,128)(2,1)S(1)}, u32[]{:S(2)}, u32[]{:S(2)}) %collective-permute-start.5) | collective-permute-done | bytes 81952 | tf_op jit(solution)/shard_map/ppermute | solution.py:215
  20.9 0.0 collective-permute-done.6.next_ref.refs_6_
  20.9 0.0 collective-permute-done.2.far_ref.refs_8_
  20.9 0.0 collective-permute-done.1.near_ref.refs_7_
  20.9 0.2 shard_map.77
  21.1 3.8 %collective-permute-start.7 = (f32[128,128]{1,0:T(8,128)S(1)}, f32[128,128]{1,0:T(8,128)S(1)}, u32[]{:S(2)}, u32[]{:S(2)}) collective-permute-start(f32[128,128]{1,0:T(8,128)S(1)} %get-tuple-element.26.refs_3_), channel_id=1, source_target_pairs={{0,1},{1,0},{2,3},{3,2},{4,5},{5,4},{6,7},{7,6},{8,9},{9,8},{10,11... | collective-permute-start | bytes 196616 | tf_op jit(solution)/shard_map/ppermute | solution.py:238
  24.9 0.0 collective-permute-done.10
  24.9 0.3 shard_map.78.refs_2_
  25.2 0.6 %collective-permute-done.7.refs_4_ = f32[128,128]{1,0:T(8,128)S(1)} collective-permute-done((f32[128,128]{1,0:T(8,128)S(1)}, f32[128,128]{1,0:T(8,128)S(1)}, u32[]{:S(2)}, u32[]{:S(2)}) %collective-permute-start.7) | collective-permute-done | bytes 65568 | tf_op jit(solution)/shard_map/ppermute | solution.py:238
  25.8 1.2 %shard_map.79 = bf16[96,1280]{1,0:T(8,128)(2,1)} custom-call(s32[1]{0:T(128)S(6)} %copy.8.refs_0_.frames_ref, f32[8,128]{1,0:T(8,128)S(1)} %get-tuple-element.18.refs_1_, f32[10,96,96]{2,1,0:T(8,128)S(1)} %shard_map.78.refs_2_, f32[128,128]{1,0:T(8,128)S(1)} %get-tuple-element.26.refs_3_, f32[128,128]{1,0:T(8,128)S(1)} %collective-permute-done.7.refs_4_, ...), custom_call_target="tpu_custom_call" | custom-call | tf_op jit(solution)/shard_map/pallas_call | solution.py:38
  (8 shorter events, 0.1 us)
Async XLA Ops:
  0.0 0.9 %copy-start = (bf16[96,1280]{1,0:T(8,128)(2,1)S(1)}, bf16[96,1280]{1,0:T(8,128)(2,1)}, u32[]{:S(2)}) copy-start(bf16[96,1280]{1,0:T(8,128)(2,1)} %k_hbm.1) | copy-start | bytes 737284
  0.0 1.1 %copy-start.2 = (bf16[96,1280]{1,0:T(8,128)(2,1)S(1)}, bf16[96,1280]{1,0:T(8,128)(2,1)}, u32[]{:S(2)}) copy-start(bf16[96,1280]{1,0:T(8,128)(2,1)} %refs_2_.1) | copy-start | bytes 737284
  0.0 3.9 %copy-start.1 = (bf16[96,1280]{1,0:T(8,128)(2,1)S(1)}, bf16[96,1280]{1,0:T(8,128)(2,1)}, u32[]{:S(2)}) copy-start(bf16[96,1280]{1,0:T(8,128)(2,1)} %v_hbm.1) | copy-start | bytes 737284
  0.0 12.0 %collective-permute-start.3 = (bf16[32,1280]{1,0:T(8,128)(2,1)S(1)}, bf16[32,1280]{1,0:T(8,128)(2,1)S(1)}, u32[]{:S(2)}, u32[]{:S(2)}) collective-permute-start(bf16[32,1280]{1,0:T(8,128)(2,1)S(1)} %get-tuple-element.22), channel_id=1, source_target_pairs={{0,8},{1,9},{16,24},{17,25}} | collective-permute-start | bytes 245768 | tf_op jit(solution)/shard_map/ppermute | solution.py:215
  1.2 6.0 %collective-permute-start = (f32[96,128]{1,0:T(8,128)S(1)}, f32[96,128]{1,0:T(8,128)S(1)}, u32[]{:S(2)}, u32[]{:S(2)}) collective-permute-start(f32[96,128]{1,0:T(8,128)S(1)} %shard_map.73.refs_7_), channel_id=1, source_target_pairs={{0,1},{1,0},{2,3},{3,2},{4,5},{5,4},{6,7},{7,6},{8,9},{9,8},{10,11... | collective-permute-start | bytes 147464 | tf_op jit(solution)/shard_map/ppermute | solution.py:221
  2.0 10.8 %collective-permute-start.8 = (bf16[32,1280]{1,0:T(8,128)(2,1)S(1)}, bf16[32,1280]{1,0:T(8,128)(2,1)S(1)}, u32[]{:S(2)}, u32[]{:S(2)}) collective-permute-start(bf16[32,1280]{1,0:T(8,128)(2,1)S(1)} %get-tuple-element.27), channel_id=1, source_target_pairs={{0,8},{1,9},{16,24},{17,25}} | collective-permute-start | bytes 245768 | tf_op jit(solution)/shard_map/ppermute | solution.py:216
  2.6 18.3 %collective-permute-start.6 = (bf16[32,2560]{1,0:T(8,128)(2,1)S(1)}, bf16[32,2560]{1,0:T(8,128)(2,1)S(1)}, u32[]{:S(2)}, u32[]{:S(2)}) collective-permute-start(bf16[32,2560]{1,0:T(8,128)(2,1)S(1)} %get-tuple-element.23), channel_id=1, source_target_pairs={{0,2},{1,3},{16,18},{17,19}} | collective-permute-start | bytes 491528 | tf_op jit(solution)/shard_map/ppermute | solution.py:211
  4.0 16.9 %collective-permute-start.2 = (bf16[32,2688]{1,0:T(8,128)(2,1)S(1)}, bf16[32,2688]{1,0:T(8,128)(2,1)S(1)}, u32[]{:S(2)}, u32[]{:S(2)}) collective-permute-start(bf16[32,2688]{1,0:T(8,128)(2,1)S(1)} %get-tuple-element.21), channel_id=1, source_target_pairs={{0,4},{2,6},{4,8},{6,10},{8,12},{10,14},{1,5},{3,7},{5,9},{7,11},{... | collective-permute-start | bytes 516104 | tf_op jit(solution)/shard_map/ppermute | solution.py:210
  7.3 13.7 %collective-permute-start.1 = (bf16[64,2688]{1,0:T(8,128)(2,1)S(1)}, bf16[64,2688]{1,0:T(8,128)(2,1)S(1)}, u32[]{:S(2)}, u32[]{:S(2)}) collective-permute-start(bf16[64,2688]{1,0:T(8,128)(2,1)S(1)} %get-tuple-element.20), channel_id=1, source_target_pairs={{0,2},{2,4},{4,6},{6,8},{8,10},{10,12},{12,14},{1,3},{3,5},{5,7},{... | collective-permute-start | bytes 1032200 | tf_op jit(solution)/shard_map/ppermute | solution.py:209
  12.1 1.4 %collective-permute-start.4 = (bf16[32,1280]{1,0:T(8,128)(2,1)S(1)}, bf16[32,1280]{1,0:T(8,128)(2,1)S(1)}, u32[]{:S(2)}, u32[]{:S(2)}) collective-permute-start(bf16[32,1280]{1,0:T(8,128)(2,1)S(1)} %broadcast_select_fusion.1), channel_id=1, source_target_pairs={{0,4},{8,12},{1,5},{9,13},{16,20},{24,28},{17,21},{25,29}} | collective-permute-start | bytes 245768 | tf_op jit(solution)/shard_map/ppermute | solution.py:215
  12.8 2.0 %collective-permute-start.9 = (bf16[32,1280]{1,0:T(8,128)(2,1)S(1)}, bf16[32,1280]{1,0:T(8,128)(2,1)S(1)}, u32[]{:S(2)}, u32[]{:S(2)}) collective-permute-start(bf16[32,1280]{1,0:T(8,128)(2,1)S(1)} %broadcast_select_fusion), channel_id=1, source_target_pairs={{0,4},{8,12},{1,5},{9,13},{16,20},{24,28},{17,21},{25,29}} | collective-permute-start | bytes 245768 | tf_op jit(solution)/shard_map/ppermute | solution.py:216
  13.5 7.4 %collective-permute-start.5 = (bf16[32,1280]{1,0:T(8,128)(2,1)S(1)}, bf16[32,1280]{1,0:T(8,128)(2,1)S(1)}, u32[]{:S(2)}, u32[]{:S(2)}) collective-permute-start(bf16[32,1280]{1,0:T(8,128)(2,1)S(1)} %broadcast_select_fusion.3), channel_id=1, source_target_pairs={{4,6},{8,10},{12,14},{5,7},{9,11},{13,15},{20,22},{24,26},{28,30},... | collective-permute-start | bytes 245768 | tf_op jit(solution)/shard_map/ppermute | solution.py:215
  14.8 10.1 %collective-permute-start.10 = (bf16[32,1280]{1,0:T(8,128)(2,1)S(1)}, bf16[32,1280]{1,0:T(8,128)(2,1)S(1)}, u32[]{:S(2)}, u32[]{:S(2)}) collective-permute-start(bf16[32,1280]{1,0:T(8,128)(2,1)S(1)} %broadcast_select_fusion.2), channel_id=1, source_target_pairs={{4,6},{8,10},{12,14},{5,7},{9,11},{13,15},{20,22},{24,26},{28,30},... | collective-permute-start | bytes 245768 | tf_op jit(solution)/shard_map/ppermute | solution.py:216
  21.1 4.7 %collective-permute-start.7 = (f32[128,128]{1,0:T(8,128)S(1)}, f32[128,128]{1,0:T(8,128)S(1)}, u32[]{:S(2)}, u32[]{:S(2)}) collective-permute-start(f32[128,128]{1,0:T(8,128)S(1)} %get-tuple-element.26.refs_3_), channel_id=1, source_target_pairs={{0,1},{1,0},{2,3},{3,2},{4,5},{5,4},{6,7},{7,6},{8,9},{9,8},{10,11... | collective-permute-start | bytes 196616 | tf_op jit(solution)/shard_map/ppermute | solution.py:238

commit v7 on v6

--- a/solution.py
+++ b/solution.py
@@ -127,32 +127,36 @@
         den_ref[:, a:b] = both[:, HD:]
 
 
-def gather_kernel(near_ref, far_ref, sink_k_ref, next_ref, gains_ref, keys_ref, sums_ref, raw_ref):
+def gather_kernel(near_ref, far_ref, sink_k_ref, next_ref, keys_ref, sums_ref):
     cols = sink_k_ref.shape[1]
     pick = jnp.broadcast_to(near_ref[:1, 2 * cols:2 * cols + 1].astype(F32), (FT, cols)) > 1.5
     second = jnp.full((FT, cols), lax.axis_index("tm"), jnp.int32) == 1
-    raw_ref[:FT, :] = near_ref[:FT, :cols]
-    raw_ref[FT:2 * FT, :] = jnp.where(pick, near_ref[FT:, :cols], far_ref[:, :cols])
-    raw_ref[2 * FT:, :] = jnp.where(second, next_ref[:, :cols], sink_k_ref[...])
-    sums_ref[...] = jnp.zeros_like(sums_ref)
-    sums_ref[:3 * FT, :] = jnp.broadcast_to(square_sums(raw_ref), (3 * FT, LANES))
-    keys_ref[...] = (raw_ref[...].astype(F32) * gains_ref[1:2, :]).astype(BF16)
-
-
-def score_kernel(q_ref, keys_ref, score_ref):
+    keys_ref[:FT, :] = near_ref[:FT, :cols]
+    keys_ref[FT:2 * FT, :] = jnp.where(pick, near_ref[FT:, :cols], far_ref[:, :cols])
+    keys_ref[2 * FT:, :] = jnp.where(second, next_ref[:, :cols], sink_k_ref[...])
+    sums = jnp.broadcast_to(square_sums(keys_ref), (3 * FT, LANES))
+    square = jnp.concatenate([sums, jnp.zeros((LANES - 3 * FT, LANES), F32)], 0)
+    sums_ref[...] = jnp.transpose(square)[:8, :]
+
+
+def score_kernel(q_ref, keys_ref, gains_ref, score_ref, high_ref, low_ref):
+    scaled = keys_ref[...].astype(F32) * gains_ref[1:2, :]
+    high_ref[...] = scaled.astype(BF16)
+    low_ref[...] = (scaled - high_ref[...].astype(F32)).astype(BF16)
     for i in range(q_ref.shape[1] // HD):
         a, b = i * HD, (i + 1) * HD
         score_ref[i] = lax.dot_general(
-            q_ref[:, a:b], keys_ref[:, a:b], (((1,), (1,)), ((), ())), preferred_element_type=F32
+            jnp.concatenate([q_ref[:, a:b], q_ref[:, a:b]], 1), jnp.concatenate([high_ref[:, a:b], low_ref[:, a:b]], 1),
+            (((1,), (1,)), ((), ())), preferred_element_type=F32,
         )
 
 
 def finish_kernel(full_width, frames_ref, ctl_ref, score_ref, mine_ref, other_ref, sink_v_ref, next_ref,
-                  near_ref, far_ref, acc_ref, top_ref, den_ref, out_ref, weight_ref, keep_ref):
+                  near_ref, far_ref, acc_ref, top_ref, den_ref, out_hbm, weight_ref, keep_ref, out_ref, sem):
     rows, cols = out_ref.shape
     span = 3 * FT
     factor = lax.rsqrt((mine_ref[...] + other_ref[...]) / full_width + EPSILON) * (1.0 / math.sqrt(HD))
-    factor = jnp.broadcast_to(jnp.transpose(factor)[:1, :span], (rows, span))
+    factor = jnp.broadcast_to(factor[:1, :span], (rows, span))
     heads = [(i, i * HD, (i + 1) * HD) for i in range(cols // HD)]
     sink = ctl_ref[:1, :1]
     window = ctl_ref[1:2, :1]
@@ -172,6 +176,11 @@
         top = jnp.maximum(old, jnp.max(score, axis=1, keepdims=True))
         keep_ref[i] = jnp.exp(old - top)
         weight_ref[i] = jnp.exp(score - top[:, :span]).astype(BF16)
+    half = (len(heads) + 1) // 2
+    copies = [
+        pltpu.make_async_copy(out_ref.at[:, a:b], out_hbm.at[:, a:b], sem.at[n])
+        for n, (a, b) in enumerate(((0, half * HD), (half * HD, cols))) if a < b
+    ]
     for i, a, b in heads:
         c, d = cols + a, cols + b
         before = jnp.where(pick, near_ref[FT:, c:d], far_ref[:, c:d])
@@ -181,6 +190,12 @@
         keep = keep_ref[i]
         blended = (acc_ref[:, a:b] * keep + both[:, :HD]) / (den_ref[:, a:b] * keep + both[:, HD:])
         out_ref[:, a:b] = jnp.where(live, blended, 0.0).astype(BF16)
+        if i == half - 1:
+            copies[0].start()
+    for copy in copies[1:]:
+        copy.start()
+    for copy in copies:
+        copy.wait()
 
 
 def local(queries, keys, values, q_gain, k_gain, frames, flags):
@@ -231,19 +246,21 @@
             pltpu.SemaphoreType.DMA((3,)),
         ],
     )
-    keys, mine = call(
-        gather_kernel, (shape((3 * FT, cols), BF16), shape((LANES, LANES), F32)),
-        (near, far, sink_k, both, gains), scratch=[pltpu.VMEM((3 * FT, cols), BF16)],
-    )
+    keys, mine = call(gather_kernel, (shape((3 * FT, cols), BF16), shape((8, LANES), F32)), (near, far, sink_k, both))
     other = lax.ppermute(mine, "head", swap)
-    score = call(score_kernel, shape((cols // HD, rows, 3 * FT), F32), (qn, keys))
+    score = call(
+        score_kernel, shape((cols // HD, rows, 3 * FT), F32), (qn, keys, gains),
+        scratch=[pltpu.VMEM((3 * FT, cols), BF16)] * 2,
+    )
     return call(
         lambda *refs: finish_kernel(full_width, *refs), block,
         (frames, ctl, score, mine, other, sink_v, both, near, far, acc, top, den),
         specs=[SMEM] + [VMEM] * 11,
         scratch=[
             pltpu.VMEM((cols // HD, rows, 3 * FT), BF16), pltpu.VMEM((cols // HD, rows, HD), F32),
+            pltpu.VMEM((rows, cols), BF16), pltpu.SemaphoreType.DMA((2,)),
         ],
+        out_specs=HBM,
     )
 
 

time: 27.4 us -> 28.8 us (1.051)
  waiting for transfers between devices: 5.41 us -> 6.65 us
  starting transfers between devices: 16.9 us -> 17.2 us
    ppermute x3, waiting for transfers between devices: 4.76 us -> 6.14 us  [local(): came_k = lax.ppermute(sink_k, 'tm', pairs)]
    ppermute x1, starting transfers between devices: 3.18 us -> 3.61 us  [local(): near = lax.ppermute(near, 'tm', [(i, i + 1) for i in range(count - 1)])]
    ppermute x1, starting transfers between devices: 3.2 us -> 2.77 us  [local(): far = lax.ppermute(far, 'tm', [(i, i + 2) for i in range(count - 2)])]
where the time goes in v7:
time: 28.8 us; the launch traced here: 28.5 us
  starting transfers between devices  17.2 us (60%)
  waiting for transfers between devices  6.65 us (23%)
  Pallas kernels  3.42 us (12%)
  between operations  0.92 us (3%)
    ppermute x3, waiting for transfers between devices, local(): came_k = lax.ppermute(sink_k, 'tm', pairs)  6.14 us
    ppermute x2, starting transfers between devices, local(): other = lax.ppermute(mine, 'head', swap)  4.76 us
    ppermute x1, starting transfers between devices, local(): near = lax.ppermute(near, 'tm', [(i, i + 1) for i in range(count - 1)])  3.61 us
    pallas_call x7, Pallas kernels, call(): pl.pallas_call(kernel, out_shape=shapes, in_specs=[VMEM] * len(operands)...  3.42 us
    ppermute x1, starting transfers between devices, local(): far = lax.ppermute(far, 'tm', [(i, i + 2) for i in range(count - 2)])  2.77 us
    ppermute x3, starting transfers between devices, local(): came_k = lax.ppermute(sink_k, 'tm', pairs)  2.76 us
    ppermute x3, starting transfers between devices, local(): came_v = lax.ppermute(sink_v, 'tm', pairs)  2.62 us
    ppermute x1, starting transfers between devices, local(): both = lax.ppermute(both, 'tm', [(0, 1)])  0.67 us
  transfers between devices with their start and end apart: 11, of which 2 were waited for; matrix products, arithmetic and copies ran while one was open for 0% of the time, Pallas kernels for 8%

profile of v7, /device:TPU:15, one launch (start us, length us, event | category | flops | bytes accessed | tf_op | source)
XLA Modules:
  0.0 28.5 jit_solution(15516503494623144601)
XLA Ops:
  0.0 0.0 copy-start
  0.0 0.0 copy-start.2
  0.0 0.0 copy-start.1
  0.0 0.8 %collective-permute-start.3 = (bf16[32,1280]{1,0:T(8,128)(2,1)S(1)}, bf16[32,1280]{1,0:T(8,128)(2,1)S(1)}, u32[]{:S(2)}, u32[]{:S(2)}) collective-permute-start(bf16[32,1280]{1,0:T(8,128)(2,1)S(1)} %get-tuple-element.22), channel_id=1, source_target_pairs={{0,8},{1,9},{16,24},{17,25}} | collective-permute-start | bytes 245768 | tf_op jit(solution)/shard_map/ppermute | solution.py:230
  0.8 0.1 copy-done
  0.9 0.1 copy-done.2
  1.1 0.2 shard_map.73.refs_7_
  1.2 0.7 %collective-permute-start = (f32[96,128]{1,0:T(8,128)S(1)}, f32[96,128]{1,0:T(8,128)S(1)}, u32[]{:S(2)}, u32[]{:S(2)}) collective-permute-start(f32[96,128]{1,0:T(8,128)S(1)} %shard_map.73.refs_7_), channel_id=1, source_target_pairs={{0,1},{1,0},{2,3},{3,2},{4,5},{5,4},{6,7},{7,6},{8,9},{9,8},{10,11... | collective-permute-start | bytes 147464 | tf_op jit(solution)/shard_map/ppermute | solution.py:236
  2.6 0.0 copy-done.1
  2.7 3.6 %collective-permute-start.1 = (bf16[64,2688]{1,0:T(8,128)(2,1)S(1)}, bf16[64,2688]{1,0:T(8,128)(2,1)S(1)}, u32[]{:S(2)}, u32[]{:S(2)}) collective-permute-start(bf16[64,2688]{1,0:T(8,128)(2,1)S(1)} %get-tuple-element.20), channel_id=1, source_target_pairs={{0,2},{2,4},{4,6},{6,8},{8,10},{10,12},{12,14},{1,3},{3,5},{5,7},{... | collective-permute-start | bytes 1032200 | tf_op jit(solution)/shard_map/ppermute | solution.py:224
  6.3 2.8 %collective-permute-start.2 = (bf16[32,2688]{1,0:T(8,128)(2,1)S(1)}, bf16[32,2688]{1,0:T(8,128)(2,1)S(1)}, u32[]{:S(2)}, u32[]{:S(2)}) collective-permute-start(bf16[32,2688]{1,0:T(8,128)(2,1)S(1)} %get-tuple-element.21), channel_id=1, source_target_pairs={{0,4},{2,6},{4,8},{6,10},{8,12},{10,14},{1,5},{3,7},{5,9},{7,11},{... | collective-permute-start | bytes 516104 | tf_op jit(solution)/shard_map/ppermute | solution.py:225
  9.1 0.7 %collective-permute-start.6 = (bf16[32,2560]{1,0:T(8,128)(2,1)S(1)}, bf16[32,2560]{1,0:T(8,128)(2,1)S(1)}, u32[]{:S(2)}, u32[]{:S(2)}) collective-permute-start(bf16[32,2560]{1,0:T(8,128)(2,1)S(1)} %get-tuple-element.23), channel_id=1, source_target_pairs={{0,2},{1,3},{16,18},{17,19}} | collective-permute-start | bytes 491528 | tf_op jit(solution)/shard_map/ppermute | solution.py:226
  9.8 0.0 collective-permute-done.refs_8_
  9.8 0.7 %collective-permute-start.8 = (bf16[32,1280]{1,0:T(8,128)(2,1)S(1)}, bf16[32,1280]{1,0:T(8,128)(2,1)S(1)}, u32[]{:S(2)}, u32[]{:S(2)}) collective-permute-start(bf16[32,1280]{1,0:T(8,128)(2,1)S(1)} %get-tuple-element.27), channel_id=1, source_target_pairs={{0,8},{1,9},{16,24},{17,25}} | collective-permute-start | bytes 245768 | tf_op jit(solution)/shard_map/ppermute | solution.py:231
  10.5 1.6 %shard_map.74 = (f32[8,128]{1,0:T(8,128)S(1)}, f32[8,1280]{1,0:T(8,128)S(1)}, bf16[96,1280]{1,0:T(8,128)(2,1)S(1)}, f32[96,1280]{1,0:T(8,128)S(1)}, f32[96,1280]{1,0:T(8,128)S(1)}, /*index=5*/f32[96,1280]{1,0:T(8,128)S(1)}) custom-call(s32[1]{0:T(128)S(6)} %copy.8.refs_0_.frames_ref, s32[1,2]{1,0:T(1,128)} %refs_1_.1, bf16[96,1280]{1,0:T(8,128)(2,1)S(1)} %copy-done.2, ...), custom_call_target="tpu_custom_call" | custom-call | tf_op jit(solution)/shard_map/pallas_call | solution.py:38
  12.1 0.0 collective-permute-done.3
  12.1 0.7 %collective-permute-start.4 = (bf16[32,1280]{1,0:T(8,128)(2,1)S(1)}, bf16[32,1280]{1,0:T(8,128)(2,1)S(1)}, u32[]{:S(2)}, u32[]{:S(2)}) collective-permute-start(bf16[32,1280]{1,0:T(8,128)(2,1)S(1)} %broadcast_select_fusion.1), channel_id=1, source_target_pairs={{0,4},{8,12},{1,5},{9,13},{16,20},{24,28},{17,21},{25,29}} | collective-permute-start | bytes 245768 | tf_op jit(solution)/shard_map/ppermute | solution.py:230
  12.8 0.0 collective-permute-done.8
  12.8 0.7 %collective-permute-start.9 = (bf16[32,1280]{1,0:T(8,128)(2,1)S(1)}, bf16[32,1280]{1,0:T(8,128)(2,1)S(1)}, u32[]{:S(2)}, u32[]{:S(2)}) collective-permute-start(bf16[32,1280]{1,0:T(8,128)(2,1)S(1)} %broadcast_select_fusion), channel_id=1, source_target_pairs={{0,4},{8,12},{1,5},{9,13},{16,20},{24,28},{17,21},{25,29}} | collective-permute-start | bytes 245768 | tf_op jit(solution)/shard_map/ppermute | solution.py:231
  13.5 0.0 collective-permute-done.4
  13.5 1.3 %collective-permute-start.5 = (bf16[32,1280]{1,0:T(8,128)(2,1)S(1)}, bf16[32,1280]{1,0:T(8,128)(2,1)S(1)}, u32[]{:S(2)}, u32[]{:S(2)}) collective-permute-start(bf16[32,1280]{1,0:T(8,128)(2,1)S(1)} %broadcast_select_fusion.3), channel_id=1, source_target_pairs={{4,6},{8,10},{12,14},{5,7},{9,11},{13,15},{20,22},{24,26},{28,30},... | collective-permute-start | bytes 245768 | tf_op jit(solution)/shard_map/ppermute | solution.py:230
  14.8 0.0 collective-permute-done.9
  14.8 1.3 %collective-permute-start.10 = (bf16[32,1280]{1,0:T(8,128)(2,1)S(1)}, bf16[32,1280]{1,0:T(8,128)(2,1)S(1)}, u32[]{:S(2)}, u32[]{:S(2)}) collective-permute-start(bf16[32,1280]{1,0:T(8,128)(2,1)S(1)} %broadcast_select_fusion.2), channel_id=1, source_target_pairs={{4,6},{8,10},{12,14},{5,7},{9,11},{13,15},{20,22},{24,26},{28,30},... | collective-permute-start | bytes 245768 | tf_op jit(solution)/shard_map/ppermute | solution.py:231
  16.1 6.1 %collective-permute-done.5 = bf16[32,1280]{1,0:T(8,128)(2,1)S(1)} collective-permute-done((bf16[32,1280]{1,0:T(8,128)(2,1)S(1)}, bf16[32,1280]{1,0:T(8,128)(2,1)S(1)}, u32[]{:S(2)}, u32[]{:S(2)}) %collective-permute-start.5) | collective-permute-done | bytes 81952 | tf_op jit(solution)/shard_map/ppermute | solution.py:230
  22.3 0.0 collective-permute-done.6.next_ref.refs_6_
  22.3 0.0 collective-permute-done.2.far_ref.refs_8_
  22.3 0.0 collective-permute-done.1.near_ref.refs_7_
  22.3 0.2 shard_map.77
  22.5 4.0 %collective-permute-start.7 = (f32[8,128]{1,0:T(8,128)S(1)}, f32[8,128]{1,0:T(8,128)S(1)}, u32[]{:S(2)}, u32[]{:S(2)}) collective-permute-start(f32[8,128]{1,0:T(8,128)S(1)} %get-tuple-element.26.refs_3_), channel_id=1, source_target_pairs={{0,1},{1,0},{2,3},{3,2},{4,5},{5,4},{6,7},{7,6},{8,9},{9,8},{10,11... | collective-permute-start | bytes 12296 | tf_op jit(solution)/shard_map/ppermute | solution.py:250
  26.5 0.0 collective-permute-done.10
  26.5 0.3 %shard_map.78.refs_2_ = f32[10,96,96]{2,1,0:T(8,128)S(1)} custom-call(bf16[96,1280]{1,0:T(8,128)(2,1)S(1)} %get-tuple-element.19.q_ref, bf16[96,1280]{1,0:T(8,128)(2,1)S(1)} %get-tuple-element.24.keys_ref, f32[8,1280]{1,0:T(8,128)S(1)} %get-tuple-element.25.gains_ref), custom_call_target="tpu_custom_call" | custom-call | tf_op jit(solution)/shard_map/pallas_call | solution.py:38
  26.8 0.5 %collective-permute-done.7.refs_4_ = f32[8,128]{1,0:T(8,128)S(1)} collective-permute-done((f32[8,128]{1,0:T(8,128)S(1)}, f32[8,128]{1,0:T(8,128)S(1)}, u32[]{:S(2)}, u32[]{:S(2)}) %collective-permute-start.7) | collective-permute-done | bytes 4128 | tf_op jit(solution)/shard_map/ppermute | solution.py:250
  27.3 1.1 %shard_map.79 = bf16[96,1280]{1,0:T(8,128)(2,1)} custom-call(s32[1]{0:T(128)S(6)} %copy.8.refs_0_.frames_ref, f32[8,128]{1,0:T(8,128)S(1)} %get-tuple-element.18.refs_1_, f32[10,96,96]{2,1,0:T(8,128)S(1)} %shard_map.78.refs_2_, f32[8,128]{1,0:T(8,128)S(1)} %get-tuple-element.26.refs_3_, f32[8,128]{1,0:T(8,128)S(1)} %collective-permute-done.7.refs_4_, ...), custom_call_target="tpu_custom_call" | custom-call | tf_op jit(solution)/shard_map/pallas_call | solution.py:38
  (8 shorter events, 0.1 us)
Async XLA Ops:
  0.0 0.9 %copy-start = (bf16[96,1280]{1,0:T(8,128)(2,1)S(1)}, bf16[96,1280]{1,0:T(8,128)(2,1)}, u32[]{:S(2)}) copy-start(bf16[96,1280]{1,0:T(8,128)(2,1)} %k_hbm.1) | copy-start | bytes 737284
  0.0 1.1 %copy-start.2 = (bf16[96,1280]{1,0:T(8,128)(2,1)S(1)}, bf16[96,1280]{1,0:T(8,128)(2,1)}, u32[]{:S(2)}) copy-start(bf16[96,1280]{1,0:T(8,128)(2,1)} %refs_2_.1) | copy-start | bytes 737284
  0.0 2.6 %copy-start.1 = (bf16[96,1280]{1,0:T(8,128)(2,1)S(1)}, bf16[96,1280]{1,0:T(8,128)(2,1)}, u32[]{:S(2)}) copy-start(bf16[96,1280]{1,0:T(8,128)(2,1)} %v_hbm.1) | copy-start | bytes 737284
  0.0 12.0 %collective-permute-start.3 = (bf16[32,1280]{1,0:T(8,128)(2,1)S(1)}, bf16[32,1280]{1,0:T(8,128)(2,1)S(1)}, u32[]{:S(2)}, u32[]{:S(2)}) collective-permute-start(bf16[32,1280]{1,0:T(8,128)(2,1)S(1)} %get-tuple-element.22), channel_id=1, source_target_pairs={{0,8},{1,9},{16,24},{17,25}} | collective-permute-start | bytes 245768 | tf_op jit(solution)/shard_map/ppermute | solution.py:230
  1.2 8.6 %collective-permute-start = (f32[96,128]{1,0:T(8,128)S(1)}, f32[96,128]{1,0:T(8,128)S(1)}, u32[]{:S(2)}, u32[]{:S(2)}) collective-permute-start(f32[96,128]{1,0:T(8,128)S(1)} %shard_map.73.refs_7_), channel_id=1, source_target_pairs={{0,1},{1,0},{2,3},{3,2},{4,5},{5,4},{6,7},{7,6},{8,9},{9,8},{10,11... | collective-permute-start | bytes 147464 | tf_op jit(solution)/shard_map/ppermute | solution.py:236
  2.7 19.6 %collective-permute-start.1 = (bf16[64,2688]{1,0:T(8,128)(2,1)S(1)}, bf16[64,2688]{1,0:T(8,128)(2,1)S(1)}, u32[]{:S(2)}, u32[]{:S(2)}) collective-permute-start(bf16[64,2688]{1,0:T(8,128)(2,1)S(1)} %get-tuple-element.20), channel_id=1, source_target_pairs={{0,2},{2,4},{4,6},{6,8},{8,10},{10,12},{12,14},{1,3},{3,5},{5,7},{... | collective-permute-start | bytes 1032200 | tf_op jit(solution)/shard_map/ppermute | solution.py:224
  6.3 16.0 %collective-permute-start.2 = (bf16[32,2688]{1,0:T(8,128)(2,1)S(1)}, bf16[32,2688]{1,0:T(8,128)(2,1)S(1)}, u32[]{:S(2)}, u32[]{:S(2)}) collective-permute-start(bf16[32,2688]{1,0:T(8,128)(2,1)S(1)} %get-tuple-element.21), channel_id=1, source_target_pairs={{0,4},{2,6},{4,8},{6,10},{8,12},{10,14},{1,5},{3,7},{5,9},{7,11},{... | collective-permute-start | bytes 516104 | tf_op jit(solution)/shard_map/ppermute | solution.py:225
  9.1 13.2 %collective-permute-start.6 = (bf16[32,2560]{1,0:T(8,128)(2,1)S(1)}, bf16[32,2560]{1,0:T(8,128)(2,1)S(1)}, u32[]{:S(2)}, u32[]{:S(2)}) collective-permute-start(bf16[32,2560]{1,0:T(8,128)(2,1)S(1)} %get-tuple-element.23), channel_id=1, source_target_pairs={{0,2},{1,3},{16,18},{17,19}} | collective-permute-start | bytes 491528 | tf_op jit(solution)/shard_map/ppermute | solution.py:226
  9.8 3.0 %collective-permute-start.8 = (bf16[32,1280]{1,0:T(8,128)(2,1)S(1)}, bf16[32,1280]{1,0:T(8,128)(2,1)S(1)}, u32[]{:S(2)}, u32[]{:S(2)}) collective-permute-start(bf16[32,1280]{1,0:T(8,128)(2,1)S(1)} %get-tuple-element.27), channel_id=1, source_target_pairs={{0,8},{1,9},{16,24},{17,25}} | collective-permute-start | bytes 245768 | tf_op jit(solution)/shard_map/ppermute | solution.py:231
  12.1 1.4 %collective-permute-start.4 = (bf16[32,1280]{1,0:T(8,128)(2,1)S(1)}, bf16[32,1280]{1,0:T(8,128)(2,1)S(1)}, u32[]{:S(2)}, u32[]{:S(2)}) collective-permute-start(bf16[32,1280]{1,0:T(8,128)(2,1)S(1)} %broadcast_select_fusion.1), channel_id=1, source_target_pairs={{0,4},{8,12},{1,5},{9,13},{16,20},{24,28},{17,21},{25,29}} | collective-permute-start | bytes 245768 | tf_op jit(solution)/shard_map/ppermute | solution.py:230
  12.8 2.0 %collective-permute-start.9 = (bf16[32,1280]{1,0:T(8,128)(2,1)S(1)}, bf16[32,1280]{1,0:T(8,128)(2,1)S(1)}, u32[]{:S(2)}, u32[]{:S(2)}) collective-permute-start(bf16[32,1280]{1,0:T(8,128)(2,1)S(1)} %broadcast_select_fusion), channel_id=1, source_target_pairs={{0,4},{8,12},{1,5},{9,13},{16,20},{24,28},{17,21},{25,29}} | collective-permute-start | bytes 245768 | tf_op jit(solution)/shard_map/ppermute | solution.py:231
  13.5 8.8 %collective-permute-start.5 = (bf16[32,1280]{1,0:T(8,128)(2,1)S(1)}, bf16[32,1280]{1,0:T(8,128)(2,1)S(1)}, u32[]{:S(2)}, u32[]{:S(2)}) collective-permute-start(bf16[32,1280]{1,0:T(8,128)(2,1)S(1)} %broadcast_select_fusion.3), channel_id=1, source_target_pairs={{4,6},{8,10},{12,14},{5,7},{9,11},{13,15},{20,22},{24,26},{28,30},... | collective-permute-start | bytes 245768 | tf_op jit(solution)/shard_map/ppermute | solution.py:230
  14.8 11.7 %collective-permute-start.10 = (bf16[32,1280]{1,0:T(8,128)(2,1)S(1)}, bf16[32,1280]{1,0:T(8,128)(2,1)S(1)}, u32[]{:S(2)}, u32[]{:S(2)}) collective-permute-start(bf16[32,1280]{1,0:T(8,128)(2,1)S(1)} %broadcast_select_fusion.2), channel_id=1, source_target_pairs={{4,6},{8,10},{12,14},{5,7},{9,11},{13,15},{20,22},{24,26},{28,30},... | collective-permute-start | bytes 245768 | tf_op jit(solution)/shard_map/ppermute | solution.py:231
  22.5 4.8 %collective-permute-start.7 = (f32[8,128]{1,0:T(8,128)S(1)}, f32[8,128]{1,0:T(8,128)S(1)}, u32[]{:S(2)}, u32[]{:S(2)}) collective-permute-start(f32[8,128]{1,0:T(8,128)S(1)} %get-tuple-element.26.refs_3_), channel_id=1, source_target_pairs={{0,1},{1,0},{2,3},{3,2},{4,5},{5,4},{6,7},{7,6},{8,9},{9,8},{10,11... | collective-permute-start | bytes 12296 | tf_op jit(solution)/shard_map/ppermute | solution.py:250

commit v8 on v7

--- a/solution.py
+++ b/solution.py
@@ -12,6 +12,7 @@
 FT = 32
 EPSILON = 1e-06
 LANES = 128
+MISSING = 4096.0
 VMEM = pl.BlockSpec(memory_space=pltpu.VMEM)
 HBM = pl.BlockSpec(memory_space=pltpu.HBM)
 SMEM = pl.BlockSpec(memory_space=pltpu.SMEM)
@@ -64,7 +65,6 @@
     rows, cols = k_ref.shape
     count = jnp.full((1, 1), frames_ref[0].astype(F32))
     counts = jnp.broadcast_to(count, (FT, cols))
-    mark = jnp.broadcast_to(count, (FT, LANES)).astype(BF16)
     for ref, at in ((k_ref, 0), (v_ref, cols)):
         last, before = ref[:FT, :], ref[:FT, :]
         for frame in range(1, rows // FT):
@@ -74,9 +74,7 @@
         near_ref[:FT, at:at + cols] = last
         near_ref[FT:, at:at + cols] = before
         far_ref[:, at:at + cols] = last
-    near_ref[:FT, 2 * cols:] = mark
-    near_ref[FT:, 2 * cols:] = mark
-    far_ref[:, 2 * cols:] = mark
+    near_ref[FT:, :cols] = jnp.where(counts > 1.5, near_ref[FT:, :cols], jnp.full((FT, cols), MISSING, BF16))
 
 
 def square_sums(ref):
@@ -129,7 +127,7 @@
 
 def gather_kernel(near_ref, far_ref, sink_k_ref, next_ref, keys_ref, sums_ref):
     cols = sink_k_ref.shape[1]
-    pick = jnp.broadcast_to(near_ref[:1, 2 * cols:2 * cols + 1].astype(F32), (FT, cols)) > 1.5
+    pick = jnp.broadcast_to(near_ref[FT:FT + 1, :1].astype(F32), (FT, cols)) < MISSING / 2
     second = jnp.full((FT, cols), lax.axis_index("tm"), jnp.int32) == 1
     keys_ref[:FT, :] = near_ref[:FT, :cols]
     keys_ref[FT:2 * FT, :] = jnp.where(pick, near_ref[FT:, :cols], far_ref[:, :cols])
@@ -160,15 +158,16 @@
     heads = [(i, i * HD, (i + 1) * HD) for i in range(cols // HD)]
     sink = ctl_ref[:1, :1]
     window = ctl_ref[1:2, :1]
-    near_mark = near_ref[:1, 2 * cols:2 * cols + 1].astype(F32)
-    far_mark = far_ref[:1, 2 * cols:2 * cols + 1].astype(F32)
-    has_before = jnp.where(near_mark > 1.5, near_mark, far_mark) * window
+    here = lax.axis_index("tm")
+    two = near_ref[FT:FT + 1, :1].astype(F32)
+    has_last = jnp.where(jnp.full((1, 1), here, jnp.int32) > 0, window, 0.0)
+    has_before = jnp.where((two < MISSING / 2) | (jnp.full((1, 1), here, jnp.int32) > 1), has_last, 0.0)
     slot = lax.broadcasted_iota(jnp.int32, (rows, span), 1)
-    allow = jnp.where(slot < FT, near_mark * window, jnp.where(slot < 2 * FT, has_before, sink))
+    allow = jnp.where(slot < FT, has_last, jnp.where(slot < 2 * FT, has_before, sink))
     allowed = allow > 0.5
     live = lax.broadcasted_iota(jnp.int32, (rows, HD), 0) < frames_ref[0] * FT
-    pick = jnp.broadcast_to(near_mark, (FT, HD)) > 1.5
-    second = jnp.full((FT, HD), lax.axis_index("tm"), jnp.int32) == 1
+    pick = jnp.broadcast_to(two, (FT, HD)) < MISSING / 2
+    second = jnp.full((FT, HD), here, jnp.int32) == 1
     ones = jnp.ones((span, HD), BF16)
     for i, a, b in heads:
         score = jnp.where(allowed, score_ref[i] * factor, -jnp.inf)
@@ -218,7 +217,7 @@
     )
     near, far = call(
         pack_kernel,
-        (shape((2 * FT, 2 * cols + LANES), BF16), shape((FT, 2 * cols + LANES), BF16)),
+        (shape((2 * FT, 2 * cols), BF16), shape((FT, 2 * cols), BF16)),
         (frames, keys, values), specs=[SMEM, VMEM, VMEM],
     )
     near = lax.ppermute(near, "tm", [(i, i + 1) for i in range(count - 1)])

time: 28.8 us -> 28.8 us (level)
  the two profiles are of different devices: /device:TPU:15 before, /device:TPU:11 now
where the time goes in v8:
time: 28.8 us; the launch traced here: 28.5 us
  starting transfers between devices  17.2 us (60%)
  waiting for transfers between devices  6.65 us (23%)
  Pallas kernels  3.44 us (12%)
  between operations  0.91 us (3%)
    ppermute x3, waiting for transfers between devices, local(): came_k = lax.ppermute(sink_k, 'tm', pairs)  6.14 us
    ppermute x2, starting transfers between devices, local(): other = lax.ppermute(mine, 'head', swap)  4.76 us
    ppermute x1, starting transfers between devices, local(): near = lax.ppermute(near, 'tm', [(i, i + 1) for i in range(count - 1)])  3.61 us
    pallas_call x7, Pallas kernels, call(): pl.pallas_call(kernel, out_shape=shapes, in_specs=[VMEM] * len(operands)...  3.44 us
    ppermute x1, starting transfers between devices, local(): far = lax.ppermute(far, 'tm', [(i, i + 2) for i in range(count - 2)])  2.77 us
    ppermute x3, starting transfers between devices, local(): came_k = lax.ppermute(sink_k, 'tm', pairs)  2.76 us
    ppermute x3, starting transfers between devices, local(): came_v = lax.ppermute(sink_v, 'tm', pairs)  2.62 us
    ppermute x1, starting transfers between devices, local(): both = lax.ppermute(both, 'tm', [(0, 1)])  0.67 us
  transfers between devices with their start and end apart: 11, of which 2 were waited for; matrix products, arithmetic and copies ran while one was open for 0% of the time, Pallas kernels for 8%

profile of v8, /device:TPU:11, one launch (start us, length us, event | category | flops | bytes accessed | tf_op | source)
XLA Modules:
  0.0 28.5 jit_solution(13843665923713543569)
XLA Ops:
  0.0 0.0 copy-start
  0.0 0.0 copy-start.2
  0.0 0.0 copy-start.1
  0.0 0.8 %collective-permute-start.3 = (bf16[32,1280]{1,0:T(8,128)(2,1)S(1)}, bf16[32,1280]{1,0:T(8,128)(2,1)S(1)}, u32[]{:S(2)}, u32[]{:S(2)}) collective-permute-start(bf16[32,1280]{1,0:T(8,128)(2,1)S(1)} %get-tuple-element.22), channel_id=1, source_target_pairs={{0,8},{1,9},{16,24},{17,25}} | collective-permute-start | bytes 245768 | tf_op jit(solution)/shard_map/ppermute | solution.py:229
  0.8 0.1 copy-done
  0.9 0.1 copy-done.2
  1.1 0.2 shard_map.73.refs_7_
  1.2 0.7 %collective-permute-start = (f32[96,128]{1,0:T(8,128)S(1)}, f32[96,128]{1,0:T(8,128)S(1)}, u32[]{:S(2)}, u32[]{:S(2)}) collective-permute-start(f32[96,128]{1,0:T(8,128)S(1)} %shard_map.73.refs_7_), channel_id=1, source_target_pairs={{0,1},{1,0},{2,3},{3,2},{4,5},{5,4},{6,7},{7,6},{8,9},{9,8},{10,11... | collective-permute-start | bytes 147464 | tf_op jit(solution)/shard_map/ppermute | solution.py:235
  2.6 0.0 copy-done.1
  2.6 0.1 shard_map.75
  2.7 3.6 %collective-permute-start.1 = (bf16[64,2560]{1,0:T(8,128)(2,1)S(1)}, bf16[64,2560]{1,0:T(8,128)(2,1)S(1)}, u32[]{:S(2)}, u32[]{:S(2)}) collective-permute-start(bf16[64,2560]{1,0:T(8,128)(2,1)S(1)} %get-tuple-element.20), channel_id=1, source_target_pairs={{0,2},{2,4},{4,6},{6,8},{8,10},{10,12},{12,14},{1,3},{3,5},{5,7},{... | collective-permute-start | bytes 983048 | tf_op jit(solution)/shard_map/ppermute | solution.py:223
  6.3 2.8 %collective-permute-start.2 = (bf16[32,2560]{1,0:T(8,128)(2,1)S(1)}, bf16[32,2560]{1,0:T(8,128)(2,1)S(1)}, u32[]{:S(2)}, u32[]{:S(2)}) collective-permute-start(bf16[32,2560]{1,0:T(8,128)(2,1)S(1)} %get-tuple-element.21), channel_id=1, source_target_pairs={{0,4},{2,6},{4,8},{6,10},{8,12},{10,14},{1,5},{3,7},{5,9},{7,11},{... | collective-permute-start | bytes 491528 | tf_op jit(solution)/shard_map/ppermute | solution.py:224
  9.1 0.7 %collective-permute-start.6 = (bf16[32,2560]{1,0:T(8,128)(2,1)S(1)}, bf16[32,2560]{1,0:T(8,128)(2,1)S(1)}, u32[]{:S(2)}, u32[]{:S(2)}) collective-permute-start(bf16[32,2560]{1,0:T(8,128)(2,1)S(1)} %get-tuple-element.23), channel_id=1, source_target_pairs={{0,2},{1,3},{16,18},{17,19}} | collective-permute-start | bytes 491528 | tf_op jit(solution)/shard_map/ppermute | solution.py:225
  9.8 0.0 collective-permute-done.refs_8_
  9.8 0.7 %collective-permute-start.8 = (bf16[32,1280]{1,0:T(8,128)(2,1)S(1)}, bf16[32,1280]{1,0:T(8,128)(2,1)S(1)}, u32[]{:S(2)}, u32[]{:S(2)}) collective-permute-start(bf16[32,1280]{1,0:T(8,128)(2,1)S(1)} %get-tuple-element.27), channel_id=1, source_target_pairs={{0,8},{1,9},{16,24},{17,25}} | collective-permute-start | bytes 245768 | tf_op jit(solution)/shard_map/ppermute | solution.py:230
  10.5 1.6 %shard_map.74 = (f32[8,128]{1,0:T(8,128)S(1)}, f32[8,1280]{1,0:T(8,128)S(1)}, bf16[96,1280]{1,0:T(8,128)(2,1)S(1)}, f32[96,1280]{1,0:T(8,128)S(1)}, f32[96,1280]{1,0:T(8,128)S(1)}, /*index=5*/f32[96,1280]{1,0:T(8,128)S(1)}) custom-call(s32[1]{0:T(128)S(6)} %copy.8.refs_0_.frames_ref, s32[1,2]{1,0:T(1,128)} %refs_1_.1, bf16[96,1280]{1,0:T(8,128)(2,1)S(1)} %copy-done.2, ...), custom_call_target="tpu_custom_call" | custom-call | tf_op jit(solution)/shard_map/pallas_call | solution.py:39
  12.1 0.0 collective-permute-done.3
  12.1 0.7 %collective-permute-start.4 = (bf16[32,1280]{1,0:T(8,128)(2,1)S(1)}, bf16[32,1280]{1,0:T(8,128)(2,1)S(1)}, u32[]{:S(2)}, u32[]{:S(2)}) collective-permute-start(bf16[32,1280]{1,0:T(8,128)(2,1)S(1)} %broadcast_select_fusion.1), channel_id=1, source_target_pairs={{0,4},{8,12},{1,5},{9,13},{16,20},{24,28},{17,21},{25,29}} | collective-permute-start | bytes 245768 | tf_op jit(solution)/shard_map/ppermute | solution.py:229
  12.8 0.0 collective-permute-done.8
  12.8 0.7 %collective-permute-start.9 = (bf16[32,1280]{1,0:T(8,128)(2,1)S(1)}, bf16[32,1280]{1,0:T(8,128)(2,1)S(1)}, u32[]{:S(2)}, u32[]{:S(2)}) collective-permute-start(bf16[32,1280]{1,0:T(8,128)(2,1)S(1)} %broadcast_select_fusion), channel_id=1, source_target_pairs={{0,4},{8,12},{1,5},{9,13},{16,20},{24,28},{17,21},{25,29}} | collective-permute-start | bytes 245768 | tf_op jit(solution)/shard_map/ppermute | solution.py:230
  13.5 0.0 collective-permute-done.4
  13.5 1.3 %collective-permute-start.5 = (bf16[32,1280]{1,0:T(8,128)(2,1)S(1)}, bf16[32,1280]{1,0:T(8,128)(2,1)S(1)}, u32[]{:S(2)}, u32[]{:S(2)}) collective-permute-start(bf16[32,1280]{1,0:T(8,128)(2,1)S(1)} %broadcast_select_fusion.3), channel_id=1, source_target_pairs={{4,6},{8,10},{12,14},{5,7},{9,11},{13,15},{20,22},{24,26},{28,30},... | collective-permute-start | bytes 245768 | tf_op jit(solution)/shard_map/ppermute | solution.py:229
  14.8 0.0 collective-permute-done.9
  14.9 1.3 %collective-permute-start.10 = (bf16[32,1280]{1,0:T(8,128)(2,1)S(1)}, bf16[32,1280]{1,0:T(8,128)(2,1)S(1)}, u32[]{:S(2)}, u32[]{:S(2)}) collective-permute-start(bf16[32,1280]{1,0:T(8,128)(2,1)S(1)} %broadcast_select_fusion.2), channel_id=1, source_target_pairs={{4,6},{8,10},{12,14},{5,7},{9,11},{13,15},{20,22},{24,26},{28,30},... | collective-permute-start | bytes 245768 | tf_op jit(solution)/shard_map/ppermute | solution.py:230
  16.2 6.1 %collective-permute-done.5 = bf16[32,1280]{1,0:T(8,128)(2,1)S(1)} collective-permute-done((bf16[32,1280]{1,0:T(8,128)(2,1)S(1)}, bf16[32,1280]{1,0:T(8,128)(2,1)S(1)}, u32[]{:S(2)}, u32[]{:S(2)}) %collective-permute-start.5) | collective-permute-done | bytes 81952 | tf_op jit(solution)/shard_map/ppermute | solution.py:229
  22.3 0.0 collective-permute-done.2.far_ref.refs_8_
  22.3 0.0 collective-permute-done.6.next_ref.refs_6_
  22.3 0.0 collective-permute-done.1.near_ref.refs_7_
  22.3 0.2 shard_map.77
  22.5 4.0 %collective-permute-start.7 = (f32[8,128]{1,0:T(8,128)S(1)}, f32[8,128]{1,0:T(8,128)S(1)}, u32[]{:S(2)}, u32[]{:S(2)}) collective-permute-start(f32[8,128]{1,0:T(8,128)S(1)} %get-tuple-element.26.refs_3_), channel_id=1, source_target_pairs={{0,1},{1,0},{2,3},{3,2},{4,5},{5,4},{6,7},{7,6},{8,9},{9,8},{10,11... | collective-permute-start | bytes 12296 | tf_op jit(solution)/shard_map/ppermute | solution.py:249
  26.5 0.0 collective-permute-done.10
  26.5 0.3 %shard_map.78.refs_2_ = f32[10,96,96]{2,1,0:T(8,128)S(1)} custom-call(bf16[96,1280]{1,0:T(8,128)(2,1)S(1)} %get-tuple-element.19.q_ref, bf16[96,1280]{1,0:T(8,128)(2,1)S(1)} %get-tuple-element.24.keys_ref, f32[8,1280]{1,0:T(8,128)S(1)} %get-tuple-element.25.gains_ref), custom_call_target="tpu_custom_call" | custom-call | tf_op jit(solution)/shard_map/pallas_call | solution.py:39
  26.9 0.5 %collective-permute-done.7.refs_4_ = f32[8,128]{1,0:T(8,128)S(1)} collective-permute-done((f32[8,128]{1,0:T(8,128)S(1)}, f32[8,128]{1,0:T(8,128)S(1)}, u32[]{:S(2)}, u32[]{:S(2)}) %collective-permute-start.7) | collective-permute-done | bytes 4128 | tf_op jit(solution)/shard_map/ppermute | solution.py:249
  27.3 1.1 %shard_map.79 = bf16[96,1280]{1,0:T(8,128)(2,1)} custom-call(s32[1]{0:T(128)S(6)} %copy.8.refs_0_.frames_ref, f32[8,128]{1,0:T(8,128)S(1)} %get-tuple-element.18.refs_1_, f32[10,96,96]{2,1,0:T(8,128)S(1)} %shard_map.78.refs_2_, f32[8,128]{1,0:T(8,128)S(1)} %get-tuple-element.26.refs_3_, f32[8,128]{1,0:T(8,128)S(1)} %collective-permute-done.7.refs_4_, ...), custom_call_target="tpu_custom_call" | custom-call | tf_op jit(solution)/shard_map/pallas_call | solution.py:39
  (7 shorter events, 0.1 us)
Async XLA Ops:
  0.0 0.9 %copy-start = (bf16[96,1280]{1,0:T(8,128)(2,1)S(1)}, bf16[96,1280]{1,0:T(8,128)(2,1)}, u32[]{:S(2)}) copy-start(bf16[96,1280]{1,0:T(8,128)(2,1)} %k_hbm.1) | copy-start | bytes 737284
  0.0 1.1 %copy-start.2 = (bf16[96,1280]{1,0:T(8,128)(2,1)S(1)}, bf16[96,1280]{1,0:T(8,128)(2,1)}, u32[]{:S(2)}) copy-start(bf16[96,1280]{1,0:T(8,128)(2,1)} %refs_2_.1) | copy-start | bytes 737284
  0.0 2.6 %copy-start.1 = (bf16[96,1280]{1,0:T(8,128)(2,1)S(1)}, bf16[96,1280]{1,0:T(8,128)(2,1)}, u32[]{:S(2)}) copy-start(bf16[96,1280]{1,0:T(8,128)(2,1)} %v_hbm.1) | copy-start | bytes 737284
  0.0 12.0 %collective-permute-start.3 = (bf16[32,1280]{1,0:T(8,128)(2,1)S(1)}, bf16[32,1280]{1,0:T(8,128)(2,1)S(1)}, u32[]{:S(2)}, u32[]{:S(2)}) collective-permute-start(bf16[32,1280]{1,0:T(8,128)(2,1)S(1)} %get-tuple-element.22), channel_id=1, source_target_pairs={{0,8},{1,9},{16,24},{17,25}} | collective-permute-start | bytes 245768 | tf_op jit(solution)/shard_map/ppermute | solution.py:229
  1.2 8.6 %collective-permute-start = (f32[96,128]{1,0:T(8,128)S(1)}, f32[96,128]{1,0:T(8,128)S(1)}, u32[]{:S(2)}, u32[]{:S(2)}) collective-permute-start(f32[96,128]{1,0:T(8,128)S(1)} %shard_map.73.refs_7_), channel_id=1, source_target_pairs={{0,1},{1,0},{2,3},{3,2},{4,5},{5,4},{6,7},{7,6},{8,9},{9,8},{10,11... | collective-permute-start | bytes 147464 | tf_op jit(solution)/shard_map/ppermute | solution.py:235
  2.7 19.6 %collective-permute-start.1 = (bf16[64,2560]{1,0:T(8,128)(2,1)S(1)}, bf16[64,2560]{1,0:T(8,128)(2,1)S(1)}, u32[]{:S(2)}, u32[]{:S(2)}) collective-permute-start(bf16[64,2560]{1,0:T(8,128)(2,1)S(1)} %get-tuple-element.20), channel_id=1, source_target_pairs={{0,2},{2,4},{4,6},{6,8},{8,10},{10,12},{12,14},{1,3},{3,5},{5,7},{... | collective-permute-start | bytes 983048 | tf_op jit(solution)/shard_map/ppermute | solution.py:223
  6.3 16.0 %collective-permute-start.2 = (bf16[32,2560]{1,0:T(8,128)(2,1)S(1)}, bf16[32,2560]{1,0:T(8,128)(2,1)S(1)}, u32[]{:S(2)}, u32[]{:S(2)}) collective-permute-start(bf16[32,2560]{1,0:T(8,128)(2,1)S(1)} %get-tuple-element.21), channel_id=1, source_target_pairs={{0,4},{2,6},{4,8},{6,10},{8,12},{10,14},{1,5},{3,7},{5,9},{7,11},{... | collective-permute-start | bytes 491528 | tf_op jit(solution)/shard_map/ppermute | solution.py:224
  9.1 13.2 %collective-permute-start.6 = (bf16[32,2560]{1,0:T(8,128)(2,1)S(1)}, bf16[32,2560]{1,0:T(8,128)(2,1)S(1)}, u32[]{:S(2)}, u32[]{:S(2)}) collective-permute-start(bf16[32,2560]{1,0:T(8,128)(2,1)S(1)} %get-tuple-element.23), channel_id=1, source_target_pairs={{0,2},{1,3},{16,18},{17,19}} | collective-permute-start | bytes 491528 | tf_op jit(solution)/shard_map/ppermute | solution.py:225
  9.8 3.0 %collective-permute-start.8 = (bf16[32,1280]{1,0:T(8,128)(2,1)S(1)}, bf16[32,1280]{1,0:T(8,128)(2,1)S(1)}, u32[]{:S(2)}, u32[]{:S(2)}) collective-permute-start(bf16[32,1280]{1,0:T(8,128)(2,1)S(1)} %get-tuple-element.27), channel_id=1, source_target_pairs={{0,8},{1,9},{16,24},{17,25}} | collective-permute-start | bytes 245768 | tf_op jit(solution)/shard_map/ppermute | solution.py:230
  12.1 1.4 %collective-permute-start.4 = (bf16[32,1280]{1,0:T(8,128)(2,1)S(1)}, bf16[32,1280]{1,0:T(8,128)(2,1)S(1)}, u32[]{:S(2)}, u32[]{:S(2)}) collective-permute-start(bf16[32,1280]{1,0:T(8,128)(2,1)S(1)} %broadcast_select_fusion.1), channel_id=1, source_target_pairs={{0,4},{8,12},{1,5},{9,13},{16,20},{24,28},{17,21},{25,29}} | collective-permute-start | bytes 245768 | tf_op jit(solution)/shard_map/ppermute | solution.py:229
  12.8 2.0 %collective-permute-start.9 = (bf16[32,1280]{1,0:T(8,128)(2,1)S(1)}, bf16[32,1280]{1,0:T(8,128)(2,1)S(1)}, u32[]{:S(2)}, u32[]{:S(2)}) collective-permute-start(bf16[32,1280]{1,0:T(8,128)(2,1)S(1)} %broadcast_select_fusion), channel_id=1, source_target_pairs={{0,4},{8,12},{1,5},{9,13},{16,20},{24,28},{17,21},{25,29}} | collective-permute-start | bytes 245768 | tf_op jit(solution)/shard_map/ppermute | solution.py:230
  13.5 8.8 %collective-permute-start.5 = (bf16[32,1280]{1,0:T(8,128)(2,1)S(1)}, bf16[32,1280]{1,0:T(8,128)(2,1)S(1)}, u32[]{:S(2)}, u32[]{:S(2)}) collective-permute-start(bf16[32,1280]{1,0:T(8,128)(2,1)S(1)} %broadcast_select_fusion.3), channel_id=1, source_target_pairs={{4,6},{8,10},{12,14},{5,7},{9,11},{13,15},{20,22},{24,26},{28,30},... | collective-permute-start | bytes 245768 | tf_op jit(solution)/shard_map/ppermute | solution.py:229
  14.9 11.7 %collective-permute-start.10 = (bf16[32,1280]{1,0:T(8,128)(2,1)S(1)}, bf16[32,1280]{1,0:T(8,128)(2,1)S(1)}, u32[]{:S(2)}, u32[]{:S(2)}) collective-permute-start(bf16[32,1280]{1,0:T(8,128)(2,1)S(1)} %broadcast_select_fusion.2), channel_id=1, source_target_pairs={{4,6},{8,10},{12,14},{5,7},{9,11},{13,15},{20,22},{24,26},{28,30},... | collective-permute-start | bytes 245768 | tf_op jit(solution)/shard_map/ppermute | solution.py:230
  22.5 4.8 %collective-permute-start.7 = (f32[8,128]{1,0:T(8,128)S(1)}, f32[8,128]{1,0:T(8,128)S(1)}, u32[]{:S(2)}, u32[]{:S(2)}) collective-permute-start(f32[8,128]{1,0:T(8,128)S(1)} %get-tuple-element.26.refs_3_), channel_id=1, source_target_pairs={{0,1},{1,0},{2,3},{3,2},{4,5},{5,4},{6,7},{7,6},{8,9},{9,8},{10,11... | collective-permute-start | bytes 12296 | tf_op jit(solution)/shard_map/ppermute | solution.py:249

commit v9 on v8

--- a/solution.py
+++ b/solution.py
@@ -125,13 +125,14 @@
         den_ref[:, a:b] = both[:, HD:]
 
 
-def gather_kernel(near_ref, far_ref, sink_k_ref, next_ref, keys_ref, sums_ref):
+def gather_kernel(near_ref, far_ref, sink_k_ref, came_k_ref, next_ref, keys_ref, sums_ref):
     cols = sink_k_ref.shape[1]
     pick = jnp.broadcast_to(near_ref[FT:FT + 1, :1].astype(F32), (FT, cols)) < MISSING / 2
-    second = jnp.full((FT, cols), lax.axis_index("tm"), jnp.int32) == 1
+    here = jnp.full((FT, cols), lax.axis_index("tm"), jnp.int32)
     keys_ref[:FT, :] = near_ref[:FT, :cols]
     keys_ref[FT:2 * FT, :] = jnp.where(pick, near_ref[FT:, :cols], far_ref[:, :cols])
-    keys_ref[2 * FT:, :] = jnp.where(second, next_ref[:, :cols], sink_k_ref[...])
+    came = jnp.where(here == 1, next_ref[:, :cols], came_k_ref[...])
+    keys_ref[2 * FT:, :] = jnp.where(here % 2 == 0, sink_k_ref[...], came)
     sums = jnp.broadcast_to(square_sums(keys_ref), (3 * FT, LANES))
     square = jnp.concatenate([sums, jnp.zeros((LANES - 3 * FT, LANES), F32)], 0)
     sums_ref[...] = jnp.transpose(square)[:8, :]
@@ -149,7 +150,7 @@
         )
 
 
-def finish_kernel(full_width, frames_ref, ctl_ref, score_ref, mine_ref, other_ref, sink_v_ref, next_ref,
+def finish_kernel(full_width, frames_ref, ctl_ref, score_ref, mine_ref, other_ref, sink_v_ref, came_v_ref, next_ref,
                   near_ref, far_ref, acc_ref, top_ref, den_ref, out_hbm, weight_ref, keep_ref, out_ref, sem):
     rows, cols = out_ref.shape
     span = 3 * FT
@@ -167,7 +168,8 @@
     allowed = allow > 0.5
     live = lax.broadcasted_iota(jnp.int32, (rows, HD), 0) < frames_ref[0] * FT
     pick = jnp.broadcast_to(two, (FT, HD)) < MISSING / 2
-    second = jnp.full((FT, HD), here, jnp.int32) == 1
+    place = jnp.full((FT, HD), here, jnp.int32)
+    second, even = place == 1, place % 2 == 0
     ones = jnp.ones((span, HD), BF16)
     for i, a, b in heads:
         score = jnp.where(allowed, score_ref[i] * factor, -jnp.inf)
@@ -183,11 +185,12 @@
     for i, a, b in heads:
         c, d = cols + a, cols + b
         before = jnp.where(pick, near_ref[FT:, c:d], far_ref[:, c:d])
-        first = jnp.where(second, next_ref[:, c:d], sink_v_ref[:, a:b])
+        first = jnp.where(second, next_ref[:, c:d], came_v_ref[:, a:b])
+        first = jnp.where(even, sink_v_ref[:, a:b], first)
         vals = jnp.concatenate([near_ref[:FT, c:d], before, first], 0)
         both = jnp.dot(weight_ref[i], jnp.concatenate([vals, ones], 1), preferred_element_type=F32)
         keep = keep_ref[i]
-        blended = (acc_ref[:, a:b] * keep + both[:, :HD]) / (den_ref[:, a:b] * keep + both[:, HD:])
+        blended = (acc_ref[:, a:b] * keep + both[:, :HD]) * pl.reciprocal(den_ref[:, a:b] * keep + both[:, HD:])
         out_ref[:, a:b] = jnp.where(live, blended, 0.0).astype(BF16)
         if i == half - 1:
             copies[0].start()
@@ -224,13 +227,14 @@
     far = lax.ppermute(far, "tm", [(i, i + 2) for i in range(count - 2)])
     both = lax.ppermute(both, "tm", [(0, 1)])
     rounds = tree_rounds(count)
-    for pairs, period in rounds:
+    for number, (pairs, period) in enumerate(rounds):
         pairs = [pair for pair in pairs if pair != (0, 1)]
         came_k = lax.ppermute(sink_k, "tm", pairs)
         came_v = lax.ppermute(sink_v, "tm", pairs)
-        kept = here % period == 0
-        sink_k = jnp.where(kept, sink_k, came_k)
-        sink_v = jnp.where(kept, sink_v, came_v)
+        if number < len(rounds) - 1:
+            kept = here % period == 0
+            sink_k = jnp.where(kept, sink_k, came_k)
+            sink_v = jnp.where(kept, sink_v, came_v)
     mine = call(sums_kernel, shape((rows, LANES), F32), (queries, keys))
     other = lax.ppermute(mine, "head", swap)
     ctl, gains, qn, acc, top, den = call(
@@ -245,7 +249,9 @@
             pltpu.SemaphoreType.DMA((3,)),
         ],
     )
-    keys, mine = call(gather_kernel, (shape((3 * FT, cols), BF16), shape((8, LANES), F32)), (near, far, sink_k, both))
+    keys, mine = call(
+        gather_kernel, (shape((3 * FT, cols), BF16), shape((8, LANES), F32)), (near, far, sink_k, came_k, both)
+    )
     other = lax.ppermute(mine, "head", swap)
     score = call(
         score_kernel, shape((cols // HD, rows, 3 * FT), F32), (qn, keys, gains),
@@ -253,8 +259,8 @@
     )
     return call(
         lambda *refs: finish_kernel(full_width, *refs), block,
-        (frames, ctl, score, mine, other, sink_v, both, near, far, acc, top, den),
-        specs=[SMEM] + [VMEM] * 11,
+        (frames, ctl, score, mine, other, sink_v, came_v, both, near, far, acc, top, den),
+        specs=[SMEM] + [VMEM] * 12,
         scratch=[
             pltpu.VMEM((cols // HD, rows, 3 * FT), BF16), pltpu.VMEM((cols // HD, rows, HD), F32),
             pltpu.VMEM((rows, cols), BF16), pltpu.SemaphoreType.DMA((2,)),

time: 28.8 us -> 28.1 us (0.976)
  the two profiles are of different devices: /device:TPU:11 before, /device:TPU:25 now
where the time goes in v9:
time: 28.1 us; the launch traced here: 27.8 us
  starting transfers between devices  15.7 us (56%)
  waiting for transfers between devices  7.79 us (28%)
  Pallas kernels  3.43 us (12%)
  between operations  0.89 us (3%)
    ppermute x2, starting transfers between devices, local(): other = lax.ppermute(mine, 'head', swap)  3.82 us
    ppermute x3, waiting for transfers between devices, local(): came_v = lax.ppermute(sink_v, 'tm', pairs)  3.62 us
    ppermute x3, waiting for transfers between devices, local(): came_k = lax.ppermute(sink_k, 'tm', pairs)  3.52 us
    pallas_call x7, Pallas kernels, call(): pl.pallas_call(kernel, out_shape=shapes, in_specs=[VMEM] * len(operands)...  3.43 us
    ppermute x3, starting transfers between devices, local(): came_v = lax.ppermute(sink_v, 'tm', pairs)  3.38 us
    ppermute x3, starting transfers between devices, local(): came_k = lax.ppermute(sink_k, 'tm', pairs)  3.38 us
    ppermute x1, starting transfers between devices, local(): near = lax.ppermute(near, 'tm', [(i, i + 1) for i in range(count - 1)])  3.12 us
    ppermute x1, starting transfers between devices, local(): far = lax.ppermute(far, 'tm', [(i, i + 2) for i in range(count - 2)])  1.29 us
  transfers between devices with their start and end apart: 11, of which 3 were waited for; matrix products, arithmetic and copies ran while one was open for 0% of the time, Pallas kernels for 8%

profile of v9, /device:TPU:25, one launch (start us, length us, event | category | flops | bytes accessed | tf_op | source)
XLA Modules:
  0.0 27.8 jit_solution(8545311882148057309)
XLA Ops:
  0.0 0.0 copy-start
  0.0 0.0 copy-start.1
  0.0 0.8 %collective-permute-start.3 = (bf16[32,1280]{1,0:T(8,128)(2,1)S(1)}, bf16[32,1280]{1,0:T(8,128)(2,1)S(1)}, u32[]{:S(2)}, u32[]{:S(2)}) collective-permute-start(bf16[32,1280]{1,0:T(8,128)(2,1)S(1)} %get-tuple-element.22), channel_id=1, source_target_pairs={{0,8},{1,9},{16,24},{17,25}} | collective-permute-start | bytes 245768 | tf_op jit(solution)/shard_map/ppermute | solution.py:232
  1.5 0.0 copy-done
  1.5 0.0 copy-done.1
  1.5 0.1 shard_map.75
  1.6 3.1 %collective-permute-start.1 = (bf16[64,2560]{1,0:T(8,128)(2,1)S(1)}, bf16[64,2560]{1,0:T(8,128)(2,1)S(1)}, u32[]{:S(2)}, u32[]{:S(2)}) collective-permute-start(bf16[64,2560]{1,0:T(8,128)(2,1)S(1)} %get-tuple-element.20), channel_id=1, source_target_pairs={{0,2},{2,4},{4,6},{6,8},{8,10},{10,12},{12,14},{1,3},{3,5},{5,7},{... | collective-permute-start | bytes 983048 | tf_op jit(solution)/shard_map/ppermute | solution.py:226
  4.7 1.3 %collective-permute-start.2 = (bf16[32,2560]{1,0:T(8,128)(2,1)S(1)}, bf16[32,2560]{1,0:T(8,128)(2,1)S(1)}, u32[]{:S(2)}, u32[]{:S(2)}) collective-permute-start(bf16[32,2560]{1,0:T(8,128)(2,1)S(1)} %get-tuple-element.21), channel_id=1, source_target_pairs={{0,4},{2,6},{4,8},{6,10},{8,12},{10,14},{1,5},{3,7},{5,9},{7,11},{... | collective-permute-start | bytes 491528 | tf_op jit(solution)/shard_map/ppermute | solution.py:227
  6.0 0.7 %collective-permute-start.6 = (bf16[32,2560]{1,0:T(8,128)(2,1)S(1)}, bf16[32,2560]{1,0:T(8,128)(2,1)S(1)}, u32[]{:S(2)}, u32[]{:S(2)}) collective-permute-start(bf16[32,2560]{1,0:T(8,128)(2,1)S(1)} %get-tuple-element.23), channel_id=1, source_target_pairs={{0,2},{1,3},{16,18},{17,19}} | collective-permute-start | bytes 491528 | tf_op jit(solution)/shard_map/ppermute | solution.py:228
  6.7 0.7 %collective-permute-start.8 = (bf16[32,1280]{1,0:T(8,128)(2,1)S(1)}, bf16[32,1280]{1,0:T(8,128)(2,1)S(1)}, u32[]{:S(2)}, u32[]{:S(2)}) collective-permute-start(bf16[32,1280]{1,0:T(8,128)(2,1)S(1)} %get-tuple-element.27), channel_id=1, source_target_pairs={{0,8},{1,9},{16,24},{17,25}} | collective-permute-start | bytes 245768 | tf_op jit(solution)/shard_map/ppermute | solution.py:233
  7.4 0.0 collective-permute-done.3
  7.4 1.3 %collective-permute-start.4 = (bf16[32,1280]{1,0:T(8,128)(2,1)S(1)}, bf16[32,1280]{1,0:T(8,128)(2,1)S(1)}, u32[]{:S(2)}, u32[]{:S(2)}) collective-permute-start(bf16[32,1280]{1,0:T(8,128)(2,1)S(1)} %broadcast_select_fusion.1), channel_id=1, source_target_pairs={{0,4},{8,12},{1,5},{9,13},{16,20},{24,28},{17,21},{25,29}} | collective-permute-start | bytes 245768 | tf_op jit(solution)/shard_map/ppermute | solution.py:232
  8.7 0.0 collective-permute-done.8
  8.7 0.0 copy-start.2
  8.7 1.4 %collective-permute-start.9 = (bf16[32,1280]{1,0:T(8,128)(2,1)S(1)}, bf16[32,1280]{1,0:T(8,128)(2,1)S(1)}, u32[]{:S(2)}, u32[]{:S(2)}) collective-permute-start(bf16[32,1280]{1,0:T(8,128)(2,1)S(1)} %broadcast_select_fusion), channel_id=1, source_target_pairs={{0,4},{8,12},{1,5},{9,13},{16,20},{24,28},{17,21},{25,29}} | collective-permute-start | bytes 245768 | tf_op jit(solution)/shard_map/ppermute | solution.py:233
  10.2 3.5 %collective-permute-done.4 = bf16[32,1280]{1,0:T(8,128)(2,1)S(1)} collective-permute-done((bf16[32,1280]{1,0:T(8,128)(2,1)S(1)}, bf16[32,1280]{1,0:T(8,128)(2,1)S(1)}, u32[]{:S(2)}, u32[]{:S(2)}) %collective-permute-start.4) | collective-permute-done | bytes 81952 | tf_op jit(solution)/shard_map/ppermute | solution.py:232
  13.7 1.3 %collective-permute-start.5 = (bf16[32,1280]{1,0:T(8,128)(2,1)S(1)}, bf16[32,1280]{1,0:T(8,128)(2,1)S(1)}, u32[]{:S(2)}, u32[]{:S(2)}) collective-permute-start(bf16[32,1280]{1,0:T(8,128)(2,1)S(1)} %broadcast_select_fusion.3.sink_k_ref), channel_id=1, source_target_pairs={{4,6},{8,10},{12,14},{5,7},{9,11},{13,15},{20,22},{24,26},{28,30},... | collective-permute-start | bytes 245768 | tf_op jit(solution)/shard_map/ppermute | solution.py:232
  15.0 3.6 %collective-permute-done.9 = bf16[32,1280]{1,0:T(8,128)(2,1)S(1)} collective-permute-done((bf16[32,1280]{1,0:T(8,128)(2,1)S(1)}, bf16[32,1280]{1,0:T(8,128)(2,1)S(1)}, u32[]{:S(2)}, u32[]{:S(2)}) %collective-permute-start.9) | collective-permute-done | bytes 81952 | tf_op jit(solution)/shard_map/ppermute | solution.py:233
  18.6 1.3 %collective-permute-start.10 = (bf16[32,1280]{1,0:T(8,128)(2,1)S(1)}, bf16[32,1280]{1,0:T(8,128)(2,1)S(1)}, u32[]{:S(2)}, u32[]{:S(2)}) collective-permute-start(bf16[32,1280]{1,0:T(8,128)(2,1)S(1)} %broadcast_select_fusion.2.refs_5_), channel_id=1, source_target_pairs={{4,6},{8,10},{12,14},{5,7},{9,11},{13,15},{20,22},{24,26},{28,30},... | collective-permute-start | bytes 245768 | tf_op jit(solution)/shard_map/ppermute | solution.py:233
  19.9 0.0 copy-done.2
  19.9 0.2 shard_map.73.refs_7_
  20.1 0.0 collective-permute-done.2.far_ref.refs_9_
  20.1 3.8 %collective-permute-start = (f32[96,128]{1,0:T(8,128)S(1)}, f32[96,128]{1,0:T(8,128)S(1)}, u32[]{:S(2)}, u32[]{:S(2)}) collective-permute-start(f32[96,128]{1,0:T(8,128)S(1)} %shard_map.73.refs_7_), channel_id=1, source_target_pairs={{0,1},{1,0},{2,3},{3,2},{4,5},{5,4},{6,7},{7,6},{8,9},{9,8},{10,11... | collective-permute-start | bytes 147464 | tf_op jit(solution)/shard_map/ppermute | solution.py:239
  23.9 0.0 collective-permute-done.6.next_ref.refs_7_
  23.9 0.0 collective-permute-done.5.came_k_ref
  23.9 0.0 collective-permute-done.1.near_ref.refs_8_
  23.9 0.2 shard_map.77
  24.0 0.1 collective-permute-start.7
  24.1 0.6 %collective-permute-done.refs_8_ = f32[96,128]{1,0:T(8,128)S(1)} collective-permute-done((f32[96,128]{1,0:T(8,128)S(1)}, f32[96,128]{1,0:T(8,128)S(1)}, u32[]{:S(2)}, u32[]{:S(2)}) %collective-permute-start) | collective-permute-done | bytes 49184 | tf_op jit(solution)/shard_map/ppermute | solution.py:239
  24.7 1.6 %shard_map.74 = (f32[8,128]{1,0:T(8,128)S(1)}, f32[8,1280]{1,0:T(8,128)S(1)}, bf16[96,1280]{1,0:T(8,128)(2,1)S(1)}, f32[96,1280]{1,0:T(8,128)S(1)}, f32[96,1280]{1,0:T(8,128)S(1)}, /*index=5*/f32[96,1280]{1,0:T(8,128)S(1)}) custom-call(s32[1]{0:T(128)S(6)} %copy.8.refs_0_.frames_ref, s32[1,2]{1,0:T(1,128)} %refs_1_.1, bf16[96,1280]{1,0:T(8,128)(2,1)S(1)} %copy-done.2, ...), custom_call_target="tpu_custom_call" | custom-call | tf_op jit(solution)/shard_map/pallas_call | solution.py:39
  26.3 0.3 %shard_map.78.refs_2_ = f32[10,96,96]{2,1,0:T(8,128)S(1)} custom-call(bf16[96,1280]{1,0:T(8,128)(2,1)S(1)} %get-tuple-element.19.q_ref, bf16[96,1280]{1,0:T(8,128)(2,1)S(1)} %get-tuple-element.24.keys_ref, f32[8,1280]{1,0:T(8,128)S(1)} %get-tuple-element.25.gains_ref), custom_call_target="tpu_custom_call" | custom-call | tf_op jit(solution)/shard_map/pallas_call | solution.py:39
  26.6 0.0 collective-permute-done.10.refs_6_
  26.7 0.0 collective-permute-done.7.refs_4_
  26.7 1.2 %shard_map.79 = bf16[96,1280]{1,0:T(8,128)(2,1)} custom-call(s32[1]{0:T(128)S(6)} %copy.8.refs_0_.frames_ref, f32[8,128]{1,0:T(8,128)S(1)} %get-tuple-element.18.refs_1_, f32[10,96,96]{2,1,0:T(8,128)S(1)} %shard_map.78.refs_2_, f32[8,128]{1,0:T(8,128)S(1)} %get-tuple-element.26.refs_3_, f32[8,128]{1,0:T(8,128)S(1)} %collective-permute-done.7.refs_4_, ...), custom_call_target="tpu_custom_call" | custom-call | tf_op jit(solution)/shard_map/pallas_call | solution.py:39
  (5 shorter events, 0.1 us)
Async XLA Ops:
  0.0 1.5 %copy-start = (bf16[96,1280]{1,0:T(8,128)(2,1)S(1)}, bf16[96,1280]{1,0:T(8,128)(2,1)}, u32[]{:S(2)}) copy-start(bf16[96,1280]{1,0:T(8,128)(2,1)} %k_hbm.1) | copy-start | bytes 737284
  0.0 1.5 %copy-start.1 = (bf16[96,1280]{1,0:T(8,128)(2,1)S(1)}, bf16[96,1280]{1,0:T(8,128)(2,1)}, u32[]{:S(2)}) copy-start(bf16[96,1280]{1,0:T(8,128)(2,1)} %v_hbm.1) | copy-start | bytes 737284
  0.0 7.3 %collective-permute-start.3 = (bf16[32,1280]{1,0:T(8,128)(2,1)S(1)}, bf16[32,1280]{1,0:T(8,128)(2,1)S(1)}, u32[]{:S(2)}, u32[]{:S(2)}) collective-permute-start(bf16[32,1280]{1,0:T(8,128)(2,1)S(1)} %get-tuple-element.22), channel_id=1, source_target_pairs={{0,8},{1,9},{16,24},{17,25}} | collective-permute-start | bytes 245768 | tf_op jit(solution)/shard_map/ppermute | solution.py:232
  1.6 22.3 %collective-permute-start.1 = (bf16[64,2560]{1,0:T(8,128)(2,1)S(1)}, bf16[64,2560]{1,0:T(8,128)(2,1)S(1)}, u32[]{:S(2)}, u32[]{:S(2)}) collective-permute-start(bf16[64,2560]{1,0:T(8,128)(2,1)S(1)} %get-tuple-element.20), channel_id=1, source_target_pairs={{0,2},{2,4},{4,6},{6,8},{8,10},{10,12},{12,14},{1,3},{3,5},{5,7},{... | collective-permute-start | bytes 983048 | tf_op jit(solution)/shard_map/ppermute | solution.py:226
  4.7 15.4 %collective-permute-start.2 = (bf16[32,2560]{1,0:T(8,128)(2,1)S(1)}, bf16[32,2560]{1,0:T(8,128)(2,1)S(1)}, u32[]{:S(2)}, u32[]{:S(2)}) collective-permute-start(bf16[32,2560]{1,0:T(8,128)(2,1)S(1)} %get-tuple-element.21), channel_id=1, source_target_pairs={{0,4},{2,6},{4,8},{6,10},{8,12},{10,14},{1,5},{3,7},{5,9},{7,11},{... | collective-permute-start | bytes 491528 | tf_op jit(solution)/shard_map/ppermute | solution.py:227
  6.0 17.9 %collective-permute-start.6 = (bf16[32,2560]{1,0:T(8,128)(2,1)S(1)}, bf16[32,2560]{1,0:T(8,128)(2,1)S(1)}, u32[]{:S(2)}, u32[]{:S(2)}) collective-permute-start(bf16[32,2560]{1,0:T(8,128)(2,1)S(1)} %get-tuple-element.23), channel_id=1, source_target_pairs={{0,2},{1,3},{16,18},{17,19}} | collective-permute-start | bytes 491528 | tf_op jit(solution)/shard_map/ppermute | solution.py:228
  6.7 2.0 %collective-permute-start.8 = (bf16[32,1280]{1,0:T(8,128)(2,1)S(1)}, bf16[32,1280]{1,0:T(8,128)(2,1)S(1)}, u32[]{:S(2)}, u32[]{:S(2)}) collective-permute-start(bf16[32,1280]{1,0:T(8,128)(2,1)S(1)} %get-tuple-element.27), channel_id=1, source_target_pairs={{0,8},{1,9},{16,24},{17,25}} | collective-permute-start | bytes 245768 | tf_op jit(solution)/shard_map/ppermute | solution.py:233
  7.4 6.3 %collective-permute-start.4 = (bf16[32,1280]{1,0:T(8,128)(2,1)S(1)}, bf16[32,1280]{1,0:T(8,128)(2,1)S(1)}, u32[]{:S(2)}, u32[]{:S(2)}) collective-permute-start(bf16[32,1280]{1,0:T(8,128)(2,1)S(1)} %broadcast_select_fusion.1), channel_id=1, source_target_pairs={{0,4},{8,12},{1,5},{9,13},{16,20},{24,28},{17,21},{25,29}} | collective-permute-start | bytes 245768 | tf_op jit(solution)/shard_map/ppermute | solution.py:232
  8.7 11.2 %copy-start.2 = (bf16[96,1280]{1,0:T(8,128)(2,1)S(1)}, bf16[96,1280]{1,0:T(8,128)(2,1)}, u32[]{:S(2)}) copy-start(bf16[96,1280]{1,0:T(8,128)(2,1)} %refs_2_.1) | copy-start | bytes 737284
  8.7 9.9 %collective-permute-start.9 = (bf16[32,1280]{1,0:T(8,128)(2,1)S(1)}, bf16[32,1280]{1,0:T(8,128)(2,1)S(1)}, u32[]{:S(2)}, u32[]{:S(2)}) collective-permute-start(bf16[32,1280]{1,0:T(8,128)(2,1)S(1)} %broadcast_select_fusion), channel_id=1, source_target_pairs={{0,4},{8,12},{1,5},{9,13},{16,20},{24,28},{17,21},{25,29}} | collective-permute-start | bytes 245768 | tf_op jit(solution)/shard_map/ppermute | solution.py:233
  13.7 10.2 %collective-permute-start.5 = (bf16[32,1280]{1,0:T(8,128)(2,1)S(1)}, bf16[32,1280]{1,0:T(8,128)(2,1)S(1)}, u32[]{:S(2)}, u32[]{:S(2)}) collective-permute-start(bf16[32,1280]{1,0:T(8,128)(2,1)S(1)} %broadcast_select_fusion.3.sink_k_ref), channel_id=1, source_target_pairs={{4,6},{8,10},{12,14},{5,7},{9,11},{13,15},{20,22},{24,26},{28,30},... | collective-permute-start | bytes 245768 | tf_op jit(solution)/shard_map/ppermute | solution.py:232
  18.6 8.0 %collective-permute-start.10 = (bf16[32,1280]{1,0:T(8,128)(2,1)S(1)}, bf16[32,1280]{1,0:T(8,128)(2,1)S(1)}, u32[]{:S(2)}, u32[]{:S(2)}) collective-permute-start(bf16[32,1280]{1,0:T(8,128)(2,1)S(1)} %broadcast_select_fusion.2.refs_5_), channel_id=1, source_target_pairs={{4,6},{8,10},{12,14},{5,7},{9,11},{13,15},{20,22},{24,26},{28,30},... | collective-permute-start | bytes 245768 | tf_op jit(solution)/shard_map/ppermute | solution.py:233
  20.1 4.6 %collective-permute-start = (f32[96,128]{1,0:T(8,128)S(1)}, f32[96,128]{1,0:T(8,128)S(1)}, u32[]{:S(2)}, u32[]{:S(2)}) collective-permute-start(f32[96,128]{1,0:T(8,128)S(1)} %shard_map.73.refs_7_), channel_id=1, source_target_pairs={{0,1},{1,0},{2,3},{3,2},{4,5},{5,4},{6,7},{7,6},{8,9},{9,8},{10,11... | collective-permute-start | bytes 147464 | tf_op jit(solution)/shard_map/ppermute | solution.py:239
  24.0 2.6 %collective-permute-start.7 = (f32[8,128]{1,0:T(8,128)S(1)}, f32[8,128]{1,0:T(8,128)S(1)}, u32[]{:S(2)}, u32[]{:S(2)}) collective-permute-start(f32[8,128]{1,0:T(8,128)S(1)} %get-tuple-element.26.refs_3_), channel_id=1, source_target_pairs={{0,1},{1,0},{2,3},{3,2},{4,5},{5,4},{6,7},{7,6},{8,9},{9,8},{10,11... | collective-permute-start | bytes 12296 | tf_op jit(solution)/shard_map/ppermute | solution.py:255
